TPU v7x, 32 devices: a whole 2x2x4 slice. The times are simulated.
32 devices in a mesh: gx: 8 (over z, x), gy: 4 (over y, core).
Axes of the slice: x: 2, y: 2, z: 4, core: 2. Of those that a mesh axis runs over, the one named last changes fastest.
Arguments:
- pair_ends: int32 [3, 462848], P(None, ('gx', 'gy')), may hold values from 0 to 65535, as said below
- pair_geometry: float32 [5, 462848], P(None, ('gx', 'gy')), may hold values from -2 to 2, as said below
- drag_coef: float32 [6, 65536], P(None, ('gx', 'gy')), may hold values from 0.2 to 2
- forces: float32 [6, 65536], P(None, ('gx', 'gy')), may hold values from -40 to 40
Outputs:
- velocity: float32 [6, 65536], P(None, ('gx', 'gy'))
- residual: float32 [6, 65536], P(None, ('gx', 'gy'))
Inputs may be any that keep to these rules, and one draw needn't show every extreme that they name: `pair_ends`: row 0 is sphere i, row 1 sphere j, row 2 the slot of j in i's row of 16 slots; slot 16 marks padding (i = j = 65535), which stands at the end of every device's list, at least one entry on each. Sphere n lies in cell block n // 2048, held by the device with gx index block // 4 and gy index block % 4. A live entry's i lies in a block of the list's own gy index; j lies in i's block or one of its eight neighbours on the periodic grid of blocks. Live entries are ordered by the gx index of i's block; one device's list holds at most 4096 entries with i in one gx index, and in every gy index some block gets exactly 4096 from every list. Each (i, slot) appears at most once in all lists; an entry (i, j) at slot 2m has an entry (j, i) at slot 2m + 1 and the reverse. `pair_geometry`: rows 0 to 2 hold j's position minus i's, cell offsets included; rows 3 and 4 the radii of i and j; entries (i, j) and (j, i) have opposite separations and swapped radii; padding holds 0, 0, 0, 1, 1.
All inputs are finite; a program needn't handle non-finite values.
Results may differ from a plain program's by a relative error of at most 0.0003.
Values sent between devices are 32-bit elements; how exact they have to be, the bound alone decides.
No kernel may reach another device: no remote copies, remote signals or barrier semaphores. Data moves between devices by JAX's collectives and lax.ppermute only.
A program may use at most 128 MiB of HBM per device.

v0:
```python
import jax
import jax.numpy as jnp
from jax import lax
from jax.sharding import PartitionSpec as P

K = 16
ITERS = 3


def extended(cells, sides, width):
    for axis, dim in sides:
        count = lax.axis_size(axis)
        head = lax.slice_in_dim(cells, 0, width, axis=dim)
        tail = lax.slice_in_dim(cells, cells.shape[dim] - width, cells.shape[dim], axis=dim)
        cells = jnp.concatenate(
            [
                lax.ppermute(tail, axis, [(i, (i + 1) % count) for i in range(count)]),
                cells,
                lax.ppermute(head, axis, [((i + 1) % count, i) for i in range(count)]),
            ],
            axis=dim,
        )
    return cells


def pair_params(geometry):
    separation = geometry[0:3]
    radius_first = geometry[3]
    radius_second = geometry[4]
    reach_sum = radius_first + radius_second
    dist_sq = (
        separation[0] * separation[0]
        + separation[1] * separation[1]
        + separation[2] * separation[2]
    )
    unit_dir = separation / jnp.sqrt(dist_sq + reach_sum * reach_sum)
    weight = 1.0 / (1.0 + dist_sq / (reach_sum * reach_sum))
    reduced = radius_first * radius_second / reach_sum
    shear_coef = reduced * weight
    squeeze_coef = shear_coef * weight
    return jnp.concatenate([unit_dir, shear_coef[None], squeeze_coef[None]], axis=0)


def build_tile(pair_terms):
    unit_dir = pair_terms[0:3]
    shear_coef = pair_terms[3]
    squeeze_coef = pair_terms[4]
    length_sq = unit_dir[0] * unit_dir[0] + unit_dir[1] * unit_dir[1] + unit_dir[2] * unit_dir[2]
    entries = []
    for row_idx in range(6):
        for col_idx in range(6):
            outer_term = unit_dir[row_idx % 3] * unit_dir[col_idx % 3]
            same_axis = row_idx % 3 == col_idx % 3
            if row_idx < 3 and col_idx < 3:
                entry_val = 6.0 * squeeze_coef * outer_term
                if same_axis:
                    entry_val = entry_val + shear_coef
            elif row_idx >= 3 and col_idx >= 3:
                if same_axis:
                    entry_val = shear_coef * (2.5 - 2.0 * outer_term)
                else:
                    entry_val = shear_coef * (-2.0 * outer_term)
            elif same_axis:
                entry_val = 0.8 * shear_coef * (outer_term - length_sq / 3.0)
            else:
                entry_val = 0.8 * shear_coef * outer_term
            entries.append(entry_val)
    return jnp.stack(entries, axis=0)


def squares(residual):
    return lax.psum(jnp.sum(residual * residual), ("gx", "gy"))


def pack_runs(values, fill_col, run_starts, run_counts, capacity):
    padded = jnp.concatenate(
        [values, jnp.broadcast_to(fill_col, (values.shape[0], capacity))], axis=1
    )
    windows = jax.vmap(
        lambda start: lax.dynamic_slice_in_dim(padded, start, capacity, 1), out_axes=1
    )(run_starts)
    keep = jnp.arange(capacity, dtype=jnp.int32)[None, :] < run_counts[:, None]
    windows = jnp.where(keep[None, :, :], windows, fill_col[:, :, None])
    return windows.reshape(values.shape[0], run_starts.shape[0] * capacity)


def on_device(pair_ends, pair_geometry, drag_coef, forces):
    spheres = drag_coef.shape[1]
    slab_count = lax.axis_size("gx")
    strip_count = lax.axis_size("gy")
    capacity = spheres * K // slab_count
    slot_total = K * spheres
    first_ids = pair_ends[0]
    second_ids = pair_ends[1]
    slot_ids = pair_ends[2]
    is_live = slot_ids < K
    first_block = first_ids // spheres
    second_block = second_ids // spheres
    owner_x = first_block // strip_count
    shift_x = (second_block // strip_count - owner_x + 1) % slab_count
    shift_y = (second_block % strip_count - first_block % strip_count + 1) % strip_count
    source_col = (shift_x * 3 + shift_y) * spheres + second_ids % spheres
    target_slot = slot_ids * spheres + first_ids % spheres
    owner_hits = jnp.logical_and(
        owner_x[:, None] == jnp.arange(slab_count, dtype=jnp.int32)[None, :], is_live[:, None]
    )
    owner_counts = jnp.sum(owner_hits.astype(jnp.int32), axis=0, dtype=jnp.int32)
    owner_starts = jnp.cumsum(owner_counts, dtype=jnp.int32) - owner_counts
    labels = jnp.stack([target_slot, source_col], axis=0)
    label_fill = jnp.array([[slot_total], [4 * spheres]], jnp.int32)
    label_buffer = pack_runs(labels, label_fill, owner_starts, owner_counts, capacity)
    pair_terms = pair_params(pair_geometry)
    tile_buffer = pack_runs(
        build_tile(pair_terms),
        jnp.zeros((36, 1), jnp.float32),
        owner_starts,
        owner_counts,
        capacity,
    )
    arrived, arrived_labels = (
        lax.all_to_all(tile_buffer, "gx", split_axis=1, concat_axis=1, tiled=True),
        lax.all_to_all(label_buffer, "gx", split_axis=1, concat_axis=1, tiled=True),
    )
    arrived_count = arrived.shape[1]
    position_of = (
        jnp.full((slot_total + 1,), arrived_count, jnp.int32)
        .at[arrived_labels[0]]
        .set(jnp.arange(arrived_count, dtype=jnp.int32))
    )
    position_of = position_of[:slot_total]
    arrived_ext = jnp.concatenate([arrived, jnp.zeros((36, 1), jnp.float32)], axis=1)
    columns_ext = jnp.concatenate(
        [arrived_labels[1], jnp.full((1,), 4 * spheres, jnp.int32)], axis=0
    )
    tile_grid = jnp.take(arrived_ext, position_of, axis=1).reshape(6, 6, K, spheres)
    columns = jnp.take(columns_ext, position_of, axis=0)
    velocity = jnp.zeros_like(forces)
    residual = forces
    direction = forces
    norm_now = squares(residual)
    for iteration in range(ITERS):
        beside_all = extended(direction.reshape(6, 1, 1, spheres), (("gx", 1), ("gy", 2)), 1)
        neighbourhood = beside_all.reshape(6, 9 * spheres)
        gathered = jnp.take(neighbourhood, columns, axis=1).reshape(6, K, spheres)
        change = direction[:, None, :] - gathered
        applied = drag_coef * direction + jnp.sum(tile_grid * change[None, :, :, :], axis=(1, 2))
        step_size = norm_now / lax.psum(jnp.sum(direction * applied), ("gx", "gy"))
        velocity = velocity + step_size * direction
        residual = residual - step_size * applied
        norm_next = squares(residual)
        direction = residual + norm_next / norm_now * direction
        norm_now = norm_next
    return (velocity, residual)


def solution(mesh):
    in_specs = (
        P(None, ("gx", "gy")),
        P(None, ("gx", "gy")),
        P(None, ("gx", "gy")),
        P(None, ("gx", "gy")),
    )
    out_specs = (P(None, ("gx", "gy")), P(None, ("gx", "gy")))
    return jax.shard_map(
        on_device, mesh=mesh, in_specs=in_specs, out_specs=out_specs, check_vma=False
    )
```

profile of v0, /device:TPU:0, one launch (start us, length us, event | category | flops | bytes accessed | tf_op | source)
XLA Modules:
  0.0 1246.3 jit_solution(14403817438908899531)
XLA Ops:
  13.7 11.9 while.4
  36.8 10.5 stack.5
  49.1 18.6 %while.5 = (s32[]{:T(128)}, f32[36,18560]{1,0:T(8,128)S(1)}, s32[8,2]{0,1:T(2,128)S(1)}, f32[8,36,4096]{2,1,0:T(8,128)}) while((s32[]{:T(128)}, f32[36,18560]{1,0:T(8,128)S(1)}, s32[8,2]{0,1:T(2,128)S(1)}, f32[8,36,4096]{2,1,0:T(8,128)}) %tuple.73), condition=%wide.while_cond.1.clone, body=%wide.while_body.1.sunk.clone | while | flops 2 | bytes 1246289 | solution.py:80
  69.6 5.7 select_bitcast_fusion
  75.7 5.1 copy.28
  80.9 5.9 all-to-all-start.1
  87.2 120.1 %scatter_custom_fusion = s32[32769]{0:T(1024)S(1)} fusion(s32[32768]{0:T(1024)S(1)} %bitcast.75, s32[32768]{0:T(1024)S(1)} %iota.16, s32[]{:T(128)} %constant.141.clone.1), kind=kCustom, calls=%fused_computation.76 | custom fusion | bytes 131080 | tf_op jit(solution)/shard_map/scatter | solution.py:128
  207.3 180.5 %gather_fusion.1 = s32[32768]{0:T(1024)S(1)} fusion(s32[32769]{0:T(1024)S(1)} %pad_add_fusion.1, s32[32768]{0:T(1024)S(1)} %get-tuple-element.77), kind=kCustom, calls=%fused_computation.4 | custom fusion | bytes 393216 | tf_op jit(solution)/shard_map/jit(_take)/gather | solution.py:136
  388.0 112.0 %gather_fusion.2 = f32[32768,6]{1,0:T(8,128)} fusion(f32[6,18432]{0,1:T(8,128)} %bitcast.55, s32[32768]{0:T(1024)S(1)} %broadcast_clamp_fusion), kind=kCustom, calls=%fused_computation.clone | custom fusion | bytes 1703936 | tf_op jit(solution)/shard_map/jit(_take)/gather | solution.py:144
  500.0 17.9 %broadcast_select_fusion.2 = f32[32768,6]{1,0:T(8,128)S(1)} fusion(f32[32768,6]{1,0:T(8,128)} %gather_fusion.2, pred[32768]{0:T(1024)(128)(4,1)S(1)} %compare_and_fusion), kind=kLoop, calls=%fused_computation.12 | loop fusion | flops 196608 | bytes 1605632 | tf_op jit(solution)/shard_map/jit(_take)/select_n | solution.py:144
  518.0 6.1 broadcast_subtract_fusion.2
  524.0 10.1 copy.29
  534.2 11.1 copy.25
  545.4 13.3 %concatenate.37 = f32[36,32769]{0,1:T(8,128)} pad(f32[36,32768]{0,1:T(8,128)} %bitcast.53, f32[]{:T(128)} %constant.140.clone.1), padding=0_0x0_1 | pad | bytes 9437332 | tf_op jit(solution)/shard_map/concatenate | solution.py:131
  558.7 114.7 %gather_fusion = f32[32768,36]{1,0:T(8,128)} fusion(f32[36,32769]{0,1:T(8,128)} %concatenate.37, s32[32768]{0:T(1024)S(1)} %get-tuple-element.77), kind=kCustom, calls=%fused_computation.3 | custom fusion | bytes 9568256 | tf_op jit(solution)/shard_map/jit(_take)/gather | solution.py:135
  673.4 11.9 copy.26
  685.3 5.5 copy.36
  694.9 41.2 %all-reduce.3 = (f32[]{:T(128)}, f32[]{:T(128)}) all-reduce(f32[]{:T(128)} %get-tuple-element.20, f32[]{:T(128)} %get-tuple-element.19), channel_id=1, replica_groups=mesh['gx'=8,'gy'=4] {'gx','gy'}, use_global_device_ids=true, to_apply=%region_1.2 | all-reduce | flops 2 | bytes 16 | tf_op jit(solution)/shard_map/psum | solution.py:72
  738.0 40.4 %psum.44 = f32[]{:T(128)} all-reduce(f32[]{:T(128)} %get-tuple-element.41), channel_id=1, replica_groups=mesh['gx'=8,'gy'=4] {'gx','gy'}, use_global_device_ids=true, to_apply=%region_9.11 | all-reduce | flops 1 | bytes 8 | tf_op jit(solution)/shard_map/psum | solution.py:72
  794.1 5.1 copy.31
  799.2 111.9 %gather_fusion.3 = f32[32768,6]{1,0:T(8,128)} fusion(f32[6,18432]{0,1:T(8,128)} %bitcast.57, s32[32768]{0:T(1024)S(1)} %broadcast_clamp_fusion), kind=kCustom, calls=%fused_computation.1.clone | custom fusion | bytes 1703936 | tf_op jit(solution)/shard_map/jit(_take)/gather | solution.py:144
  911.1 17.9 %broadcast_select_fusion.1 = f32[32768,6]{1,0:T(8,128)S(1)} fusion(f32[32768,6]{1,0:T(8,128)} %gather_fusion.3, pred[32768]{0:T(1024)(128)(4,1)S(1)} %compare_and_fusion), kind=kLoop, calls=%fused_computation.11 | loop fusion | flops 196608 | bytes 1605632 | tf_op jit(solution)/shard_map/jit(_take)/select_n | solution.py:144
  929.0 6.1 broadcast_subtract_fusion.1
  935.1 10.1 copy.32
  948.9 41.1 %psum.45 = f32[]{:T(128)} all-reduce(f32[]{:T(128)} %multiply_reduce_fusion.5), channel_id=1, replica_groups=mesh['gx'=8,'gy'=4] {'gx','gy'}, use_global_device_ids=true, to_apply=%region_12.14 | all-reduce | flops 1 | bytes 8 | tf_op jit(solution)/shard_map/psum | solution.py:147
  992.0 40.7 %psum.46 = f32[]{:T(128)} all-reduce(f32[]{:T(128)} %get-tuple-element.39), channel_id=1, replica_groups=mesh['gx'=8,'gy'=4] {'gx','gy'}, use_global_device_ids=true, to_apply=%region_14.16 | all-reduce | flops 1 | bytes 8 | tf_op jit(solution)/shard_map/psum | solution.py:72
  1048.4 5.1 copy.34
  1053.5 111.9 %gather_fusion.4 = f32[32768,6]{1,0:T(8,128)} fusion(f32[6,18432]{0,1:T(8,128)} %bitcast.56, s32[32768]{0:T(1024)S(1)} %broadcast_clamp_fusion), kind=kCustom, calls=%fused_computation.2.clone | custom fusion | bytes 1703936 | tf_op jit(solution)/shard_map/jit(_take)/gather | solution.py:144
  1165.4 17.9 %broadcast_select_fusion = f32[32768,6]{1,0:T(8,128)S(1)} fusion(f32[32768,6]{1,0:T(8,128)} %gather_fusion.4, pred[32768]{0:T(1024)(128)(4,1)S(1)} %compare_and_fusion), kind=kLoop, calls=%fused_computation.10 | loop fusion | flops 196608 | bytes 1605632 | tf_op jit(solution)/shard_map/jit(_take)/select_n | solution.py:144
  1183.3 6.1 broadcast_subtract_fusion
  1189.4 10.1 copy.35
  1203.2 41.1 %psum.47 = f32[]{:T(128)} all-reduce(f32[]{:T(128)} %multiply_reduce_fusion.3), channel_id=1, replica_groups=mesh['gx'=8,'gy'=4] {'gx','gy'}, use_global_device_ids=true, to_apply=%region_17.19 | all-reduce | flops 1 | bytes 8 | tf_op jit(solution)/shard_map/psum | solution.py:147
  (131 shorter events, 101.2 us)
Async XLA Ops:
  0.6 67.1 %collective-permute-start = (f32[6,1,1,2048]{3,0,2,1:T(8,128)}, f32[6,1,1,2048]{3,0,2,1:T(8,128)S(1)}, u32[]{:S(2)}, u32[]{:S(2)}) collective-permute-start(f32[6,1,1,2048]{3,0,2,1:T(8,128)} %bitcast.65), channel_id=1, source_target_pairs={{0,4},{4,8},{8,12},{12,16},{16,20},{20,24},{24,28},{28,0},{1,5},{5... | collective-permute-start | bytes 147464 | tf_op jit(solution)/shard_map/ppermute | solution.py:17
  3.6 64.1 %collective-permute-start.1 = (f32[6,1,1,2048]{3,0,2,1:T(8,128)}, f32[6,1,1,2048]{3,0,2,1:T(8,128)S(1)}, u32[]{:S(2)}, u32[]{:S(2)}) collective-permute-start(f32[6,1,1,2048]{3,0,2,1:T(8,128)} %bitcast.66), channel_id=1, source_target_pairs={{4,0},{8,4},{12,8},{16,12},{20,16},{24,20},{28,24},{0,28},{5,1},{9... | collective-permute-start | bytes 147464 | tf_op jit(solution)/shard_map/ppermute | solution.py:19
  27.2 53.7 %all-to-all-start = ((s32[2,8,4096]{2,0,1:T(2,128)}), s32[2,8,4096]{2,0,1:T(2,128)S(1)}, u32[]{:S(2)}, u32[]{:S(2)}) async-start(s32[2,8,4096]{2,0,1:T(2,128)} %select_bitcast_fusion.1), calls=%async_computation | async-start | bytes 524288 | tf_op jit(solution)/shard_map/all_to_all | solution.py:122
  33.3 34.5 %copy-start.1 = (f32[6,2048]{1,0:T(8,128)S(1)}, f32[6,2048]{1,0:T(8,128)}, u32[]{:S(2)}) copy-start(f32[6,2048]{1,0:T(8,128)} %param.10) | copy-start | bytes 147460
  67.8 7.9 collective-permute-start.2
  67.9 7.8 collective-permute-start.3
  80.9 453.4 %all-to-all-start.1 = ((f32[36,8,4096]{2,0,1:T(8,128)}), f32[36,8,4096]{2,0,1:T(8,128)}, u32[]{:S(2)}, u32[]{:S(2)}) async-start(f32[36,8,4096]{2,0,1:T(8,128)} %select_bitcast_fusion), calls=%async_computation.1 | async-start | bytes 10485760 | tf_op jit(solution)/shard_map/all_to_all | solution.py:121
  690.8 3.4 copy-start.2
  691.4 2.1 copy-start
  779.8 7.1 collective-permute-start.4
  782.1 5.0 collective-permute-start.5
  787.1 5.1 collective-permute-start.6
  787.2 6.9 collective-permute-start.7
  1034.1 7.1 collective-permute-start.8
  1036.4 5.0 collective-permute-start.9
  1041.4 5.1 collective-permute-start.10
  1041.5 6.9 collective-permute-start.11
where the time goes:
time: 1250 us
  local copies, waits for them, and re-layouts  886 us (71%)
  blocking collectives  205 us (16%)
  other arithmetic  103 us (8%)
  starting transfers between devices  30.4 us (2%)
  waiting for transfers between devices  14.7 us (1%)
    gather x3, local copies, waits for them, and re-layouts, on_device(): gathered = jnp.take(neighbourhood, columns, axis=1).reshape(6, K, spheres)  336 us
    gather x1, local copies, waits for them, and re-layouts, on_device(): columns = jnp.take(columns_ext, position_of, axis=0)  181 us
    gather x2, local copies, waits for them, and re-layouts, on_device(): jnp.take(arrived_ext, position_of, axis=1).reshape(6, 6, K, spheres)  127 us
    psum x3, blocking collectives, squares(): return lax.psum(jnp.sum(residual * residual), ('gx', 'gy'))  122 us
    scatter x1, local copies, waits for them, and re-layouts, on_device(): position_of = jnp.full((slot_total + 1,), arrived_count, jnp.int32).at[ar...  120 us
    psum x2, blocking collectives, on_device(): step_size = norm_now / lax.psum(jnp.sum(direction * applied), ('gx', 'gy'))  82.2 us
    select_n x3, other arithmetic, on_device(): gathered = jnp.take(neighbourhood, columns, axis=1).reshape(6, K, spheres)  53.8 us
    gather x48, local copies, waits for them, and re-layouts  30.4 us
  transfers between devices with their start and end apart: 14, of which 8 were waited for; matrix products, arithmetic and copies ran while one was open for 41% of the time, Pallas kernels for 0%

commit v1 on v0

v1 whole, which is shorter than its diff:
```python
import functools

import jax
import jax.numpy as jnp
from jax import lax
from jax.experimental import pallas as pl
from jax.experimental.pallas import tpu as pltpu
from jax.sharding import PartitionSpec as P

K = 16
ITERS = 3
LANES = 128
SUB = 8
FIELDS = 6
SENT = 6

f32 = jnp.float32
i32 = jnp.int32
bf16 = jnp.bfloat16


def log2(n):
    assert n & (n - 1) == 0
    return n.bit_length() - 1


def iota(shape, dim):
    return lax.broadcasted_iota(i32, shape, dim)


def pack_kernel(slabs, strips, spheres, ends_ref, geo_ref, force_ref, send_ref, dense_ref, ends_s, geo_s, out_s):
    rows = ends_ref.shape[1] // LANES
    padded = ends_s.shape[0] // 3
    cap_rows = send_ref.shape[2]
    chunks = spheres // LANES
    for r in range(rows):
        cols = slice(r * LANES, (r + 1) * LANES)
        ends_s[pl.ds(r, 3, stride=padded), :] = ends_ref[:, cols]
        geo_s[pl.ds(r, 5, stride=padded), :] = geo_ref[:, cols]
    for r in range(chunks):
        dense_ref[pl.ds(r, FIELDS, stride=chunks), :] = force_ref[:, r * LANES : (r + 1) * LANES]
    first = ends_s[0:padded, :]
    second = ends_s[padded : 2 * padded, :]
    slot = ends_s[2 * padded : 3 * padded, :]
    inside = iota((padded, LANES), 0) < rows
    live = jnp.logical_and(slot < K, inside)
    shift = log2(spheres)
    first_block = first >> shift
    second_block = second >> shift
    owner = first_block >> log2(strips)
    shift_x = ((second_block >> log2(strips)) - owner + 1) & (slabs - 1)
    shift_y = ((second_block & (strips - 1)) - (first_block & (strips - 1)) + 1) & (strips - 1)
    column = (shift_x * 3 + shift_y) * spheres + (second & (spheres - 1))
    target = slot * spheres + (first & (spheres - 1))
    owner = jnp.where(live, owner, slabs)
    sep = [geo_s[c * padded : (c + 1) * padded, :] for c in range(3)]
    a = geo_s[3 * padded : 4 * padded, :]
    b = geo_s[4 * padded : 5 * padded, :]
    h = a + b
    total = sep[0] * sep[0] + sep[1] * sep[1] + sep[2] * sep[2] + h * h
    inv = lax.rsqrt(total)
    values = [target.astype(f32), column.astype(f32)] + [d * inv for d in sep] + [a * b * h * (inv * inv)]
    for c, value in enumerate(values):
        out_s[c, 0:padded, :] = value
    lane = iota((cap_rows, LANES), 1)
    place = iota((cap_rows, LANES), 0) * LANES + lane
    start = jnp.int32(0)
    for o in range(slabs):
        end = jnp.sum(jnp.where(owner <= o, 1.0, 0.0)).astype(i32)
        row = start >> 7
        off = start & (LANES - 1)
        back = (LANES - off) & (LANES - 1)
        for c in range(SENT):
            here = pltpu.roll(out_s[c, pl.ds(row, cap_rows), :], back, 1)
            after = pltpu.roll(out_s[c, pl.ds(row + 1, cap_rows), :], back, 1)
            value = jnp.where(lane < LANES - off, here, after)
            if c == 0:
                value = jnp.where(place < end - start, value, -1.0)
            send_ref[o, c] = value
        start = end


def pack(ends, geo, forces, slabs, strips):
    spheres = forces.shape[1]
    cap_rows = spheres * K // slabs // LANES
    rows = ends.shape[1] // LANES
    padded = -(-rows // SUB) * SUB
    return pl.pallas_call(
        functools.partial(pack_kernel, slabs, strips, spheres),
        out_shape=(
            jax.ShapeDtypeStruct((slabs, SENT, cap_rows, LANES), f32),
            jax.ShapeDtypeStruct((FIELDS * spheres // LANES, LANES), f32),
        ),
        scratch_shapes=[
            pltpu.VMEM((3 * padded, LANES), i32),
            pltpu.VMEM((5 * padded, LANES), f32),
            pltpu.VMEM((SENT, padded + cap_rows + SUB, LANES), f32),
        ],
        name="pack",
    )(ends, geo, forces)


def place_kernel(spheres, got_ref, terms_ref, col_ref, span_ref, acc, tgt, lo_v, n_v, lo_s, n_s, sem):
    sources = got_ref.shape[0]
    cap_rows = got_ref.shape[2]
    groups = sources // SUB
    tiles = K * spheres // (SUB * LANES)
    shift = log2(spheres)
    lane = iota((SUB, LANES), 1)
    big = 1 << 20

    acc[...] = jnp.zeros_like(acc)
    hi_iota = iota((2 * LANES, LANES), 0).astype(f32).astype(bf16)
    lo_iota = iota((LANES, LANES), 0).astype(f32).astype(bf16)
    lane_value = iota((LANES, LANES), 1).astype(f32).astype(bf16)
    one = jnp.ones((), bf16)
    zero = jnp.zeros((), bf16)

    for s in range(sources):

        def step(g, carry):
            t = got_ref[s, 0, pl.ds(pl.multiple_of(g * SUB, SUB), SUB), :].astype(i32)
            hi = (t >> 7).astype(f32)
            lo = (t & (LANES - 1)).astype(f32)
            left = []
            right_row = []
            right_lane = []
            for u in range(SUB):
                hi_row = jnp.broadcast_to(hi[u : u + 1, :], (2 * LANES, LANES)).astype(bf16)
                lo_row = jnp.broadcast_to(lo[u : u + 1, :], (LANES, LANES)).astype(bf16)
                left.append(jnp.where(hi_iota == hi_row, one, zero))
                number = jnp.full((LANES, LANES), (g * SUB + (u + s * cap_rows + 1)).astype(f32), f32).astype(bf16)
                match = lo_iota == lo_row
                right_row.append(jnp.where(match, number, zero))
                right_lane.append(jnp.where(match, lane_value, zero))
            left = jnp.concatenate(left, axis=1)
            right = jnp.concatenate([jnp.concatenate(right_row, axis=1), jnp.concatenate(right_lane, axis=1)], axis=0)
            acc[...] += lax.dot_general(left, right, (((1,), (1,)), ((), ())), preferred_element_type=f32)
            return carry

        lax.fori_loop(0, cap_rows // SUB, step, 0)

    for group in range(groups):
        low = jnp.full((SUB, LANES), big, i32)
        high = jnp.full((SUB, LANES), -1, i32)
        for k in range(cap_rows):
            for u in range(SUB):
                tgt[u : u + 1, :] = got_ref[group * SUB + u, 0, k : k + 1, :]
            t = tgt[...]
            tile = jnp.floor(t * (1.0 / (SUB * LANES)))
            t_low = jnp.min(jnp.where(t < 0.0, float(big), tile), axis=1, keepdims=True).astype(i32)
            t_high = jnp.max(jnp.where(t < 0.0, -1.0, tile), axis=1, keepdims=True).astype(i32)
            low = jnp.where(lane == k, t_low, low)
            high = jnp.where(lane == k, t_high, high)
        starts = jnp.full((SUB, LANES), 0, i32)
        counts = jnp.full((SUB, LANES), 0, i32)
        lane_f = lane.astype(f32)
        for q in range(tiles):
            hit = jnp.logical_and(low <= q, high >= q)
            k_low = jnp.min(jnp.where(hit, lane_f, float(cap_rows - 1)), axis=1, keepdims=True)
            k_high = jnp.max(jnp.where(hit, lane_f, -1.0), axis=1, keepdims=True)
            starts = jnp.where(lane == q, k_low.astype(i32), starts)
            counts = jnp.where(lane == q, (k_high - k_low).astype(i32) + 1, counts)
        lo_v[group] = starts
        n_v[group] = jnp.broadcast_to(jnp.max(counts.astype(f32), axis=0, keepdims=True).astype(i32), (SUB, LANES))
    lo_copy = pltpu.make_async_copy(lo_v, lo_s, sem.at[0])
    n_copy = pltpu.make_async_copy(n_v, n_s, sem.at[1])
    lo_copy.start()
    n_copy.start()
    lo_copy.wait()
    n_copy.wait()

    def place(q, carry):
        low, high = carry
        rows = pl.ds(pl.multiple_of(q * SUB, SUB), SUB)
        number = acc[rows, 0:LANES].astype(i32)
        at = acc[rows, LANES : 2 * LANES].astype(i32)
        values = tuple(jnp.zeros((SUB, LANES), f32) for _ in range(SENT - 1))
        for group in range(groups):

            def pick(kk, values):
                values = list(values)
                for u in range(SUB):
                    s = group * SUB + u
                    k = jnp.minimum(lo_s[group, u, q] + kk, cap_rows - 1)
                    match = number == s * cap_rows + k + 1
                    for c in range(1, SENT):
                        row = jnp.broadcast_to(got_ref[s, c, pl.ds(k, 1), :], (SUB, LANES))
                        found = jnp.take_along_axis(row, at, axis=1)
                        values[c - 1] = jnp.where(match, found, values[c - 1])
                return tuple(values)

            values = lax.fori_loop(0, n_s[group, 0, q], pick, values)
        filled = number > 0
        col = jnp.where(filled, values[0], -1.0)
        col_ref[rows, :] = col.astype(i32)
        for c in range(SENT - 2):
            terms_ref[c, rows, :] = values[c + 1]
        block = jnp.floor(col * (1.0 / spheres))
        b_low = jnp.min(jnp.where(filled, block, float(big)), axis=1, keepdims=True)
        b_high = jnp.max(block, axis=1, keepdims=True)
        return (jnp.where(lane == q, b_low, low), jnp.where(lane == q, b_high, high))

    low, high = lax.fori_loop(
        0, tiles, place, (jnp.full((SUB, LANES), float(big), f32), jnp.full((SUB, LANES), -1.0, f32))
    )
    span_ref[0:SUB, :] = jnp.broadcast_to(jnp.min(low, axis=0, keepdims=True), (SUB, LANES)).astype(i32)
    span_ref[SUB : 2 * SUB, :] = jnp.broadcast_to(jnp.max(high, axis=0, keepdims=True), (SUB, LANES)).astype(i32)


def place_entries(got, spheres):
    sources = got.shape[0]
    groups = sources // SUB
    slot_rows = K * spheres // LANES
    assert slot_rows == 2 * LANES
    return pl.pallas_call(
        functools.partial(place_kernel, spheres),
        out_shape=(
            jax.ShapeDtypeStruct((SENT - 2, slot_rows, LANES), f32),
            jax.ShapeDtypeStruct((slot_rows, LANES), i32),
            jax.ShapeDtypeStruct((2 * SUB, LANES), i32),
        ),
        scratch_shapes=[
            pltpu.VMEM((slot_rows, 2 * LANES), f32),
            pltpu.VMEM((SUB, LANES), f32),
            pltpu.VMEM((groups, SUB, LANES), i32),
            pltpu.VMEM((groups, SUB, LANES), i32),
            pltpu.SMEM((groups, SUB, LANES), i32),
            pltpu.SMEM((groups, SUB, LANES), i32),
            pltpu.SemaphoreType.DMA((2,)),
        ],
        name="place",
    )(got)


def lane_pick(row, k):
    return jnp.sum(jnp.where(iota(row.shape, 1) == k, row, 0.0), axis=1, keepdims=True)


def apply_operator(table, span_ref, col_ref, terms_ref, drag_ref, out_ref):
    chunks = table.shape[2]
    halves = chunks // SUB
    centre = 4
    tiles = K * halves

    def slot(k, sums):
        base = [(k * halves + h) * SUB for h in range(halves)]
        rows = [pl.ds(pl.multiple_of(b, SUB), SUB) for b in base]
        col = [col_ref[r, :] for r in rows]
        at = [c & (LANES - 1) for c in col]
        number = [c >> 7 for c in col]
        low = span_ref[0, k * halves]
        high = span_ref[SUB, k * halves]
        for h in range(1, halves):
            low = jnp.minimum(low, span_ref[0, k * halves + h])
            high = jnp.maximum(high, span_ref[SUB, k * halves + h])

        def block(b, values):
            values = list(values)
            for r in range(chunks):
                match = [n == b * chunks + r for n in number]
                for c in range(FIELDS):
                    row = jnp.broadcast_to(table[b, c, r : r + 1, :], (SUB, LANES))
                    for h in range(halves):
                        found = jnp.take_along_axis(row, at[h], axis=1)
                        values[h * FIELDS + c] = jnp.where(match[h], found, values[h * FIELDS + c])
            return tuple(values)

        zeros = tuple(jnp.zeros((SUB, LANES), f32) for _ in range(FIELDS * halves))
        other = lax.fori_loop(low, high + 1, block, zeros)
        sums = list(sums)
        for h in range(halves):
            own = [table[centre, c, h * SUB : (h + 1) * SUB, :] for c in range(FIELDS)]
            diff = [own[c] - other[h * FIELDS + c] for c in range(FIELDS)]
            e = [terms_ref[c, rows[h], :] for c in range(3)]
            c1 = terms_ref[3, rows[h], :]
            size = e[0] * e[0] + e[1] * e[1] + e[2] * e[2]
            c2 = c1 * (1.0 - size)
            p = e[0] * diff[0] + e[1] * diff[1] + e[2] * diff[2]
            t = e[0] * diff[3] + e[1] * diff[4] + e[2] * diff[5]
            mix = 0.8 * c1
            along_top = 6.0 * c2 * p + mix * t
            along_bottom = mix * p - 2.0 * c1 * t
            cross = mix * (size * (1.0 / 3.0))
            strong = 2.5 * c1
            for c in range(3):
                top = e[c] * along_top + c1 * diff[c] - cross * diff[3 + c]
                bottom = e[c] * along_bottom - cross * diff[c] + strong * diff[3 + c]
                sums[h * FIELDS + c] = sums[h * FIELDS + c] + top
                sums[h * FIELDS + 3 + c] = sums[h * FIELDS + 3 + c] + bottom
        return tuple(sums)

    start = []
    for h in range(halves):
        for c in range(FIELDS):
            own = table[centre, c, h * SUB : (h + 1) * SUB, :]
            start.append(drag_ref[c * chunks + h * SUB : c * chunks + (h + 1) * SUB, :] * own)
    sums = lax.fori_loop(0, K, slot, tuple(start))
    for h in range(halves):
        for c in range(FIELDS):
            out_ref[c, h * SUB : (h + 1) * SUB, :] = sums[h * FIELDS + c]


def total(x):
    x = jnp.sum(x, axis=0)
    return jnp.sum(jnp.sum(x, axis=0, keepdims=True), axis=1, keepdims=True)


def put_dots(dots_ref, values):
    lane = iota((1, LANES), 1)
    row = jnp.zeros((1, LANES), f32)
    for k, value in enumerate(values):
        row = jnp.where(lane == k, value, row)
    dots_ref[...] = jnp.broadcast_to(row, dots_ref.shape)


def join(table, west, mid, east):
    for y in range(3):
        table[y] = west[y]
        table[3 + y] = mid[y]
        table[6 + y] = east[y]


def first_kernel(span, col, terms, drag, west, mid, east, drag_out, r_out, s_out, dots_out):
    chunks = s_out.shape[1]
    for r in range(chunks):
        drag_out[pl.ds(r, FIELDS, stride=chunks), :] = drag[:, r * LANES : (r + 1) * LANES]
    join(r_out, west, mid, east)
    apply_operator(r_out, span, col, terms, drag_out, s_out)
    r = r_out[4]
    put_dots(dots_out, [total(r * r), total(r * s_out[...])])


def next_kernel(
    first, span, col, terms, drag, west, mid, east, r_in, w_in, d_in, v_in, scal_in, dots,
    r_out, w_out, d_out, v_out, scal_out, s_out, dots_out,
):
    beta, step = scalars(first, dots, scal_in, scal_out)
    parts = [(west, 0), (mid, 3), (east, 6)]
    for part, base in parts:
        for y in range(3):
            w = part[y]
            if not first:
                w = w + beta * w_in[base + y]
            w_out[base + y] = w
            r_out[base + y] = r_in[base + y] - step * w
    d = r_in[4]
    if first:
        v_out[...] = step * d
    else:
        d = d + beta * d_in[...]
        v_out[...] = v_in[...] + step * d
    d_out[...] = d
    apply_operator(r_out, span, col, terms, drag, s_out)
    r = r_out[4]
    s = s_out[...]
    put_dots(dots_out, [total(r * r), total(r * s), total(r * w_out[4] + d * s)])


def scalars(first, dots, scal_in, scal_out):
    row = jnp.sum(dots[...], axis=0, keepdims=True)
    rr = lane_pick(row, 0)
    rs = lane_pick(row, 1)
    if first:
        beta = None
        dad = rs
    else:
        old = scal_in[0:1, :]
        beta = rr / lane_pick(old, 0)
        dad = rs + beta * (lane_pick(row, 2) + beta * lane_pick(old, 1))
    if scal_out is not None:
        put_dots(scal_out, [rr, dad])
    return beta, rr / dad


def last_kernel(s_in, r_in, w_in, d_in, v_in, scal_in, dots, v_final, r_final, v_s, r_s):
    beta, step = scalars(False, dots, scal_in, None)
    chunks = s_in.shape[1]
    for c in range(FIELDS):
        w = s_in[c] + beta * w_in[4, c]
        d = r_in[4, c] + beta * d_in[c]
        v_s[c * chunks : (c + 1) * chunks, :] = v_in[c] + step * d
        r_s[c * chunks : (c + 1) * chunks, :] = r_in[4, c] - step * w
    for r in range(chunks):
        v_final[:, r * LANES : (r + 1) * LANES] = v_s[pl.ds(r, FIELDS, stride=chunks), :]
        r_final[:, r * LANES : (r + 1) * LANES] = r_s[pl.ds(r, FIELDS, stride=chunks), :]


VMEM = pl.BlockSpec(memory_space=pltpu.VMEM)
SMEM = pl.BlockSpec(memory_space=pltpu.SMEM)


def shapes(*dims):
    return tuple(jax.ShapeDtypeStruct(d, f32) for d in dims)


def ring(axis, step):
    count = lax.axis_size(axis)
    return [(i, (i + step) % count) for i in range(count)]


def beside(x):
    below = lax.ppermute(x, "gy", ring("gy", 1))
    above = lax.ppermute(x, "gy", ring("gy", -1))
    mid = jnp.stack([below, x, above])
    west = lax.ppermute(mid, "gx", ring("gx", 1))
    east = lax.ppermute(mid, "gx", ring("gx", -1))
    return west, mid, east


def share(dots):
    return lax.all_to_all(dots, ("gx", "gy"), split_axis=0, concat_axis=0, tiled=True)


def on_device(pair_ends, pair_geometry, drag_coef, forces):
    spheres = drag_coef.shape[1]
    chunks = spheres // LANES
    slabs = lax.axis_size("gx")
    strips = lax.axis_size("gy")
    devices = slabs * strips
    send, force_rows = pack(pair_ends, pair_geometry, forces, slabs, strips)
    got = lax.all_to_all(send, "gx", split_axis=0, concat_axis=0, tiled=True)
    field = (FIELDS, chunks, LANES)
    table = (9, FIELDS, chunks, LANES)
    west, mid, east = beside(force_rows.reshape(field))
    terms, col, span = place_entries(got, spheres)
    drag, r, s, dots = pl.pallas_call(
        first_kernel,
        out_shape=shapes((FIELDS * chunks, LANES), table, field, (devices, LANES)),
        in_specs=[SMEM] + [VMEM] * 6,
        name="first",
    )(span, col, terms, drag_coef, west, mid, east)
    w = d = v = scal = None
    for iteration in range(1, ITERS):
        first = iteration == 1
        west, mid, east = beside(s)
        shared = share(dots)
        state = [r] if first else [r, w, d, v, scal]

        def kernel(*refs, first=first):
            refs = list(refs)
            if first:
                refs[8:8] = [None] * 4
            next_kernel(first, *refs)

        r, w, d, v, scal, s, dots = pl.pallas_call(
            kernel,
            out_shape=shapes(table, table, field, field, (SUB, LANES), field, (devices, LANES)),
            in_specs=[SMEM] + [VMEM] * (6 + len(state) + 1),
            name=f"next{iteration}",
        )(span, col, terms, drag, west, mid, east, *state, shared)
    return pl.pallas_call(
        last_kernel,
        out_shape=shapes((FIELDS, spheres), (FIELDS, spheres)),
        scratch_shapes=[pltpu.VMEM((FIELDS * chunks, LANES), f32)] * 2,
        name="last",
    )(s, r, w, d, v, scal, share(dots))


def solution(mesh):
    spec = P(None, ("gx", "gy"))
    return jax.shard_map(
        on_device, mesh=mesh, in_specs=(spec,) * 4, out_specs=(spec, spec), check_vma=False
    )
```

time: 1250 us -> 129 us (0.10)
  local copies, waits for them, and re-layouts: 886 us -> 3 us
  blocking collectives: 205 us -> 32.4 us
  other arithmetic: 103 us -> 1.65 us
  Pallas kernels: 0 us -> 48.3 us
    gather x54 -> x0, local copies, waits for them, and re-layouts: 673 us -> none  [the longest x3 336 us: on_device(): gathered = jnp.take(neighbourhood, columns, axis=1).reshape(6, K, spheres)]
    psum x5 -> x0, blocking collectives: 205 us -> none  [the longest x3 122 us: squares(): return lax.psum(jnp.sum(residual * residual), ('gx', 'gy'))]
    scatter x1 -> x0, local copies, waits for them, and re-layouts: 120 us -> none  [on_device(): position_of = jnp.full((slot_total + 1,), arrived_count, jnp.int32).at[ar...]
    select_n x8 -> x0, other arithmetic: 61.3 us -> none  [the longest x3 53.8 us: on_device(): gathered = jnp.take(neighbourhood, columns, axis=1).reshape(6, K, spheres)]
    pallas_call x0 -> x6, Pallas kernels: none -> 48.3 us  [the longest x1 21.3 us: place_entries(): pl.pallas_call(functools.partial(place_kernel, spheres), out_shape=(jax.S...]
    all_to_all x0 -> x3, blocking collectives: none -> 32.4 us  [share(): lax.all_to_all(dots, ('gx', 'gy'), split_axis=0, concat_axis=0, tiled=True)]
    concatenate x6 -> x0, local copies, waits for them, and re-layouts: 30.4 us -> none  [the longest x3 15.3 us: extended(): jnp.concatenate([lax.ppermute(tail, axis, [(i, (i + 1) % count) for i in...]
    sub x3 -> x0, local copies, waits for them, and re-layouts: 30.3 us -> none  [on_device(): change = direction[:, None, :] - gathered]
  transfers between devices with their start and end apart: 14 -> 13, of which waited for: 8 -> 7; matrix products, arithmetic and copies ran while one was open for 41% -> 0% of each run, Pallas kernels for 0% -> 17%
where the time goes in v1:
time: 129 us; the launch traced here: 128 us
  Pallas kernels  48.3 us (37%)
  blocking collectives  32.4 us (25%)
  waiting for transfers between devices  23.4 us (18%)
  starting transfers between devices  18.8 us (15%)
  local copies, waits for them, and re-layouts  3 us (2%)
  other arithmetic  1.65 us (1%)
    all_to_all x3, blocking collectives, share(): lax.all_to_all(dots, ('gx', 'gy'), split_axis=0, concat_axis=0, tiled=True)  32.4 us
    pallas_call x1, Pallas kernels, place_entries(): pl.pallas_call(functools.partial(place_kernel, spheres), out_shape=(jax.S...  21.3 us
    pallas_call x2, Pallas kernels, on_device(): pl.pallas_call(kernel, out_shape=shapes(table, table, field, field, (SUB,...  15.1 us
    all_to_all x1, waiting for transfers between devices, on_device(): got = lax.all_to_all(send, 'gx', split_axis=0, concat_axis=0, tiled=True)  12.7 us
    all_to_all x1, starting transfers between devices, on_device(): got = lax.all_to_all(send, 'gx', split_axis=0, concat_axis=0, tiled=True)  7.38 us
    pallas_call x1, Pallas kernels, on_device(): pl.pallas_call(first_kernel, out_shape=shapes((FIELDS * chunks, LANES), t...  7.01 us
    ppermute x3, starting transfers between devices, beside(): east = lax.ppermute(mid, 'gx', ring('gx', -1))  6.81 us
    ppermute x3, waiting for transfers between devices, beside(): below = lax.ppermute(x, 'gy', ring('gy', 1))  5.86 us
  transfers between devices with their start and end apart: 13, of which 7 were waited for; matrix products, arithmetic and copies ran while one was open for 0% of the time, Pallas kernels for 17%

profile of v1, /device:TPU:0, one launch (start us, length us, event | category | flops | bytes accessed | tf_op | source)
XLA Modules:
  0.0 128.4 jit_solution(2707136722635864679)
XLA Ops:
  0.6 2.9 %pack.1 = (f32[8,6,32,128]{3,2,1,0:T(8,128)}, f32[96,128]{1,0:T(8,128)}) custom-call(s32[3,14464]{1,0:T(4,128)} %ends_ref.1, f32[5,14464]{1,0:T(8,128)} %geo_ref.1, f32[6,2048]{1,0:T(8,128)} %force_ref.1), custom_call_target="tpu_custom_call" | custom-call | tf_op jit(solution)/shard_map/pack/pallas_call | solution.py:88
  3.5 7.4 %all-to-all-start = ((f32[8,6,32,128]{3,2,1,0:T(8,128)}), f32[8,6,32,128]{3,2,1,0:T(8,128)S(1)}, u32[]{:S(2)}, u32[]{:S(2)}) async-start(f32[8,6,32,128]{3,2,1,0:T(8,128)} %get-tuple-element.25), calls=%async_computation | async-start | bytes 1572864 | tf_op jit(solution)/shard_map/all_to_all | solution.py:422
  10.9 0.7 collective-permute-start.1
  11.7 1.8 %collective-permute-done.1 = f32[6,16,128]{2,1,0:T(8,128)S(1)} collective-permute-done((f32[6,16,128]{2,1,0:T(8,128)S(1)}, f32[6,16,128]{2,1,0:T(8,128)S(1)}, u32[]{:S(2)}, u32[]{:S(2)}) %collective-permute-start.1) | collective-permute-done | bytes 49184 | tf_op jit(solution)/shard_map/ppermute | solution.py:404
  13.5 1.7 %collective-permute-done = f32[6,16,128]{2,1,0:T(8,128)S(1)} collective-permute-done((f32[6,16,128]{2,1,0:T(8,128)S(1)}, f32[6,16,128]{2,1,0:T(8,128)S(1)}, u32[]{:S(2)}, u32[]{:S(2)}) %collective-permute-start) | collective-permute-done | bytes 49184 | tf_op jit(solution)/shard_map/ppermute | solution.py:403
  15.2 4.6 %collective-permute-start.3 = (f32[3,6,16,128]{3,2,1,0:T(8,128)S(1)}, f32[3,6,16,128]{3,2,1,0:T(8,128)S(1)}, u32[]{:S(2)}, u32[]{:S(2)}) collective-permute-start(f32[3,6,16,128]{3,2,1,0:T(8,128)S(1)} %pad_maximum_fusion.mid), channel_id=1, source_target_pairs={{0,28},{4,0},{8,4},{12,8},{16,12},{20,16},{24,20},{28,24},{1,29},{... | collective-permute-start | bytes 442376 | tf_op jit(solution)/shard_map/ppermute | solution.py:407
  19.8 12.7 %all-to-all-done.got_ref = f32[8,6,32,128]{3,2,1,0:T(8,128)S(1)} async-done(((f32[8,6,32,128]{3,2,1,0:T(8,128)}), f32[8,6,32,128]{3,2,1,0:T(8,128)S(1)}, u32[]{:S(2)}, u32[]{:S(2)}) %all-to-all-start) | async-done | bytes 786464 | tf_op jit(solution)/shard_map/all_to_all | solution.py:422
  32.5 0.9 copy-done
  33.4 21.3 %place.1 = (f32[4,256,128]{2,1,0:T(8,128)}, s32[256,128]{1,0:T(8,128)}, s32[16,128]{1,0:T(8,128)}) custom-call(f32[8,6,32,128]{3,2,1,0:T(8,128)} %copy-done), custom_call_target="tpu_custom_call" | custom-call | tf_op jit(solution)/shard_map/place/pallas_call | solution.py:216
  54.7 0.6 copy-done.6
  55.4 7.0 %first.1 = (f32[96,128]{1,0:T(8,128)}, f32[9,6,16,128]{3,2,1,0:T(8,128)}, f32[6,16,128]{2,1,0:T(8,128)}, f32[32,128]{1,0:T(8,128)}) custom-call(s32[16,128]{1,0:T(8,128)} %get-tuple-element.26.span.refs_0_, s32[256,128]{1,0:T(8,128)} %get-tuple-element.27.col.refs_1_, f32[4,256,128]{2,1,0:T(8,128)} %get-tuple-element.28.terms.refs_2_, f32[6,2048]{1,0:T(8,128)} %drag.1, ...), custom_call_target="tpu_custom_call" | custom-call | tf_op jit(solution)/shard_map/first/pallas_call | solution.py:427
  62.4 0.5 collective-permute-start.4
  62.9 1.6 %collective-permute-done.5 = f32[6,16,128]{2,1,0:T(8,128)S(1)} collective-permute-done((f32[6,16,128]{2,1,0:T(8,128)}, f32[6,16,128]{2,1,0:T(8,128)S(1)}, u32[]{:S(2)}, u32[]{:S(2)}) %collective-permute-start.5) | collective-permute-done | bytes 49184 | tf_op jit(solution)/shard_map/ppermute | solution.py:404
  64.5 2.0 %collective-permute-done.4 = f32[6,16,128]{2,1,0:T(8,128)S(1)} collective-permute-done((f32[6,16,128]{2,1,0:T(8,128)}, f32[6,16,128]{2,1,0:T(8,128)S(1)}, u32[]{:S(2)}, u32[]{:S(2)}) %collective-permute-start.4) | collective-permute-done | bytes 49184 | tf_op jit(solution)/shard_map/ppermute | solution.py:403
  66.5 0.8 pad_maximum_fusion.1.refs_5_
  67.4 1.5 %collective-permute-start.7 = (f32[3,6,16,128]{3,2,1,0:T(8,128)S(1)}, f32[3,6,16,128]{3,2,1,0:T(8,128)S(1)}, u32[]{:S(2)}, u32[]{:S(2)}) collective-permute-start(f32[3,6,16,128]{3,2,1,0:T(8,128)S(1)} %pad_maximum_fusion.1.refs_5_), channel_id=1, source_target_pairs={{0,28},{4,0},{8,4},{12,8},{16,12},{20,16},{24,20},{28,24},{1,29},{... | collective-permute-start | bytes 442376 | tf_op jit(solution)/shard_map/ppermute | solution.py:407
  68.8 1.4 %collective-permute-start.6 = (f32[3,6,16,128]{3,2,1,0:T(8,128)S(1)}, f32[3,6,16,128]{3,2,1,0:T(8,128)S(1)}, u32[]{:S(2)}, u32[]{:S(2)}) collective-permute-start(f32[3,6,16,128]{3,2,1,0:T(8,128)S(1)} %pad_maximum_fusion.1.refs_5_), channel_id=1, source_target_pairs={{0,4},{4,8},{8,12},{12,16},{16,20},{20,24},{24,28},{28,0},{1,5},{5... | collective-permute-start | bytes 442376 | tf_op jit(solution)/shard_map/ppermute | solution.py:406
  70.3 11.1 %all_to_all.38 = f32[32,1,128]{2,1,0:T(1,128)} all-to-all(f32[32,1,128]{2,1,0:T(1,128)S(1)} %bitcast.37), channel_id=1, replica_groups=mesh['gx'=8,'gy'=4] {'gx','gy'}, dimensions={0} | all-to-all | bytes 32768 | tf_op jit(solution)/shard_map/all_to_all | solution.py:412
  81.4 0.6 copy-done.8
  82.1 7.4 %next1.1 = (f32[9,6,16,128]{3,2,1,0:T(8,128)}, f32[9,6,16,128]{3,2,1,0:T(8,128)}, f32[6,16,128]{2,1,0:T(8,128)}, f32[6,16,128]{2,1,0:T(8,128)}, f32[8,128]{1,0:T...) custom-call(s32[16,128]{1,0:T(8,128)} %get-tuple-element.26.span.refs_0_, s32[256,128]{1,0:T(8,128)} %get-tuple-element.27.col.refs_1_, ...), custom_call_target="tpu_custom_call" | custom-call | tf_op jit(solution)/shard_map/next1/pallas_call | solution.py:446
  89.6 0.5 collective-permute-start.8
  90.1 1.6 %collective-permute-done.9 = f32[6,16,128]{2,1,0:T(8,128)S(1)} collective-permute-done((f32[6,16,128]{2,1,0:T(8,128)}, f32[6,16,128]{2,1,0:T(8,128)S(1)}, u32[]{:S(2)}, u32[]{:S(2)}) %collective-permute-start.9) | collective-permute-done | bytes 49184 | tf_op jit(solution)/shard_map/ppermute | solution.py:404
  91.7 2.1 %collective-permute-done.8 = f32[6,16,128]{2,1,0:T(8,128)S(1)} collective-permute-done((f32[6,16,128]{2,1,0:T(8,128)}, f32[6,16,128]{2,1,0:T(8,128)S(1)}, u32[]{:S(2)}, u32[]{:S(2)}) %collective-permute-start.8) | collective-permute-done | bytes 49184 | tf_op jit(solution)/shard_map/ppermute | solution.py:403
  93.8 0.8 pad_maximum_fusion.2.refs_5_
  94.6 0.7 collective-permute-start.11
  95.3 1.4 %collective-permute-start.10 = (f32[3,6,16,128]{3,2,1,0:T(8,128)S(1)}, f32[3,6,16,128]{3,2,1,0:T(8,128)S(1)}, u32[]{:S(2)}, u32[]{:S(2)}) collective-permute-start(f32[3,6,16,128]{3,2,1,0:T(8,128)S(1)} %pad_maximum_fusion.2.refs_5_), channel_id=1, source_target_pairs={{0,4},{4,8},{8,12},{12,16},{16,20},{20,24},{24,28},{28,0},{1,5},{5... | collective-permute-start | bytes 442376 | tf_op jit(solution)/shard_map/ppermute | solution.py:406
  96.7 11.2 %all_to_all.39 = f32[32,1,128]{2,1,0:T(1,128)} all-to-all(f32[32,1,128]{2,1,0:T(1,128)S(1)} %bitcast.36), channel_id=1, replica_groups=mesh['gx'=8,'gy'=4] {'gx','gy'}, dimensions={0} | all-to-all | bytes 32768 | tf_op jit(solution)/shard_map/all_to_all | solution.py:412
  107.9 0.6 copy-done.4
  108.5 0.1 copy-done.5
  108.6 7.7 %next2.1 = (f32[9,6,16,128]{3,2,1,0:T(8,128)}, f32[9,6,16,128]{3,2,1,0:T(8,128)}, f32[6,16,128]{2,1,0:T(8,128)}, f32[6,16,128]{2,1,0:T(8,128)}, f32[8,128]{1,0:T...) custom-call(s32[16,128]{1,0:T(8,128)} %get-tuple-element.26.span.refs_0_, s32[256,128]{1,0:T(8,128)} %get-tuple-element.27.col.refs_1_, ...), custom_call_target="tpu_custom_call" | custom-call | tf_op jit(solution)/shard_map/next2/pallas_call | solution.py:446
  116.3 10.1 %all_to_all.40 = f32[32,1,128]{2,1,0:T(1,128)} all-to-all(f32[32,1,128]{2,1,0:T(1,128)} %bitcast.38), channel_id=1, replica_groups=mesh['gx'=8,'gy'=4] {'gx','gy'}, dimensions={0} | all-to-all | bytes 32768 | tf_op jit(solution)/shard_map/all_to_all | solution.py:412
  126.4 2.0 %last.1 = (f32[6,2048]{1,0:T(8,128)}, f32[6,2048]{1,0:T(8,128)}) custom-call(f32[6,16,128]{2,1,0:T(8,128)} %get-tuple-element.41.s_in, f32[9,6,16,128]{3,2,1,0:T(8,128)} %get-tuple-element.42.r_in, f32[9,6,16,128]{3,2,1,0:T(8,128)} %get-tuple-element.43.w_in, f32[6,16,128]{2,1,0:T(8,128)} %get-tuple-element.44.d_in, f32[6,16,128]{2,1,0:T(8,128)} %get-tuple-element.45.v_in, ...), custom_call_target="tpu_custom_call" | custom-call | tf_op jit(solution)/shard_map/last/pallas_call | solution.py:452
  (32 shorter events, 0.2 us)
Async XLA Ops:
  3.5 7.4 %copy-start.10 = (f32[96,128]{1,0:T(8,128)S(1)}, f32[96,128]{1,0:T(8,128)}, u32[]{:S(2)}) copy-start(f32[96,128]{1,0:T(8,128)} %get-tuple-element.29) | copy-start | bytes 147460
  3.5 29.0 %all-to-all-start = ((f32[8,6,32,128]{3,2,1,0:T(8,128)}), f32[8,6,32,128]{3,2,1,0:T(8,128)S(1)}, u32[]{:S(2)}, u32[]{:S(2)}) async-start(f32[8,6,32,128]{3,2,1,0:T(8,128)} %get-tuple-element.25), calls=%async_computation | async-start | bytes 1572864 | tf_op jit(solution)/shard_map/all_to_all | solution.py:422
  10.9 2.5 %collective-permute-start.1 = (f32[6,16,128]{2,1,0:T(8,128)S(1)}, f32[6,16,128]{2,1,0:T(8,128)S(1)}, u32[]{:S(2)}, u32[]{:S(2)}) collective-permute-start(f32[6,16,128]{2,1,0:T(8,128)S(1)} %bitcast.26), channel_id=1, source_target_pairs={{0,3},{1,0},{2,1},{3,2},{4,7},{5,4},{6,5},{7,6},{8,11},{9,8},{10,9... | collective-permute-start | bytes 147464 | tf_op jit(solution)/shard_map/ppermute | solution.py:404
  11.6 3.5 %collective-permute-start = (f32[6,16,128]{2,1,0:T(8,128)S(1)}, f32[6,16,128]{2,1,0:T(8,128)S(1)}, u32[]{:S(2)}, u32[]{:S(2)}) collective-permute-start(f32[6,16,128]{2,1,0:T(8,128)S(1)} %bitcast.27), channel_id=1, source_target_pairs={{0,1},{1,2},{2,3},{3,0},{4,5},{5,6},{6,7},{7,4},{8,9},{9,10},{10,1... | collective-permute-start | bytes 147464 | tf_op jit(solution)/shard_map/ppermute | solution.py:403
  15.2 39.5 %copy-start.2 = (f32[3,6,16,128]{3,2,1,0:T(8,128)}, f32[3,6,16,128]{3,2,1,0:T(8,128)S(1)}, u32[]{:S(2)}) copy-start(f32[3,6,16,128]{3,2,1,0:T(8,128)S(1)} %pad_maximum_fusion.mid) | copy-start | bytes 442372
  15.2 39.5 %collective-permute-start.3 = (f32[3,6,16,128]{3,2,1,0:T(8,128)S(1)}, f32[3,6,16,128]{3,2,1,0:T(8,128)S(1)}, u32[]{:S(2)}, u32[]{:S(2)}) collective-permute-start(f32[3,6,16,128]{3,2,1,0:T(8,128)S(1)} %pad_maximum_fusion.mid), channel_id=1, source_target_pairs={{0,28},{4,0},{8,4},{12,8},{16,12},{20,16},{24,20},{28,24},{1,29},{... | collective-permute-start | bytes 442376 | tf_op jit(solution)/shard_map/ppermute | solution.py:407
  19.8 34.9 %collective-permute-start.2 = (f32[3,6,16,128]{3,2,1,0:T(8,128)S(1)}, f32[3,6,16,128]{3,2,1,0:T(8,128)S(1)}, u32[]{:S(2)}, u32[]{:S(2)}) collective-permute-start(f32[3,6,16,128]{3,2,1,0:T(8,128)S(1)} %pad_maximum_fusion.mid), channel_id=1, source_target_pairs={{0,4},{4,8},{8,12},{12,16},{16,20},{20,24},{24,28},{28,0},{1,5},{5... | collective-permute-start | bytes 442376 | tf_op jit(solution)/shard_map/ppermute | solution.py:406
  32.5 0.9 copy-start
  54.7 0.7 copy-start.6
  54.7 0.7 copy-start.7
  62.4 2.1 %collective-permute-start.5 = (f32[6,16,128]{2,1,0:T(8,128)}, f32[6,16,128]{2,1,0:T(8,128)S(1)}, u32[]{:S(2)}, u32[]{:S(2)}) collective-permute-start(f32[6,16,128]{2,1,0:T(8,128)} %get-tuple-element.31), channel_id=1, source_target_pairs={{0,3},{1,0},{2,1},{3,2},{4,7},{5,4},{6,5},{7,6},{8,11},{9,8},{10,9... | collective-permute-start | bytes 147464 | tf_op jit(solution)/shard_map/ppermute | solution.py:404
  62.4 4.1 %collective-permute-start.4 = (f32[6,16,128]{2,1,0:T(8,128)}, f32[6,16,128]{2,1,0:T(8,128)S(1)}, u32[]{:S(2)}, u32[]{:S(2)}) collective-permute-start(f32[6,16,128]{2,1,0:T(8,128)} %get-tuple-element.31), channel_id=1, source_target_pairs={{0,1},{1,2},{2,3},{3,0},{4,5},{5,6},{6,7},{7,4},{8,9},{9,10},{10,1... | collective-permute-start | bytes 147464 | tf_op jit(solution)/shard_map/ppermute | solution.py:403
  66.5 3.7 %copy-start.12 = (f32[32,128]{1,0:T(8,128)S(1)}, f32[32,128]{1,0:T(8,128)}, u32[]{:S(2)}) copy-start(f32[32,128]{1,0:T(8,128)} %get-tuple-element.33) | copy-start | bytes 49156
  67.4 14.0 %copy-start.3 = (f32[3,6,16,128]{3,2,1,0:T(8,128)}, f32[3,6,16,128]{3,2,1,0:T(8,128)S(1)}, u32[]{:S(2)}) copy-start(f32[3,6,16,128]{3,2,1,0:T(8,128)S(1)} %pad_maximum_fusion.1.refs_5_) | copy-start | bytes 442372
  67.4 14.0 %collective-permute-start.7 = (f32[3,6,16,128]{3,2,1,0:T(8,128)S(1)}, f32[3,6,16,128]{3,2,1,0:T(8,128)S(1)}, u32[]{:S(2)}, u32[]{:S(2)}) collective-permute-start(f32[3,6,16,128]{3,2,1,0:T(8,128)S(1)} %pad_maximum_fusion.1.refs_5_), channel_id=1, source_target_pairs={{0,28},{4,0},{8,4},{12,8},{16,12},{20,16},{24,20},{28,24},{1,29},{... | collective-permute-start | bytes 442376 | tf_op jit(solution)/shard_map/ppermute | solution.py:407
  68.8 12.6 %collective-permute-start.6 = (f32[3,6,16,128]{3,2,1,0:T(8,128)S(1)}, f32[3,6,16,128]{3,2,1,0:T(8,128)S(1)}, u32[]{:S(2)}, u32[]{:S(2)}) collective-permute-start(f32[3,6,16,128]{3,2,1,0:T(8,128)S(1)} %pad_maximum_fusion.1.refs_5_), channel_id=1, source_target_pairs={{0,4},{4,8},{8,12},{12,16},{16,20},{20,24},{24,28},{28,0},{1,5},{5... | collective-permute-start | bytes 442376 | tf_op jit(solution)/shard_map/ppermute | solution.py:406
  81.4 0.7 copy-start.8
  81.4 0.7 copy-start.9
  89.5 2.1 %collective-permute-start.9 = (f32[6,16,128]{2,1,0:T(8,128)}, f32[6,16,128]{2,1,0:T(8,128)S(1)}, u32[]{:S(2)}, u32[]{:S(2)}) collective-permute-start(f32[6,16,128]{2,1,0:T(8,128)} %get-tuple-element.34), channel_id=1, source_target_pairs={{0,3},{1,0},{2,1},{3,2},{4,7},{5,4},{6,5},{7,6},{8,11},{9,8},{10,9... | collective-permute-start | bytes 147464 | tf_op jit(solution)/shard_map/ppermute | solution.py:404
  89.6 4.2 %collective-permute-start.8 = (f32[6,16,128]{2,1,0:T(8,128)}, f32[6,16,128]{2,1,0:T(8,128)S(1)}, u32[]{:S(2)}, u32[]{:S(2)}) collective-permute-start(f32[6,16,128]{2,1,0:T(8,128)} %get-tuple-element.34), channel_id=1, source_target_pairs={{0,1},{1,2},{2,3},{3,0},{4,5},{5,6},{6,7},{7,4},{8,9},{9,10},{10,1... | collective-permute-start | bytes 147464 | tf_op jit(solution)/shard_map/ppermute | solution.py:403
  93.8 2.9 %copy-start.11 = (f32[32,128]{1,0:T(8,128)S(1)}, f32[32,128]{1,0:T(8,128)}, u32[]{:S(2)}) copy-start(f32[32,128]{1,0:T(8,128)} %get-tuple-element.40) | copy-start | bytes 49156
  94.6 13.3 %copy-start.1 = (f32[3,6,16,128]{3,2,1,0:T(8,128)}, f32[3,6,16,128]{3,2,1,0:T(8,128)S(1)}, u32[]{:S(2)}) copy-start(f32[3,6,16,128]{3,2,1,0:T(8,128)S(1)} %pad_maximum_fusion.2.refs_5_) | copy-start | bytes 442372
  94.6 13.3 %collective-permute-start.11 = (f32[3,6,16,128]{3,2,1,0:T(8,128)S(1)}, f32[3,6,16,128]{3,2,1,0:T(8,128)S(1)}, u32[]{:S(2)}, u32[]{:S(2)}) collective-permute-start(f32[3,6,16,128]{3,2,1,0:T(8,128)S(1)} %pad_maximum_fusion.2.refs_5_), channel_id=1, source_target_pairs={{0,28},{4,0},{8,4},{12,8},{16,12},{20,16},{24,20},{28,24},{1,29},{... | collective-permute-start | bytes 442376 | tf_op jit(solution)/shard_map/ppermute | solution.py:407
  95.3 12.6 %collective-permute-start.10 = (f32[3,6,16,128]{3,2,1,0:T(8,128)S(1)}, f32[3,6,16,128]{3,2,1,0:T(8,128)S(1)}, u32[]{:S(2)}, u32[]{:S(2)}) collective-permute-start(f32[3,6,16,128]{3,2,1,0:T(8,128)S(1)} %pad_maximum_fusion.2.refs_5_), channel_id=1, source_target_pairs={{0,4},{4,8},{8,12},{12,16},{16,20},{20,24},{24,28},{28,0},{1,5},{5... | collective-permute-start | bytes 442376 | tf_op jit(solution)/shard_map/ppermute | solution.py:406
  107.9 0.7 copy-start.4
  107.9 0.7 copy-start.5

commit v2 on v1

v2 whole, which is shorter than its diff:
```python
import functools

import jax
import jax.numpy as jnp
from jax import lax
from jax.experimental import pallas as pl
from jax.experimental.pallas import tpu as pltpu
from jax.sharding import PartitionSpec as P

K = 16
ITERS = 3
LANES = 128
SUB = 8
FIELDS = 6
SENT = 6

f32 = jnp.float32
i32 = jnp.int32
bf16 = jnp.bfloat16


def log2(n):
    assert n & (n - 1) == 0
    return n.bit_length() - 1


def iota(shape, dim):
    return lax.broadcasted_iota(i32, shape, dim)


def pack_kernel(slabs, strips, spheres, ends_ref, geo_ref, force_ref, label_ref, send_ref, dense_ref, ends_s, geo_s, out_s):
    rows = ends_ref.shape[1] // LANES
    padded = ends_s.shape[0] // 3
    cap_rows = label_ref.shape[1]
    chunks = spheres // LANES
    for r in range(rows):
        cols = slice(r * LANES, (r + 1) * LANES)
        ends_s[pl.ds(r, 3, stride=padded), :] = ends_ref[:, cols]
        geo_s[pl.ds(r, 5, stride=padded), :] = geo_ref[:, cols]
    for r in range(chunks):
        dense_ref[pl.ds(r, FIELDS, stride=chunks), :] = force_ref[:, r * LANES : (r + 1) * LANES]
    first = ends_s[0:padded, :]
    second = ends_s[padded : 2 * padded, :]
    slot = ends_s[2 * padded : 3 * padded, :]
    inside = iota((padded, LANES), 0) < rows
    live = jnp.logical_and(slot < K, inside)
    shift = log2(spheres)
    first_block = first >> shift
    second_block = second >> shift
    owner = first_block >> log2(strips)
    shift_x = ((second_block >> log2(strips)) - owner + 1) & (slabs - 1)
    shift_y = ((second_block & (strips - 1)) - (first_block & (strips - 1)) + 1) & (strips - 1)
    column = (shift_y * 3 + shift_x) * spheres + (second & (spheres - 1))
    target = slot * spheres + (first & (spheres - 1))
    owner = jnp.where(live, owner, slabs)
    sep = [geo_s[c * padded : (c + 1) * padded, :] for c in range(3)]
    a = geo_s[3 * padded : 4 * padded, :]
    b = geo_s[4 * padded : 5 * padded, :]
    h = a + b
    total = sep[0] * sep[0] + sep[1] * sep[1] + sep[2] * sep[2] + h * h
    inv = lax.rsqrt(total)
    values = [target.astype(f32), column.astype(f32)] + [d * inv for d in sep] + [a * b * h * (inv * inv)]
    for c, value in enumerate(values):
        out_s[c, 0:padded, :] = value
    lane = iota((cap_rows, LANES), 1)
    place = iota((cap_rows, LANES), 0) * LANES + lane
    start = jnp.int32(0)
    for o in range(slabs):
        end = jnp.sum(jnp.where(owner <= o, 1.0, 0.0)).astype(i32)
        row = start >> 7
        off = start & (LANES - 1)
        back = (LANES - off) & (LANES - 1)
        for c in range(SENT):
            here = pltpu.roll(out_s[c, pl.ds(row, cap_rows), :], back, 1)
            after = pltpu.roll(out_s[c, pl.ds(row + 1, cap_rows), :], back, 1)
            value = jnp.where(lane < LANES - off, here, after)
            if c == 0:
                label_ref[o] = jnp.where(place < end - start, value, -1.0)
            else:
                send_ref[o, c - 1] = value
        start = end


def pack(ends, geo, forces, slabs, strips):
    spheres = forces.shape[1]
    cap_rows = spheres * K // slabs // LANES
    rows = ends.shape[1] // LANES
    padded = -(-rows // SUB) * SUB
    return pl.pallas_call(
        functools.partial(pack_kernel, slabs, strips, spheres),
        out_shape=(
            jax.ShapeDtypeStruct((slabs, cap_rows, LANES), f32),
            jax.ShapeDtypeStruct((slabs, SENT - 1, cap_rows, LANES), f32),
            jax.ShapeDtypeStruct((FIELDS * spheres // LANES, LANES), f32),
        ),
        scratch_shapes=[
            pltpu.VMEM((3 * padded, LANES), i32),
            pltpu.VMEM((5 * padded, LANES), f32),
            pltpu.VMEM((SENT, padded + cap_rows + SUB, LANES), f32),
        ],
        compiler_params=PARAMS,
        name="pack",
    )(ends, geo, forces)


def place_ranges(spheres, got_ref, tab_v):
    sources = got_ref.shape[0]
    cap_rows = got_ref.shape[1]
    tiles = K * spheres // (SUB * LANES)
    lane = iota((SUB, LANES), 1)
    lane_f = lane.astype(f32)
    big = float(1 << 20)
    for group in range(sources // SUB):
        low = jnp.full((SUB, LANES), big, f32)
        high = jnp.full((SUB, LANES), -1.0, f32)
        for k in range(cap_rows):
            t = got_ref[group * SUB : (group + 1) * SUB, k, :]
            tile = jnp.floor(t * (1.0 / (SUB * LANES)))
            t_low = jnp.min(jnp.where(t < 0.0, big, tile), axis=1, keepdims=True)
            t_high = jnp.max(tile, axis=1, keepdims=True)
            low = jnp.where(lane == k, t_low, low)
            high = jnp.where(lane == k, t_high, high)
        starts = jnp.zeros((SUB, LANES), f32)
        counts = jnp.zeros((SUB, LANES), f32)
        for q in range(tiles):
            hit = jnp.logical_and(low <= q, high >= q)
            k_low = jnp.min(jnp.where(hit, lane_f, float(cap_rows - 1)), axis=1, keepdims=True)
            k_high = jnp.max(jnp.where(hit, lane_f, -1.0), axis=1, keepdims=True)
            starts = jnp.where(lane == q, k_low, starts)
            counts = jnp.where(lane == q, k_high - k_low + 1.0, counts)
        tab_v[group, 0] = starts.astype(i32)
        tab_v[group, 1] = jnp.broadcast_to(jnp.max(counts, axis=0, keepdims=True), (SUB, LANES)).astype(i32)
        for step in (1, 2, 4):
            low = jnp.minimum(low, pltpu.roll(low, LANES - step, 1))
            high = jnp.maximum(high, pltpu.roll(high, LANES - step, 1))
        tab_v[group, 2] = low.astype(i32)
        tab_v[group, 3] = high.astype(i32)


WINDOWS = 4


def place_invert(got_ref, tab_s, acc):
    cap_rows = got_ref.shape[1]
    chunks = cap_rows // SUB
    slot_rows = 2 * LANES
    window = slot_rows // WINDOWS
    acc[...] = jnp.zeros_like(acc)
    hi_iota = iota((window, LANES), 0).astype(f32)
    lo_iota = iota((LANES, LANES), 0).astype(f32).astype(bf16)
    lane_value = iota((window, LANES), 1).astype(f32).astype(bf16)
    one = jnp.ones((), bf16)
    zero = jnp.zeros((), bf16)

    def step(i, carry):
        s = i >> log2(chunks)
        g = i & (chunks - 1)
        group = s >> 3
        low = tab_s[group, 2, s & (SUB - 1), g * SUB]
        high = tab_s[group, 3, s & (SUB - 1), g * SUB]

        @pl.when(high >= 0)
        def _():
            t = got_ref[s, pl.ds(pl.multiple_of(g * SUB, SUB), SUB), :].astype(i32)
            hi = (t >> 7).astype(f32).astype(bf16)
            lo = (t & (LANES - 1)).astype(f32).astype(bf16)
            right = []
            for u in range(SUB):
                row = jnp.broadcast_to(lo[u : u + 1, :], (LANES, LANES))
                right.append(jnp.where(lo_iota == row, one, zero))
            right = jnp.concatenate(right, axis=1)
            for w in range(WINDOWS):
                tiles = window // SUB

                @pl.when(jnp.logical_and(low < (w + 1) * tiles, high >= w * tiles))
                def _():
                    numbers, lanes = [], []
                    iota_w = (hi_iota + float(w * window)).astype(bf16)
                    for u in range(SUB):
                        row = jnp.broadcast_to(hi[u : u + 1, :], (window, LANES))
                        match = iota_w == row
                        number = (s * cap_rows + g * SUB + (u + 1)).astype(f32)
                        number = jnp.full((window, LANES), number, f32).astype(bf16)
                        numbers.append(jnp.where(match, number, zero))
                        lanes.append(jnp.where(match, lane_value, zero))
                    left = jnp.concatenate(
                        [jnp.concatenate(numbers, axis=1), jnp.concatenate(lanes, axis=1)], axis=0
                    )
                    out = lax.dot_general(left, right, (((1,), (1,)), ((), ())), preferred_element_type=f32)
                    acc[w * window : (w + 1) * window, :] += out[:window]
                    acc[slot_rows + w * window : slot_rows + (w + 1) * window, :] += out[window:]

        return carry

    lax.fori_loop(0, got_ref.shape[0] * chunks, step, 0)


def place_pick(spheres, got_ref, tab_s, pos_ref, terms_ref, col_ref):
    sources = got_ref.shape[0]
    cap_rows = got_ref.shape[2]
    slot_rows = 2 * LANES

    def place(q, carry):
        rows = pl.ds(pl.multiple_of(q * SUB, SUB), SUB)
        number = pos_ref[rows, :].astype(i32)
        at = pos_ref[pl.ds(pl.multiple_of(slot_rows + q * SUB, SUB), SUB), :].astype(i32)
        values = tuple(jnp.zeros((SUB, LANES), f32) for _ in range(SENT - 1))
        for group in range(sources // SUB):

            def pick(kk, values):
                values = list(values)
                for u in range(SUB):
                    s = group * SUB + u
                    k = jnp.minimum(tab_s[group, 0, u, q] + kk, cap_rows - 1)
                    match = number == s * cap_rows + k + 1
                    for c in range(SENT - 1):
                        row = jnp.broadcast_to(got_ref[s, c, pl.ds(k, 1), :], (SUB, LANES))
                        found = jnp.take_along_axis(row, at, axis=1)
                        values[c] = jnp.where(match, found, values[c])
                return tuple(values)

            values = lax.fori_loop(0, tab_s[group, 1, 0, q], pick, values)
        col_ref[rows, :] = jnp.where(number > 0, values[0], -1.0).astype(i32)
        for c in range(SENT - 2):
            terms_ref[c, rows, :] = values[c + 1]
        return carry

    lax.fori_loop(0, K * spheres // (SUB * LANES), place, 0)


def place_blocks(spheres, col_ref, span_ref):
    lane = iota((SUB, LANES), 1)
    big = float(1 << 20)
    low = jnp.full((SUB, LANES), big, f32)
    high = jnp.full((SUB, LANES), -1.0, f32)
    for q in range(K * spheres // (SUB * LANES)):
        block = (col_ref[q * SUB : (q + 1) * SUB, :] >> log2(spheres)).astype(f32)
        b_low = jnp.min(jnp.where(block < 0.0, big, block), axis=1, keepdims=True)
        b_high = jnp.max(block, axis=1, keepdims=True)
        low = jnp.where(lane == q, b_low, low)
        high = jnp.where(lane == q, b_high, high)
    span_ref[0:SUB, :] = jnp.broadcast_to(jnp.min(low, axis=0, keepdims=True), (SUB, LANES)).astype(i32)
    span_ref[SUB : 2 * SUB, :] = jnp.broadcast_to(jnp.max(high, axis=0, keepdims=True), (SUB, LANES)).astype(i32)


def invert_kernel(spheres, got_ref, pos_ref, tab_ref, tab_s, sem):
    place_ranges(spheres, got_ref, tab_ref)
    copy = pltpu.make_async_copy(tab_ref, tab_s, sem)
    copy.start()
    copy.wait()
    place_invert(got_ref, tab_s, pos_ref)


def invert(got, spheres):
    assert K * spheres == 2 * LANES * LANES
    table = (got.shape[0] // SUB, 4, SUB, LANES)
    return pl.pallas_call(
        functools.partial(invert_kernel, spheres),
        out_shape=(jax.ShapeDtypeStruct((4 * LANES, LANES), f32), jax.ShapeDtypeStruct(table, i32)),
        scratch_shapes=[pltpu.SMEM(table, i32), pltpu.SemaphoreType.DMA],
        compiler_params=PARAMS,
        cost_estimate=pl.CostEstimate(flops=4 << 30, bytes_accessed=2 << 20, transcendentals=0),
        name="invert",
    )(got)


def spread(parts, big):
    for y, part in enumerate(parts):

        def strip(x, carry):
            for c in range(FIELDS):
                for r in range(part.shape[2]):
                    big[3 * y + x, c, r] = jnp.broadcast_to(part[x, c, r : r + 1, :], (SUB, LANES))
            return carry

        lax.fori_loop(0, 3, strip, 0)


def apply_operator(own_ref, big, span_ref, col_ref, terms_ref, drag_ref, out_ref):
    chunks = big.shape[2]
    halves = chunks // SUB

    def slot(k, sums):
        base = [(k * halves + h) * SUB for h in range(halves)]
        rows = [pl.ds(pl.multiple_of(b, SUB), SUB) for b in base]
        col = [col_ref[r, :] for r in rows]
        at = [c & (LANES - 1) for c in col]
        number = [c >> 7 for c in col]
        low = span_ref[0, k * halves]
        high = span_ref[SUB, k * halves]
        for h in range(1, halves):
            low = jnp.minimum(low, span_ref[0, k * halves + h])
            high = jnp.maximum(high, span_ref[SUB, k * halves + h])

        def block(b, values):
            values = list(values)
            for r in range(chunks):
                match = [n == b * chunks + r for n in number]
                for c in range(FIELDS):
                    row = big[b, c, r]
                    for h in range(halves):
                        found = jnp.take_along_axis(row, at[h], axis=1)
                        values[h * FIELDS + c] = jnp.where(match[h], found, values[h * FIELDS + c])
            return tuple(values)

        zeros = tuple(jnp.zeros((SUB, LANES), f32) for _ in range(FIELDS * halves))
        other = lax.fori_loop(low, high + 1, block, zeros)
        sums = list(sums)
        for h in range(halves):
            diff = [own_ref[c, h * SUB : (h + 1) * SUB, :] - other[h * FIELDS + c] for c in range(FIELDS)]
            e = [terms_ref[c, rows[h], :] for c in range(3)]
            c1 = terms_ref[3, rows[h], :]
            size = e[0] * e[0] + e[1] * e[1] + e[2] * e[2]
            c2 = c1 * (1.0 - size)
            p = e[0] * diff[0] + e[1] * diff[1] + e[2] * diff[2]
            t = e[0] * diff[3] + e[1] * diff[4] + e[2] * diff[5]
            mix = 0.8 * c1
            along_top = 6.0 * c2 * p + mix * t
            along_bottom = mix * p - 2.0 * c1 * t
            cross = mix * (size * (1.0 / 3.0))
            strong = 2.5 * c1
            for c in range(3):
                top = e[c] * along_top + c1 * diff[c] - cross * diff[3 + c]
                bottom = e[c] * along_bottom - cross * diff[c] + strong * diff[3 + c]
                sums[h * FIELDS + c] = sums[h * FIELDS + c] + top
                sums[h * FIELDS + 3 + c] = sums[h * FIELDS + 3 + c] + bottom
        return tuple(sums)

    start = []
    for h in range(halves):
        for c in range(FIELDS):
            own = own_ref[c, h * SUB : (h + 1) * SUB, :]
            start.append(drag_ref[c * chunks + h * SUB : c * chunks + (h + 1) * SUB, :] * own)
    sums = lax.fori_loop(0, K, slot, tuple(start))
    for h in range(halves):
        for c in range(FIELDS):
            out_ref[c, h * SUB : (h + 1) * SUB, :] = sums[h * FIELDS + c]


def two_sum(a, b):
    s = a + b
    t = s - a
    return s, (a - (s - t)) + (b - t)


def quick(a, b):
    s = a + b
    return s, b - (s - a)


def halve(a):
    t = a * 4097.0
    high = t - (t - a)
    return high, a - high


def two_prod(a, b, a_parts=None, b_parts=None):
    ah, al = a_parts or halve(a)
    bh, bl = b_parts or halve(b)
    p = a * b
    return p, ((ah * bh - p) + ah * bl + al * bh) + al * bl


class Pair:
    def __init__(self, high, low):
        self.high, self.low = high, low

    def __add__(self, other):
        s, e = two_sum(self.high, other.high)
        return Pair(*quick(s, e + (self.low + other.low)))

    def __neg__(self):
        return Pair(-self.high, -self.low)

    def __mul__(self, other):
        p, e = two_prod(self.high, other.high)
        return Pair(*quick(p, e + (self.high * other.low + self.low * other.high)))

    def __truediv__(self, other):
        q = self.high / other.high
        p, e = two_prod(q, other.high)
        rest = ((self.high - p) - e) + (self.low - q * other.low)
        return Pair(*quick(q, rest / other.high))


GRAM = [(a, b) for a in range(ITERS + 1) for b in range(a, ITERS + 1)]


def gram_row(vectors):
    zero = jnp.zeros((SUB, LANES), f32)
    sums = [(zero, zero) for _ in GRAM]
    fields, chunks, _ = vectors[0].shape
    for c in range(fields):
        for h in range(chunks // SUB):
            x = [v[c, h * SUB : (h + 1) * SUB, :] for v in vectors]
            parts = [halve(a) for a in x]
            for n, (a, b) in enumerate(GRAM):
                p, e = two_prod(x[a], x[b], parts[a], parts[b])
                s, rest = two_sum(sums[n][0], p)
                sums[n] = (s, sums[n][1] + (e + rest))
    lane = iota((SUB, LANES), 1)
    sub = iota((SUB, LANES), 0)
    row = zero
    for base in range(0, len(GRAM), SUB):
        packed = (zero, zero)
        for n in range(base, min(base + SUB, len(GRAM))):
            s, e = sums[n]
            for step in (4, 2, 1):
                s, rest = two_sum(s, pltpu.roll(s, step, 0))
                e = e + pltpu.roll(e, step, 0) + rest
            packed = tuple(jnp.where(sub == n - base, new, old) for new, old in zip((s, e), packed))
        s, e = packed
        for step in (64, 32, 16, 8, 4, 2, 1):
            s, rest = two_sum(s, pltpu.roll(s, step, 1))
            e = e + pltpu.roll(e, step, 1) + rest
        row = row + jnp.where(lane == sub + base, s, 0.0) + jnp.where(lane == sub + (base + 64), e, 0.0)
    return jnp.sum(row, axis=0, keepdims=True)


def gram_total(rows_ref):
    total = Pair(jnp.zeros((SUB, LANES), f32), jnp.zeros((SUB, LANES), f32))
    for n in range(rows_ref.shape[0] // SUB):
        x = rows_ref[n * SUB : (n + 1) * SUB, :]
        total = total + Pair(x, pltpu.roll(x, 64, 1))
    for step in (4, 2, 1):
        total = total + Pair(pltpu.roll(total.high, step, 0), pltpu.roll(total.low, step, 0))
    grid = {}
    for n, (a, b) in enumerate(GRAM):
        at = jnp.full((SUB, LANES), n, i32)
        grid[a, b] = grid[b, a] = Pair(*quick(*(jnp.take_along_axis(x, at, axis=1) for x in (total.high, total.low))))
    return grid


def weigh(grid, x, y, shift):
    out = None
    for i, a in enumerate(x):
        for j, b in enumerate(y):
            term = grid[i, j + shift] if a is None and b is None else None
            if term is None:
                term = grid[i, j + shift] * (a if b is None else b if a is None else a * b)
            out = term if out is None else out + term
    return out


def conjugate(grid):
    zero = jnp.zeros((SUB, LANES), f32)
    one = Pair(zero + 1.0, zero)
    c = [one]
    d = [one]
    x = []
    norm = grid[0, 0]
    least = None
    for iteration in range(ITERS):
        step = norm / weigh(grid, d, d, 1)
        x = [a + step * b if a is not None else step * b for a, b in zip(x + [None], d)]
        c = [
            (c[n] if n < len(c) else None, -(step * d[n - 1]) if n else None) for n in range(len(d) + 1)
        ]
        c = [a if b is None else b if a is None else a + b for a, b in c]
        new = weigh(grid, c, c, 0)
        least = new.high if least is None else jnp.minimum(least, new.high)
        ratio = new / norm
        d = [a + ratio * b if b is not None else a for a, b in zip(c, d + [None])]
        norm = new
    size = zero
    for n in range(ITERS + 1):
        size = size + jnp.abs(c[n].high) * jnp.sqrt(grid[n, n].high)
    return [a.high for a in x], [a.high for a in c], jnp.where(least > 1e-6 * (size * size), 1.0, 0.0)


def first_kernel(
    spheres, tab, pos, got, drag, below, mid, above, terms, col, span, drag_out, out, big, span_s, sem
):
    chunks = spheres // LANES
    place_pick(spheres, got, tab, pos, terms, col)
    place_blocks(spheres, col, span)
    copy = pltpu.make_async_copy(span, span_s, sem)
    copy.start()
    for r in range(chunks):
        drag_out[pl.ds(r, FIELDS, stride=chunks), :] = drag[:, r * LANES : (r + 1) * LANES]
    spread([below, mid, above], big)
    copy.wait()
    apply_operator(mid.at[1], big, span_s, col, terms, drag_out, out)


def next_kernel(span, col, terms, drag, below, mid, above, out, big):
    spread([below, mid, above], big)
    apply_operator(mid.at[1], big, span, col, terms, drag, out)


def third_kernel(span, col, terms, drag, below, mid, above, k0, k1, out, row_out, big):
    next_kernel(span, col, terms, drag, below, mid, above, out, big)
    row = gram_row([k0, k1, mid.at[1], out])
    row_out[...] = jnp.broadcast_to(row, row_out.shape)


def last_kernel(rows, k0, k1, k2, k3, velocity, residual, good, v_s, r_s):
    x, c, ok = conjugate(gram_total(rows))
    chunks = k0.shape[1]
    k = [k0, k1, k2, k3]
    for n in range(k0.shape[0]):
        for h in range(chunks // SUB):
            part = [a[n, h * SUB : (h + 1) * SUB, :] for a in k]
            rows_out = slice(n * chunks + h * SUB, n * chunks + (h + 1) * SUB)
            v_s[rows_out, :] = x[0] * part[0] + x[1] * part[1] + x[2] * part[2]
            r_s[rows_out, :] = part[0] + c[1] * part[1] + c[2] * part[2] + c[3] * part[3]
    for r in range(chunks):
        velocity[:, r * LANES : (r + 1) * LANES] = v_s[pl.ds(r, FIELDS, stride=chunks), :]
        residual[:, r * LANES : (r + 1) * LANES] = r_s[pl.ds(r, FIELDS, stride=chunks), :]
    good[0, 0] = jnp.min(ok).astype(i32)


VMEM = pl.BlockSpec(memory_space=pltpu.VMEM)
SMEM = pl.BlockSpec(memory_space=pltpu.SMEM)
PARAMS = pltpu.CompilerParams(vmem_limit_bytes=24 << 20)


def shape(dims, dtype=f32):
    return jax.ShapeDtypeStruct(dims, dtype)


def ring(axis, step):
    count = lax.axis_size(axis)
    return [(i, (i + step) % count) for i in range(count)]


def beside(x):
    west = lax.ppermute(x, "gx", ring("gx", 1))
    east = lax.ppermute(x, "gx", ring("gx", -1))
    mid = jnp.stack([west, x, east])
    below = lax.ppermute(mid, "gy", ring("gy", 1))
    above = lax.ppermute(mid, "gy", ring("gy", -1))
    return below, mid, above


def plain(apply, forces):
    def both(a, b):
        return lax.psum(jnp.sum(a * b), ("gx", "gy"))

    velocity = jnp.zeros_like(forces)
    residual = direction = forces
    norm = both(residual, residual)
    for iteration in range(ITERS):
        applied = apply(direction)
        step = norm / both(direction, applied)
        velocity = velocity + step * direction
        residual = residual - step * applied
        new = both(residual, residual)
        direction = residual + new / norm * direction
        norm = new
    return velocity, residual


def on_device(pair_ends, pair_geometry, drag_coef, forces):
    spheres = drag_coef.shape[1]
    chunks = spheres // LANES
    slabs = lax.axis_size("gx")
    devices = slabs * lax.axis_size("gy")
    field = (FIELDS, chunks, LANES)
    slot_rows = K * spheres // LANES
    big = pltpu.VMEM((9, FIELDS, chunks, SUB, LANES), f32)
    labels, values, k0 = pack(pair_ends, pair_geometry, forces, slabs, lax.axis_size("gy"))
    got_labels = lax.all_to_all(labels, "gx", split_axis=0, concat_axis=0, tiled=True)
    got = lax.all_to_all(values, "gx", split_axis=0, concat_axis=0, tiled=True)
    k0 = k0.reshape(field)
    near = beside(k0)
    pos, tab = invert(got_labels, spheres)
    terms, col, span, drag, k1 = pl.pallas_call(
        functools.partial(first_kernel, spheres),
        out_shape=(
            shape((SENT - 2, slot_rows, LANES)),
            shape((slot_rows, LANES), i32),
            shape((2 * SUB, LANES), i32),
            shape((FIELDS * chunks, LANES)),
            shape(field),
        ),
        in_specs=[SMEM] + [VMEM] * 6,
        scratch_shapes=[big, pltpu.SMEM((2 * SUB, LANES), i32), pltpu.SemaphoreType.DMA],
        compiler_params=PARAMS,
        name="first",
    )(tab, pos, got, drag_coef, *near)

    def apply(x):
        return pl.pallas_call(
            next_kernel,
            out_shape=shape(field),
            in_specs=[SMEM] + [VMEM] * 6,
            scratch_shapes=[big],
            compiler_params=PARAMS,
            name="next",
        )(span, col, terms, drag, *beside(x))

    k2 = apply(k1)
    k3, rows = pl.pallas_call(
        third_kernel,
        out_shape=(shape(field), shape((devices, LANES))),
        in_specs=[SMEM] + [VMEM] * 8,
        scratch_shapes=[big],
        compiler_params=PARAMS,
        name="third",
    )(span, col, terms, drag, *beside(k2), k0, k1)
    rows = lax.all_to_all(rows, ("gx", "gy"), split_axis=0, concat_axis=0, tiled=True)
    velocity, residual, good = pl.pallas_call(
        last_kernel,
        out_shape=(shape((FIELDS, spheres)), shape((FIELDS, spheres)), shape((1, 1), i32)),
        out_specs=(VMEM, VMEM, SMEM),
        scratch_shapes=[pltpu.VMEM((FIELDS * chunks, LANES), f32)] * 2,
        compiler_params=PARAMS,
        name="last",
    )(rows, k0, k1, k2, k3)

    def again(results):
        v, r = plain(apply, k0)
        return v.reshape(FIELDS, spheres), r.reshape(FIELDS, spheres)

    return lax.cond(good[0, 0] > 0, lambda results: results, again, (velocity, residual))


def solution(mesh):
    spec = P(None, ("gx", "gy"))
    return jax.shard_map(
        on_device, mesh=mesh, in_specs=(spec,) * 4, out_specs=(spec, spec), check_vma=False
    )
```

time: 129 us -> 115 us (0.89)
  blocking collectives: 32.4 us -> 14.4 us
  waiting for transfers between devices: 23.4 us -> 39.2 us
  Pallas kernels: 48.3 us -> 36.4 us
  other arithmetic: 1.65 us -> 0.03 us
    ppermute x12, waiting for transfers between devices: 10.8 us -> 32.2 us  [the longest x3 10.6 us: beside(): west = lax.ppermute(x, 'gx', ring('gx', 1))]
    all_to_all x3 -> x1, blocking collectives: 32.4 us -> 14.4 us  [on_device(): lax.all_to_all(labels, 'gx', split_axis=0, concat_axis=0, tiled=True)]
    pallas_call x5, Pallas kernels: 45.4 us -> 34.7 us  [the longest x1 10.6 us: on_device(): pl.pallas_call(functools.partial(first_kernel, spheres), out_shape=(shape...]
    all_to_all x1 -> x2, waiting for transfers between devices: 12.7 us -> 7.08 us  [the longest x1 7.07 us: on_device(): lax.all_to_all(rows, ('gx', 'gy'), split_axis=0, concat_axis=0, tiled=True)]
    another operation x3, other arithmetic: 1.65 us -> 0.03 us  [beside(): mid = jnp.stack([west, x, east])]
    unnamed x26 -> x12, local copies, waits for them, and re-layouts: 3 us -> 4.05 us
    all_to_all x1 -> x2, starting transfers between devices: 7.38 us -> 7.14 us  [the longest x1 3.6 us: on_device(): lax.all_to_all(rows, ('gx', 'gy'), split_axis=0, concat_axis=0, tiled=True)]
  transfers between devices with their start and end apart: 13 -> 14, of which waited for: 7 -> 11; matrix products, arithmetic and copies ran while one was open for 0% -> 0% of each run, Pallas kernels for 17% -> 8%
where the time goes in v2:
time: 115 us
  waiting for transfers between devices  39.2 us (34%)
  Pallas kernels  36.4 us (32%)
  starting transfers between devices  19.4 us (17%)
  blocking collectives  14.4 us (13%)
  local copies, waits for them, and re-layouts  4.05 us (4%)
  between operations  1.44 us (1%)
    all_to_all x1, blocking collectives, on_device(): lax.all_to_all(labels, 'gx', split_axis=0, concat_axis=0, tiled=True)  14.4 us
    ppermute x3, waiting for transfers between devices, beside(): west = lax.ppermute(x, 'gx', ring('gx', 1))  10.6 us
    pallas_call x1, Pallas kernels, on_device(): pl.pallas_call(functools.partial(first_kernel, spheres), out_shape=(shape...  10.6 us
    ppermute x3, waiting for transfers between devices, beside(): east = lax.ppermute(x, 'gx', ring('gx', -1))  10.1 us
    pallas_call x1, Pallas kernels, invert(): pl.pallas_call(functools.partial(invert_kernel, spheres), out_shape=(jax....  9.4 us
    pallas_call x1, Pallas kernels, on_device(): pl.pallas_call(third_kernel, out_shape=(shape(field), shape((devices, LAN...  7.38 us
    all_to_all x1, waiting for transfers between devices, on_device(): lax.all_to_all(rows, ('gx', 'gy'), split_axis=0, concat_axis=0, tiled=True)  7.07 us
    ppermute x3, waiting for transfers between devices, beside(): above = lax.ppermute(mid, 'gy', ring('gy', -1))  6.14 us
  transfers between devices with their start and end apart: 14, of which 11 were waited for; matrix products, arithmetic and copies ran while one was open for 0% of the time, Pallas kernels for 8%

profile of v2, /device:TPU:0, one launch (start us, length us, event | category | flops | bytes accessed | tf_op | source)
XLA Modules:
  0.0 115.0 jit_solution(694192515970904660)
XLA Ops:
  0.6 1.0 copy-done
  1.7 0.9 copy-done.1
  2.6 0.8 copy-done.2
  3.4 1.8 %pack.1 = (f32[8,32,128]{2,1,0:T(8,128)S(1)}, f32[8,5,32,128]{3,2,1,0:T(8,128)}, f32[96,128]{1,0:T(8,128)S(1)}) custom-call(s32[3,14464]{1,0:T(4,128)S(1)} %copy-done.1, f32[5,14464]{1,0:T(8,128)S(1)} %copy-done, f32[6,2048]{1,0:T(8,128)S(1)} %copy-done.2), custom_call_target="tpu_custom_call" | custom-call | tf_op jit(solution)/shard_map/pack/pallas_call | solution.py:89
  5.2 14.4 %all_to_all.21.got_ref = f32[8,32,128]{2,1,0:T(8,128)S(1)} all-to-all(f32[8,32,128]{2,1,0:T(8,128)S(1)} %get-tuple-element.39), channel_id=1, replica_groups=mesh['gx'=8,'gy'=4] {'gx'}, dimensions={0} | all-to-all | bytes 262144 | tf_op jit(solution)/shard_map/all_to_all | solution.py:563
  19.6 3.5 %all-to-all-start.1 = ((f32[8,5,32,128]{3,2,1,0:T(8,128)}), f32[8,5,32,128]{3,2,1,0:T(8,128)S(1)}, u32[]{:S(2)}, u32[]{:S(2)}) async-start(f32[8,5,32,128]{3,2,1,0:T(8,128)} %get-tuple-element.42), calls=%async_computation.1 | async-start | bytes 1310720 | tf_op jit(solution)/shard_map/all_to_all | solution.py:564
  23.1 4.7 %collective-permute-start.13 = (f32[6,16,128]{2,1,0:T(8,128)S(1)}, f32[6,16,128]{2,1,0:T(8,128)S(1)}, u32[]{:S(2)}, u32[]{:S(2)}) collective-permute-start(f32[6,16,128]{2,1,0:T(8,128)S(1)} %bitcast.37), channel_id=1, source_target_pairs={{0,28},{4,0},{8,4},{12,8},{16,12},{20,16},{24,20},{28,24},{1,29},{... | collective-permute-start | bytes 147464 | tf_op jit(solution)/shard_map/ppermute | solution.py:529
  27.8 6.0 %collective-permute-done.13 = f32[6,16,128]{2,1,0:T(8,128)S(1)} collective-permute-done((f32[6,16,128]{2,1,0:T(8,128)S(1)}, f32[6,16,128]{2,1,0:T(8,128)S(1)}, u32[]{:S(2)}, u32[]{:S(2)}) %collective-permute-start.13) | collective-permute-done | bytes 49184 | tf_op jit(solution)/shard_map/ppermute | solution.py:529
  33.8 4.8 %collective-permute-done.12 = f32[6,16,128]{2,1,0:T(8,128)S(1)} collective-permute-done((f32[6,16,128]{2,1,0:T(8,128)S(1)}, f32[6,16,128]{2,1,0:T(8,128)S(1)}, u32[]{:S(2)}, u32[]{:S(2)}) %collective-permute-start.12) | collective-permute-done | bytes 49184 | tf_op jit(solution)/shard_map/ppermute | solution.py:528
  38.7 0.5 collective-permute-start.14
  39.2 9.4 %invert.1 = (f32[512,128]{1,0:T(8,128)S(1)}, s32[1,4,8,128]{3,2,1,0:T(8,128)S(1)}) custom-call(f32[8,32,128]{2,1,0:T(8,128)S(1)} %all_to_all.21.got_ref), custom_call_target="tpu_custom_call" | custom-call | flops 4294967296 | bytes 2097152 | tf_op jit(solution)/shard_map/invert/pallas_call | solution.py:257
  48.6 10.6 %first.1 = (f32[4,256,128]{2,1,0:T(8,128)S(1)}, s32[256,128]{1,0:T(8,128)S(1)}, s32[16,128]{1,0:T(8,128)S(1)}, f32[96,128]{1,0:T(8,128)S(1)}, f32[6,16,128]{2,1,0:T(8,128)S(1)}) custom-call(s32[1,4,8,128]{3,2,1,0:T(8,128)S(1)} %get-tuple-element.40.tab, f32[512,128]{1,0:T(8,128)S(1)} %get-tuple-element.41.pos, f32[8,5,32,128]{3,2,1,0:T(8,128)S(1)} %all-to-all-done.1.got, ...), custom_call_target="tpu_custom_call" | custom-call | tf_op jit(solution)/shard_map/first/pallas_call | solution.py:568
  59.2 0.4 collective-permute-start.17
  59.6 1.6 %collective-permute-start.16 = (f32[6,16,128]{2,1,0:T(8,128)S(1)}, f32[6,16,128]{2,1,0:T(8,128)S(1)}, u32[]{:S(2)}, u32[]{:S(2)}) collective-permute-start(f32[6,16,128]{2,1,0:T(8,128)S(1)} %get-tuple-element.48.k1), channel_id=1, source_target_pairs={{0,4},{4,8},{8,12},{12,16},{16,20},{20,24},{24,28},{28,0},{1,5},{5... | collective-permute-start | bytes 147464 | tf_op jit(solution)/shard_map/ppermute | solution.py:528
  61.3 2.1 %collective-permute-done.17 = f32[6,16,128]{2,1,0:T(8,128)S(1)} collective-permute-done((f32[6,16,128]{2,1,0:T(8,128)S(1)}, f32[6,16,128]{2,1,0:T(8,128)S(1)}, u32[]{:S(2)}, u32[]{:S(2)}) %collective-permute-start.17) | collective-permute-done | bytes 49184 | tf_op jit(solution)/shard_map/ppermute | solution.py:529
  63.4 3.1 %collective-permute-done.16 = f32[6,16,128]{2,1,0:T(8,128)S(1)} collective-permute-done((f32[6,16,128]{2,1,0:T(8,128)S(1)}, f32[6,16,128]{2,1,0:T(8,128)S(1)}, u32[]{:S(2)}, u32[]{:S(2)}) %collective-permute-start.16) | collective-permute-done | bytes 49184 | tf_op jit(solution)/shard_map/ppermute | solution.py:528
  66.4 2.3 %collective-permute-start.19 = (f32[3,6,16,128]{3,2,1,0:T(8,128)S(1)}, f32[3,6,16,128]{3,2,1,0:T(8,128)S(1)}, u32[]{:S(2)}, u32[]{:S(2)}) collective-permute-start(f32[3,6,16,128]{3,2,1,0:T(8,128)S(1)} %pad_maximum_fusion.4.mid), channel_id=1, source_target_pairs={{0,3},{1,0},{2,1},{3,2},{4,7},{5,4},{6,5},{7,6},{8,11},{9,8},{10,9... | collective-permute-start | bytes 442376 | tf_op jit(solution)/shard_map/ppermute | solution.py:532
  68.8 2.7 %collective-permute-done.19.above = f32[3,6,16,128]{3,2,1,0:T(8,128)S(1)} collective-permute-done((f32[3,6,16,128]{3,2,1,0:T(8,128)S(1)}, f32[3,6,16,128]{3,2,1,0:T(8,128)S(1)}, u32[]{:S(2)}, u32[]{:S(2)}) %collective-permute-start.19) | collective-permute-done | bytes 147488 | tf_op jit(solution)/shard_map/ppermute | solution.py:532
  71.4 3.8 %collective-permute-done.18.below = f32[3,6,16,128]{3,2,1,0:T(8,128)S(1)} collective-permute-done((f32[3,6,16,128]{3,2,1,0:T(8,128)S(1)}, f32[3,6,16,128]{3,2,1,0:T(8,128)S(1)}, u32[]{:S(2)}, u32[]{:S(2)}) %collective-permute-start.18) | collective-permute-done | bytes 147488 | tf_op jit(solution)/shard_map/ppermute | solution.py:531
  75.2 5.9 %next.7.k2 = f32[6,16,128]{2,1,0:T(8,128)S(1)} custom-call(s32[16,128]{1,0:T(8,128)S(1)} %get-tuple-element.44.span, s32[256,128]{1,0:T(8,128)S(1)} %get-tuple-element.45.col, f32[4,256,128]{2,1,0:T(8,128)S(1)} %get-tuple-element.46.terms, f32[96,128]{1,0:T(8,128)S(1)} %get-tuple-element.47.drag, f32[3,6,16,128]{3,2,1,0:T(8,128)S(1)} %collective-permute-done.18.below, ...), custom_call_target="tpu_custom_call" | custom-call | tf_op jit(solution)/shard_map/next/pallas_call | solution.py:584
  81.2 2.0 %collective-permute-start.20 = (f32[6,16,128]{2,1,0:T(8,128)S(1)}, f32[6,16,128]{2,1,0:T(8,128)S(1)}, u32[]{:S(2)}, u32[]{:S(2)}) collective-permute-start(f32[6,16,128]{2,1,0:T(8,128)S(1)} %next.7.k2), channel_id=1, source_target_pairs={{0,4},{4,8},{8,12},{12,16},{16,20},{20,24},{24,28},{28,0},{1,5},{5... | collective-permute-start | bytes 147464 | tf_op jit(solution)/shard_map/ppermute | solution.py:528
  83.2 2.1 %collective-permute-done.21 = f32[6,16,128]{2,1,0:T(8,128)S(1)} collective-permute-done((f32[6,16,128]{2,1,0:T(8,128)S(1)}, f32[6,16,128]{2,1,0:T(8,128)S(1)}, u32[]{:S(2)}, u32[]{:S(2)}) %collective-permute-start.21) | collective-permute-done | bytes 49184 | tf_op jit(solution)/shard_map/ppermute | solution.py:529
  85.2 2.8 %collective-permute-done.20 = f32[6,16,128]{2,1,0:T(8,128)S(1)} collective-permute-done((f32[6,16,128]{2,1,0:T(8,128)S(1)}, f32[6,16,128]{2,1,0:T(8,128)S(1)}, u32[]{:S(2)}, u32[]{:S(2)}) %collective-permute-start.20) | collective-permute-done | bytes 49184 | tf_op jit(solution)/shard_map/ppermute | solution.py:528
  88.1 0.5 collective-permute-start.22
  88.6 3.5 %collective-permute-done.23.above = f32[3,6,16,128]{3,2,1,0:T(8,128)S(1)} collective-permute-done((f32[3,6,16,128]{3,2,1,0:T(8,128)S(1)}, f32[3,6,16,128]{3,2,1,0:T(8,128)S(1)}, u32[]{:S(2)}, u32[]{:S(2)}) %collective-permute-start.23) | collective-permute-done | bytes 147488 | tf_op jit(solution)/shard_map/ppermute | solution.py:532
  92.0 1.5 %collective-permute-done.22.below = f32[3,6,16,128]{3,2,1,0:T(8,128)S(1)} collective-permute-done((f32[3,6,16,128]{3,2,1,0:T(8,128)S(1)}, f32[3,6,16,128]{3,2,1,0:T(8,128)S(1)}, u32[]{:S(2)}, u32[]{:S(2)}) %collective-permute-start.22) | collective-permute-done | bytes 147488 | tf_op jit(solution)/shard_map/ppermute | solution.py:531
  93.6 7.4 %third.1 = (f32[6,16,128]{2,1,0:T(8,128)S(1)}, f32[32,128]{1,0:T(8,128)}) custom-call(s32[16,128]{1,0:T(8,128)S(1)} %get-tuple-element.44.span, s32[256,128]{1,0:T(8,128)S(1)} %get-tuple-element.45.col, f32[4,256,128]{2,1,0:T(8,128)S(1)} %get-tuple-element.46.terms, f32[96,128]{1,0:T(8,128)S(1)} %get-tuple-element.47.drag, ...), custom_call_target="tpu_custom_call" | custom-call | tf_op jit(solution)/shard_map/third/pallas_call | solution.py:594
  100.9 3.6 %all-to-all-start.2 = ((f32[32,1,128]{2,1,0:T(1,128)}), f32[32,1,128]{2,1,0:T(1,128)S(1)}, u32[]{:S(2)}, u32[]{:S(2)}) async-start(f32[32,1,128]{2,1,0:T(1,128)} %bitcast.20), calls=%async_computation.2 | async-start | bytes 32768 | tf_op jit(solution)/shard_map/all_to_all | solution.py:602
  104.6 7.1 %all-to-all-done.2 = f32[32,1,128]{2,1,0:T(1,128)S(1)} async-done(((f32[32,1,128]{2,1,0:T(1,128)}), f32[32,1,128]{2,1,0:T(1,128)S(1)}, u32[]{:S(2)}, u32[]{:S(2)}) %all-to-all-start.2) | async-done | bytes 16416 | tf_op jit(solution)/shard_map/all_to_all | solution.py:602
  111.6 1.4 %last.1 = (f32[6,2048]{1,0:T(8,128)S(1)}, f32[6,2048]{1,0:T(8,128)S(1)}, s32[1,1]{1,0:T(1,128)}) custom-call(f32[32,128]{1,0:T(8,128)S(1)} %bitcast.36, f32[6,16,128]{2,1,0:T(8,128)S(1)} %bitcast.41, f32[6,16,128]{2,1,0:T(8,128)S(1)} %get-tuple-element.48.k1, f32[6,16,128]{2,1,0:T(8,128)S(1)} %next.7.k2, f32[6,16,128]{2,1,0:T(8,128)S(1)} %get-tuple-element.50.k3), custom_call_target="tpu_custom_call" | custom-call | tf_op jit(solution)/shard_map/last/pallas_call | solution.py:603
  113.7 0.6 copy-done.4
  114.3 0.6 copy-done.5
  (19 shorter events, 0.2 us)
Async XLA Ops:
  0.6 1.0 copy-start
  1.7 0.9 copy-start.1
  2.6 0.8 copy-start.2
  19.6 29.0 %all-to-all-start.1 = ((f32[8,5,32,128]{3,2,1,0:T(8,128)}), f32[8,5,32,128]{3,2,1,0:T(8,128)S(1)}, u32[]{:S(2)}, u32[]{:S(2)}) async-start(f32[8,5,32,128]{3,2,1,0:T(8,128)} %get-tuple-element.42), calls=%async_computation.1 | async-start | bytes 1310720 | tf_op jit(solution)/shard_map/all_to_all | solution.py:564
  23.1 10.6 %collective-permute-start.13 = (f32[6,16,128]{2,1,0:T(8,128)S(1)}, f32[6,16,128]{2,1,0:T(8,128)S(1)}, u32[]{:S(2)}, u32[]{:S(2)}) collective-permute-start(f32[6,16,128]{2,1,0:T(8,128)S(1)} %bitcast.37), channel_id=1, source_target_pairs={{0,28},{4,0},{8,4},{12,8},{16,12},{20,16},{24,20},{28,24},{1,29},{... | collective-permute-start | bytes 147464 | tf_op jit(solution)/shard_map/ppermute | solution.py:529
  27.8 10.8 %collective-permute-start.12 = (f32[6,16,128]{2,1,0:T(8,128)S(1)}, f32[6,16,128]{2,1,0:T(8,128)S(1)}, u32[]{:S(2)}, u32[]{:S(2)}) collective-permute-start(f32[6,16,128]{2,1,0:T(8,128)S(1)} %bitcast.38), channel_id=1, source_target_pairs={{0,4},{4,8},{8,12},{12,16},{16,20},{20,24},{24,28},{28,0},{1,5},{5... | collective-permute-start | bytes 147464 | tf_op jit(solution)/shard_map/ppermute | solution.py:528
  38.6 10.0 %copy-start.3 = (f32[6,2048]{1,0:T(8,128)S(1)}, f32[6,2048]{1,0:T(8,128)}, u32[]{:S(2)}) copy-start(f32[6,2048]{1,0:T(8,128)} %drag.1) | copy-start | bytes 147460
  38.6 10.0 %collective-permute-start.15 = (f32[3,6,16,128]{3,2,1,0:T(8,128)S(1)}, f32[3,6,16,128]{3,2,1,0:T(8,128)S(1)}, u32[]{:S(2)}, u32[]{:S(2)}) collective-permute-start(f32[3,6,16,128]{3,2,1,0:T(8,128)S(1)} %pad_maximum_fusion.3.mid), channel_id=1, source_target_pairs={{0,3},{1,0},{2,1},{3,2},{4,7},{5,4},{6,5},{7,6},{8,11},{9,8},{10,9... | collective-permute-start | bytes 442376 | tf_op jit(solution)/shard_map/ppermute | solution.py:532
  38.7 9.9 %collective-permute-start.14 = (f32[3,6,16,128]{3,2,1,0:T(8,128)S(1)}, f32[3,6,16,128]{3,2,1,0:T(8,128)S(1)}, u32[]{:S(2)}, u32[]{:S(2)}) collective-permute-start(f32[3,6,16,128]{3,2,1,0:T(8,128)S(1)} %pad_maximum_fusion.3.mid), channel_id=1, source_target_pairs={{0,1},{1,2},{2,3},{3,0},{4,5},{5,6},{6,7},{7,4},{8,9},{9,10},{10,1... | collective-permute-start | bytes 442376 | tf_op jit(solution)/shard_map/ppermute | solution.py:531
  59.2 4.1 %collective-permute-start.17 = (f32[6,16,128]{2,1,0:T(8,128)S(1)}, f32[6,16,128]{2,1,0:T(8,128)S(1)}, u32[]{:S(2)}, u32[]{:S(2)}) collective-permute-start(f32[6,16,128]{2,1,0:T(8,128)S(1)} %get-tuple-element.48.k1), channel_id=1, source_target_pairs={{0,28},{4,0},{8,4},{12,8},{16,12},{20,16},{24,20},{28,24},{1,29},{... | collective-permute-start | bytes 147464 | tf_op jit(solution)/shard_map/ppermute | solution.py:529
  59.6 6.8 %collective-permute-start.16 = (f32[6,16,128]{2,1,0:T(8,128)S(1)}, f32[6,16,128]{2,1,0:T(8,128)S(1)}, u32[]{:S(2)}, u32[]{:S(2)}) collective-permute-start(f32[6,16,128]{2,1,0:T(8,128)S(1)} %get-tuple-element.48.k1), channel_id=1, source_target_pairs={{0,4},{4,8},{8,12},{12,16},{16,20},{20,24},{24,28},{28,0},{1,5},{5... | collective-permute-start | bytes 147464 | tf_op jit(solution)/shard_map/ppermute | solution.py:528
  66.4 5.0 %collective-permute-start.19 = (f32[3,6,16,128]{3,2,1,0:T(8,128)S(1)}, f32[3,6,16,128]{3,2,1,0:T(8,128)S(1)}, u32[]{:S(2)}, u32[]{:S(2)}) collective-permute-start(f32[3,6,16,128]{3,2,1,0:T(8,128)S(1)} %pad_maximum_fusion.4.mid), channel_id=1, source_target_pairs={{0,3},{1,0},{2,1},{3,2},{4,7},{5,4},{6,5},{7,6},{8,11},{9,8},{10,9... | collective-permute-start | bytes 442376 | tf_op jit(solution)/shard_map/ppermute | solution.py:532
  68.8 6.4 %collective-permute-start.18 = (f32[3,6,16,128]{3,2,1,0:T(8,128)S(1)}, f32[3,6,16,128]{3,2,1,0:T(8,128)S(1)}, u32[]{:S(2)}, u32[]{:S(2)}) collective-permute-start(f32[3,6,16,128]{3,2,1,0:T(8,128)S(1)} %pad_maximum_fusion.4.mid), channel_id=1, source_target_pairs={{0,1},{1,2},{2,3},{3,0},{4,5},{5,6},{6,7},{7,4},{8,9},{9,10},{10,1... | collective-permute-start | bytes 442376 | tf_op jit(solution)/shard_map/ppermute | solution.py:531
  81.1 4.1 %collective-permute-start.21 = (f32[6,16,128]{2,1,0:T(8,128)S(1)}, f32[6,16,128]{2,1,0:T(8,128)S(1)}, u32[]{:S(2)}, u32[]{:S(2)}) collective-permute-start(f32[6,16,128]{2,1,0:T(8,128)S(1)} %next.7.k2), channel_id=1, source_target_pairs={{0,28},{4,0},{8,4},{12,8},{16,12},{20,16},{24,20},{28,24},{1,29},{... | collective-permute-start | bytes 147464 | tf_op jit(solution)/shard_map/ppermute | solution.py:529
  81.2 6.8 %collective-permute-start.20 = (f32[6,16,128]{2,1,0:T(8,128)S(1)}, f32[6,16,128]{2,1,0:T(8,128)S(1)}, u32[]{:S(2)}, u32[]{:S(2)}) collective-permute-start(f32[6,16,128]{2,1,0:T(8,128)S(1)} %next.7.k2), channel_id=1, source_target_pairs={{0,4},{4,8},{8,12},{12,16},{16,20},{20,24},{24,28},{28,0},{1,5},{5... | collective-permute-start | bytes 147464 | tf_op jit(solution)/shard_map/ppermute | solution.py:528
  88.0 4.0 %collective-permute-start.23 = (f32[3,6,16,128]{3,2,1,0:T(8,128)S(1)}, f32[3,6,16,128]{3,2,1,0:T(8,128)S(1)}, u32[]{:S(2)}, u32[]{:S(2)}) collective-permute-start(f32[3,6,16,128]{3,2,1,0:T(8,128)S(1)} %pad_maximum_fusion.5.mid), channel_id=1, source_target_pairs={{0,3},{1,0},{2,1},{3,2},{4,7},{5,4},{6,5},{7,6},{8,11},{9,8},{10,9... | collective-permute-start | bytes 442376 | tf_op jit(solution)/shard_map/ppermute | solution.py:532
  88.1 5.5 %collective-permute-start.22 = (f32[3,6,16,128]{3,2,1,0:T(8,128)S(1)}, f32[3,6,16,128]{3,2,1,0:T(8,128)S(1)}, u32[]{:S(2)}, u32[]{:S(2)}) collective-permute-start(f32[3,6,16,128]{3,2,1,0:T(8,128)S(1)} %pad_maximum_fusion.5.mid), channel_id=1, source_target_pairs={{0,1},{1,2},{2,3},{3,0},{4,5},{5,6},{6,7},{7,4},{8,9},{9,10},{10,1... | collective-permute-start | bytes 442376 | tf_op jit(solution)/shard_map/ppermute | solution.py:531
  100.9 10.7 %all-to-all-start.2 = ((f32[32,1,128]{2,1,0:T(1,128)}), f32[32,1,128]{2,1,0:T(1,128)S(1)}, u32[]{:S(2)}, u32[]{:S(2)}) async-start(f32[32,1,128]{2,1,0:T(1,128)} %bitcast.20), calls=%async_computation.2 | async-start | bytes 32768 | tf_op jit(solution)/shard_map/all_to_all | solution.py:602
  113.7 0.6 copy-start.4
  114.3 0.6 copy-start.5

commit v3 on v2

--- a/solution.py
+++ b/solution.py
@@ -13,6 +13,7 @@
 SUB = 8
 FIELDS = 6
 SENT = 6
+TILE = SUB * LANES
 
 f32 = jnp.float32
 i32 = jnp.int32
@@ -28,10 +29,10 @@
     return lax.broadcasted_iota(i32, shape, dim)
 
 
-def pack_kernel(slabs, strips, spheres, ends_ref, geo_ref, force_ref, label_ref, send_ref, dense_ref, ends_s, geo_s, out_s):
+def pack_kernel(slabs, strips, spheres, ends_ref, geo_ref, force_ref, send_ref, dense_ref, ends_s, geo_s, out_s):
     rows = ends_ref.shape[1] // LANES
     padded = ends_s.shape[0] // 3
-    cap_rows = label_ref.shape[1]
+    cap_rows = send_ref.shape[2]
     chunks = spheres // LANES
     for r in range(rows):
         cols = slice(r * LANES, (r + 1) * LANES)
@@ -51,7 +52,9 @@
     shift_x = ((second_block >> log2(strips)) - owner + 1) & (slabs - 1)
     shift_y = ((second_block & (strips - 1)) - (first_block & (strips - 1)) + 1) & (strips - 1)
     column = (shift_y * 3 + shift_x) * spheres + (second & (spheres - 1))
-    target = slot * spheres + (first & (spheres - 1))
+    place = first & (spheres - 1)
+    tile = slot * (spheres // TILE) + (place >> log2(TILE))
+    target = ((place & (LANES - 1)) * SUB + ((place >> log2(LANES)) & (SUB - 1))) * (K * spheres // TILE) + tile
     owner = jnp.where(live, owner, slabs)
     sep = [geo_s[c * padded : (c + 1) * padded, :] for c in range(3)]
     a = geo_s[3 * padded : 4 * padded, :]
@@ -75,9 +78,8 @@
             after = pltpu.roll(out_s[c, pl.ds(row + 1, cap_rows), :], back, 1)
             value = jnp.where(lane < LANES - off, here, after)
             if c == 0:
-                label_ref[o] = jnp.where(place < end - start, value, -1.0)
-            else:
-                send_ref[o, c - 1] = value
+                value = jnp.where(place < end - start, value, -1.0)
+            send_ref[o, c] = value
         start = end
 
 
@@ -89,8 +91,7 @@
     return pl.pallas_call(
         functools.partial(pack_kernel, slabs, strips, spheres),
         out_shape=(
-            jax.ShapeDtypeStruct((slabs, cap_rows, LANES), f32),
-            jax.ShapeDtypeStruct((slabs, SENT - 1, cap_rows, LANES), f32),
+            jax.ShapeDtypeStruct((slabs, SENT, cap_rows, LANES), f32),
             jax.ShapeDtypeStruct((FIELDS * spheres // LANES, LANES), f32),
         ),
         scratch_shapes=[
@@ -98,15 +99,13 @@
             pltpu.VMEM((5 * padded, LANES), f32),
             pltpu.VMEM((SENT, padded + cap_rows + SUB, LANES), f32),
         ],
-        compiler_params=PARAMS,
         name="pack",
     )(ends, geo, forces)
 
 
-def place_ranges(spheres, got_ref, tab_v):
-    sources = got_ref.shape[0]
-    cap_rows = got_ref.shape[1]
-    tiles = K * spheres // (SUB * LANES)
+def place_ranges(got_ref, tab_v):
+    sources, _, cap_rows, _ = got_ref.shape
+    tiles = sources * cap_rows // SUB
     lane = iota((SUB, LANES), 1)
     lane_f = lane.astype(f32)
     big = float(1 << 20)
@@ -114,10 +113,10 @@
         low = jnp.full((SUB, LANES), big, f32)
         high = jnp.full((SUB, LANES), -1.0, f32)
         for k in range(cap_rows):
-            t = got_ref[group * SUB : (group + 1) * SUB, k, :]
-            tile = jnp.floor(t * (1.0 / (SUB * LANES)))
+            t = got_ref[group * SUB : (group + 1) * SUB, 0, k, :]
+            tile = t - float(tiles) * jnp.floor(t * (1.0 / tiles))
             t_low = jnp.min(jnp.where(t < 0.0, big, tile), axis=1, keepdims=True)
-            t_high = jnp.max(tile, axis=1, keepdims=True)
+            t_high = jnp.max(jnp.where(t < 0.0, -1.0, tile), axis=1, keepdims=True)
             low = jnp.where(lane == k, t_low, low)
             high = jnp.where(lane == k, t_high, high)
         starts = jnp.zeros((SUB, LANES), f32)
@@ -130,80 +129,73 @@
             counts = jnp.where(lane == q, k_high - k_low + 1.0, counts)
         tab_v[group, 0] = starts.astype(i32)
         tab_v[group, 1] = jnp.broadcast_to(jnp.max(counts, axis=0, keepdims=True), (SUB, LANES)).astype(i32)
-        for step in (1, 2, 4):
-            low = jnp.minimum(low, pltpu.roll(low, LANES - step, 1))
-            high = jnp.maximum(high, pltpu.roll(high, LANES - step, 1))
-        tab_v[group, 2] = low.astype(i32)
-        tab_v[group, 3] = high.astype(i32)
-
-
-WINDOWS = 4
-
-
-def place_invert(got_ref, tab_s, acc):
-    cap_rows = got_ref.shape[1]
-    chunks = cap_rows // SUB
-    slot_rows = 2 * LANES
-    window = slot_rows // WINDOWS
-    acc[...] = jnp.zeros_like(acc)
-    hi_iota = iota((window, LANES), 0).astype(f32)
-    lo_iota = iota((LANES, LANES), 0).astype(f32).astype(bf16)
-    lane_value = iota((window, LANES), 1).astype(f32).astype(bf16)
-    one = jnp.ones((), bf16)
-    zero = jnp.zeros((), bf16)
-
-    def step(i, carry):
-        s = i >> log2(chunks)
-        g = i & (chunks - 1)
-        group = s >> 3
-        low = tab_s[group, 2, s & (SUB - 1), g * SUB]
-        high = tab_s[group, 3, s & (SUB - 1), g * SUB]
-
-        @pl.when(high >= 0)
-        def _():
-            t = got_ref[s, pl.ds(pl.multiple_of(g * SUB, SUB), SUB), :].astype(i32)
-            hi = (t >> 7).astype(f32).astype(bf16)
-            lo = (t & (LANES - 1)).astype(f32).astype(bf16)
-            right = []
-            for u in range(SUB):
-                row = jnp.broadcast_to(lo[u : u + 1, :], (LANES, LANES))
-                right.append(jnp.where(lo_iota == row, one, zero))
-            right = jnp.concatenate(right, axis=1)
-            for w in range(WINDOWS):
-                tiles = window // SUB
-
-                @pl.when(jnp.logical_and(low < (w + 1) * tiles, high >= w * tiles))
-                def _():
-                    numbers, lanes = [], []
-                    iota_w = (hi_iota + float(w * window)).astype(bf16)
-                    for u in range(SUB):
-                        row = jnp.broadcast_to(hi[u : u + 1, :], (window, LANES))
-                        match = iota_w == row
-                        number = (s * cap_rows + g * SUB + (u + 1)).astype(f32)
-                        number = jnp.full((window, LANES), number, f32).astype(bf16)
-                        numbers.append(jnp.where(match, number, zero))
-                        lanes.append(jnp.where(match, lane_value, zero))
-                    left = jnp.concatenate(
-                        [jnp.concatenate(numbers, axis=1), jnp.concatenate(lanes, axis=1)], axis=0
-                    )
-                    out = lax.dot_general(left, right, (((1,), (1,)), ((), ())), preferred_element_type=f32)
-                    acc[w * window : (w + 1) * window, :] += out[:window]
-                    acc[slot_rows + w * window : slot_rows + (w + 1) * window, :] += out[window:]
-
-        return carry
-
-    lax.fori_loop(0, got_ref.shape[0] * chunks, step, 0)
+
+
+def place_sort(got_ref, pos_ref):
+    sources, _, cap_rows, _ = got_ref.shape
+    tiles = sources * cap_rows // SUB
+    dims = (tiles, SUB, LANES)
+    tile_bits, sub_bits = log2(tiles), log2(SUB)
+    bits = log2(tiles * TILE)
+    empty = 1 << (2 * bits)
+    t = got_ref[:, 0].reshape(dims).astype(i32)
+    home = (iota(dims, 0) * SUB + iota(dims, 1)) * LANES + iota(dims, 2)
+    x = jnp.where(t < 0, empty, t << bits) + home
+    place = (iota(dims, 2) * SUB + iota(dims, 1)) * tiles + iota(dims, 0)
+
+    def partner(x, bit):
+        axis, size, d = (1, SUB, 1 << (bit - tile_bits)) if bit < tile_bits + sub_bits else (
+            2, LANES, 1 << (bit - tile_bits - sub_bits))
+        if 2 * d == size:
+            return pltpu.roll(x, d, axis)
+        upper = (iota(dims, axis) & d) != 0
+        return jnp.where(upper, pltpu.roll(x, d, axis), pltpu.roll(x, size - d, axis))
+
+    def exchange(x, bit):
+        if bit < tile_bits:
+            pairs = x.reshape((tiles >> (bit + 1), 2, 1 << bit, SUB, LANES))
+            low = jnp.minimum(pairs[:, 0:1], pairs[:, 1:2])
+            high = jnp.maximum(pairs[:, 0:1], pairs[:, 1:2])
+            return jnp.concatenate([low, high], axis=1).reshape(dims)
+        other = partner(x, bit)
+        upper = (place & (1 << bit)) != 0
+        return jnp.where(jnp.logical_xor(x < other, upper), x, other)
+
+    for m in range(1, bits + 1):
+        flip = -(((place >> m) ^ (place >> (m - 1) if m > 1 else 0)) & 1)
+        x = x ^ flip
+        for bit in range(m - 1, -1, -1):
+            x = exchange(x, bit)
+
+    def carry(x):
+        x = pltpu.roll(x, 1, 1)
+        return jnp.where(iota(x.shape, 1) < 1, pltpu.roll(x, 1, 2), x)
+
+    for bit in range(bits - 1, -1, -1):
+        move = jnp.logical_and(x < empty, x - (place << bits) >= (1 << (bit + bits)))
+        y = jnp.where(move, x, empty)
+        x = jnp.where(move, empty, x)
+        if bit < tile_bits:
+            d = 1 << bit
+            y = jnp.concatenate([carry(y[tiles - d :]), y[: tiles - d]], axis=0)
+        elif bit < tile_bits + sub_bits:
+            d = 1 << (bit - tile_bits)
+            y = pltpu.roll(y, d, 1)
+            y = jnp.where(iota(dims, 1) < d, pltpu.roll(y, 1, 2), y)
+        else:
+            y = pltpu.roll(y, 1 << (bit - tile_bits - sub_bits), 2)
+        x = jnp.minimum(x, y)
+    pos_ref[...] = jnp.where(x < empty, x & ((1 << bits) - 1), -1)
 
 
 def place_pick(spheres, got_ref, tab_s, pos_ref, terms_ref, col_ref):
-    sources = got_ref.shape[0]
-    cap_rows = got_ref.shape[2]
-    slot_rows = 2 * LANES
+    sources, _, cap_rows, _ = got_ref.shape
 
     def place(q, carry):
         rows = pl.ds(pl.multiple_of(q * SUB, SUB), SUB)
-        number = pos_ref[rows, :].astype(i32)
-        at = pos_ref[pl.ds(pl.multiple_of(slot_rows + q * SUB, SUB), SUB), :].astype(i32)
+        pos = pos_ref[q]
+        number = pos >> log2(LANES)
+        at = pos & (LANES - 1)
         values = tuple(jnp.zeros((SUB, LANES), f32) for _ in range(SENT - 1))
         for group in range(sources // SUB):
 
@@ -212,20 +204,20 @@
                 for u in range(SUB):
                     s = group * SUB + u
                     k = jnp.minimum(tab_s[group, 0, u, q] + kk, cap_rows - 1)
-                    match = number == s * cap_rows + k + 1
-                    for c in range(SENT - 1):
+                    match = number == s * cap_rows + k
+                    for c in range(1, SENT):
                         row = jnp.broadcast_to(got_ref[s, c, pl.ds(k, 1), :], (SUB, LANES))
                         found = jnp.take_along_axis(row, at, axis=1)
-                        values[c] = jnp.where(match, found, values[c])
+                        values[c - 1] = jnp.where(match, found, values[c - 1])
                 return tuple(values)
 
             values = lax.fori_loop(0, tab_s[group, 1, 0, q], pick, values)
-        col_ref[rows, :] = jnp.where(number > 0, values[0], -1.0).astype(i32)
+        col_ref[rows, :] = jnp.where(pos >= 0, values[0], -1.0).astype(i32)
         for c in range(SENT - 2):
             terms_ref[c, rows, :] = values[c + 1]
         return carry
 
-    lax.fori_loop(0, K * spheres // (SUB * LANES), place, 0)
+    lax.fori_loop(0, K * spheres // TILE, place, 0)
 
 
 def place_blocks(spheres, col_ref, span_ref):
@@ -243,41 +235,15 @@
     span_ref[SUB : 2 * SUB, :] = jnp.broadcast_to(jnp.max(high, axis=0, keepdims=True), (SUB, LANES)).astype(i32)
 
 
-def invert_kernel(spheres, got_ref, pos_ref, tab_ref, tab_s, sem):
-    place_ranges(spheres, got_ref, tab_ref)
-    copy = pltpu.make_async_copy(tab_ref, tab_s, sem)
-    copy.start()
-    copy.wait()
-    place_invert(got_ref, tab_s, pos_ref)
-
-
-def invert(got, spheres):
-    assert K * spheres == 2 * LANES * LANES
-    table = (got.shape[0] // SUB, 4, SUB, LANES)
-    return pl.pallas_call(
-        functools.partial(invert_kernel, spheres),
-        out_shape=(jax.ShapeDtypeStruct((4 * LANES, LANES), f32), jax.ShapeDtypeStruct(table, i32)),
-        scratch_shapes=[pltpu.SMEM(table, i32), pltpu.SemaphoreType.DMA],
-        compiler_params=PARAMS,
-        cost_estimate=pl.CostEstimate(flops=4 << 30, bytes_accessed=2 << 20, transcendentals=0),
-        name="invert",
-    )(got)
-
-
-def spread(parts, big):
+def gather_blocks(parts, table):
     for y, part in enumerate(parts):
-
-        def strip(x, carry):
-            for c in range(FIELDS):
-                for r in range(part.shape[2]):
-                    big[3 * y + x, c, r] = jnp.broadcast_to(part[x, c, r : r + 1, :], (SUB, LANES))
-            return carry
-
-        lax.fori_loop(0, 3, strip, 0)
-
-
-def apply_operator(own_ref, big, span_ref, col_ref, terms_ref, drag_ref, out_ref):
-    chunks = big.shape[2]
+        for x in range(3):
+            table[3 * y + x] = part[x]
+
+
+def apply_operator(table, span_ref, col_ref, terms_ref, drag_ref, out_ref):
+    own_ref = table.at[4]
+    chunks = table.shape[2]
     halves = chunks // SUB
 
     def slot(k, sums):
@@ -297,7 +263,7 @@
             for r in range(chunks):
                 match = [n == b * chunks + r for n in number]
                 for c in range(FIELDS):
-                    row = big[b, c, r]
+                    row = jnp.broadcast_to(table[b, c, r : r + 1, :], (SUB, LANES))
                     for h in range(halves):
                         found = jnp.take_along_axis(row, at[h], axis=1)
                         values[h * FIELDS + c] = jnp.where(match[h], found, values[h * FIELDS + c])
@@ -469,49 +435,60 @@
 
 
 def first_kernel(
-    spheres, tab, pos, got, drag, below, mid, above, terms, col, span, drag_out, out, big, span_s, sem
+    spheres, got, drag, below, mid, above, terms, col, span, drag_out, out, table, pos, tab, tab_s, span_s, sem
 ):
     chunks = spheres // LANES
-    place_pick(spheres, got, tab, pos, terms, col)
+    place_ranges(got, tab)
+    copy = pltpu.make_async_copy(tab, tab_s, sem)
+    copy.start()
+    for r in range(chunks):
+        drag_out[pl.ds(r, FIELDS, stride=chunks), :] = drag[:, r * LANES : (r + 1) * LANES]
+    gather_blocks([below, mid, above], table)
+    place_sort(got, pos)
+    copy.wait()
+    place_pick(spheres, got, tab_s, pos, terms, col)
     place_blocks(spheres, col, span)
     copy = pltpu.make_async_copy(span, span_s, sem)
     copy.start()
-    for r in range(chunks):
-        drag_out[pl.ds(r, FIELDS, stride=chunks), :] = drag[:, r * LANES : (r + 1) * LANES]
-    spread([below, mid, above], big)
     copy.wait()
-    apply_operator(mid.at[1], big, span_s, col, terms, drag_out, out)
-
-
-def next_kernel(span, col, terms, drag, below, mid, above, out, big):
-    spread([below, mid, above], big)
-    apply_operator(mid.at[1], big, span, col, terms, drag, out)
-
-
-def third_kernel(span, col, terms, drag, below, mid, above, k0, k1, out, row_out, big):
-    next_kernel(span, col, terms, drag, below, mid, above, out, big)
+    apply_operator(table, span_s, col, terms, drag_out, out)
+
+
+def next_kernel(span, col, terms, drag, below, mid, above, out, table):
+    gather_blocks([below, mid, above], table)
+    apply_operator(table, span, col, terms, drag, out)
+
+
+def third_kernel(span, col, terms, drag, below, mid, above, k0, k1, out, row_out, table):
+    next_kernel(span, col, terms, drag, below, mid, above, out, table)
     row = gram_row([k0, k1, mid.at[1], out])
     row_out[...] = jnp.broadcast_to(row, row_out.shape)
 
 
-def last_kernel(rows, k0, k1, k2, k3, velocity, residual, good, v_s, r_s):
+def last_kernel(rows, k0, k1, k2, k3, velocity, residual, good, dense, flat, sem):
     x, c, ok = conjugate(gram_total(rows))
     chunks = k0.shape[1]
     k = [k0, k1, k2, k3]
     for n in range(k0.shape[0]):
         for h in range(chunks // SUB):
             part = [a[n, h * SUB : (h + 1) * SUB, :] for a in k]
-            rows_out = slice(n * chunks + h * SUB, n * chunks + (h + 1) * SUB)
-            v_s[rows_out, :] = x[0] * part[0] + x[1] * part[1] + x[2] * part[2]
-            r_s[rows_out, :] = part[0] + c[1] * part[1] + c[2] * part[2] + c[3] * part[3]
-    for r in range(chunks):
-        velocity[:, r * LANES : (r + 1) * LANES] = v_s[pl.ds(r, FIELDS, stride=chunks), :]
-        residual[:, r * LANES : (r + 1) * LANES] = r_s[pl.ds(r, FIELDS, stride=chunks), :]
+            here = slice(n * chunks + h * SUB, n * chunks + (h + 1) * SUB)
+            dense[0, here, :] = x[0] * part[0] + x[1] * part[1] + x[2] * part[2]
+            dense[1, here, :] = part[0] + c[1] * part[1] + c[2] * part[2] + c[3] * part[3]
+    copies = []
+    for out, target in enumerate((velocity, residual)):
+        for r in range(chunks):
+            flat[out, :, r * LANES : (r + 1) * LANES] = dense[out, pl.ds(r, FIELDS, stride=chunks), :]
+        copies.append(pltpu.make_async_copy(flat.at[out], target, sem.at[out]))
+        copies[-1].start()
     good[0, 0] = jnp.min(ok).astype(i32)
+    for copy in copies:
+        copy.wait()
 
 
 VMEM = pl.BlockSpec(memory_space=pltpu.VMEM)
 SMEM = pl.BlockSpec(memory_space=pltpu.SMEM)
+HBM = pl.BlockSpec(memory_space=pltpu.HBM)
 PARAMS = pltpu.CompilerParams(vmem_limit_bytes=24 << 20)
 
 
@@ -558,13 +535,12 @@
     devices = slabs * lax.axis_size("gy")
     field = (FIELDS, chunks, LANES)
     slot_rows = K * spheres // LANES
-    big = pltpu.VMEM((9, FIELDS, chunks, SUB, LANES), f32)
-    labels, values, k0 = pack(pair_ends, pair_geometry, forces, slabs, lax.axis_size("gy"))
-    got_labels = lax.all_to_all(labels, "gx", split_axis=0, concat_axis=0, tiled=True)
-    got = lax.all_to_all(values, "gx", split_axis=0, concat_axis=0, tiled=True)
+    table = pltpu.VMEM((9, FIELDS, chunks, LANES), f32)
+    ranges = (slabs // SUB, 2, SUB, LANES)
+    assert K * spheres == SUB * 4 * TILE and slabs % SUB == 0
+    send, k0 = pack(pair_ends, pair_geometry, forces, slabs, lax.axis_size("gy"))
+    got = lax.all_to_all(send, "gx", split_axis=0, concat_axis=0, tiled=True)
     k0 = k0.reshape(field)
-    near = beside(k0)
-    pos, tab = invert(got_labels, spheres)
     terms, col, span, drag, k1 = pl.pallas_call(
         functools.partial(first_kernel, spheres),
         out_shape=(
@@ -574,18 +550,25 @@
             shape((FIELDS * chunks, LANES)),
             shape(field),
         ),
-        in_specs=[SMEM] + [VMEM] * 6,
-        scratch_shapes=[big, pltpu.SMEM((2 * SUB, LANES), i32), pltpu.SemaphoreType.DMA],
+        in_specs=[VMEM] * 5,
+        scratch_shapes=[
+            table,
+            pltpu.VMEM((slot_rows // SUB, SUB, LANES), i32),
+            pltpu.VMEM(ranges, i32),
+            pltpu.SMEM(ranges, i32),
+            pltpu.SMEM((2 * SUB, LANES), i32),
+            pltpu.SemaphoreType.DMA,
+        ],
         compiler_params=PARAMS,
         name="first",
-    )(tab, pos, got, drag_coef, *near)
+    )(got, drag_coef, *beside(k0))
 
     def apply(x):
         return pl.pallas_call(
             next_kernel,
             out_shape=shape(field),
             in_specs=[SMEM] + [VMEM] * 6,
-            scratch_shapes=[big],
+            scratch_shapes=[table],
             compiler_params=PARAMS,
             name="next",
         )(span, col, terms, drag, *beside(x))
@@ -595,7 +578,7 @@
         third_kernel,
         out_shape=(shape(field), shape((devices, LANES))),
         in_specs=[SMEM] + [VMEM] * 8,
-        scratch_shapes=[big],
+        scratch_shapes=[table],
         compiler_params=PARAMS,
         name="third",
     )(span, col, terms, drag, *beside(k2), k0, k1)
@@ -603,17 +586,21 @@
     velocity, residual, good = pl.pallas_call(
         last_kernel,
         out_shape=(shape((FIELDS, spheres)), shape((FIELDS, spheres)), shape((1, 1), i32)),
-        out_specs=(VMEM, VMEM, SMEM),
-        scratch_shapes=[pltpu.VMEM((FIELDS * chunks, LANES), f32)] * 2,
+        out_specs=(HBM, HBM, SMEM),
+        scratch_shapes=[
+            pltpu.VMEM((2, FIELDS * chunks, LANES), f32),
+            pltpu.VMEM((2, FIELDS, spheres), f32),
+            pltpu.SemaphoreType.DMA((2,)),
+        ],
         compiler_params=PARAMS,
         name="last",
     )(rows, k0, k1, k2, k3)
 
-    def again(results):
+    def again(state):
         v, r = plain(apply, k0)
-        return v.reshape(FIELDS, spheres), r.reshape(FIELDS, spheres)
-
-    return lax.cond(good[0, 0] > 0, lambda results: results, again, (velocity, residual))
+        return jnp.ones_like(good), v.reshape(FIELDS, spheres), r.reshape(FIELDS, spheres)
+
+    return lax.while_loop(lambda state: state[0][0, 0] == 0, again, (good, velocity, residual))[1:]
 
 
 def solution(mesh):

time: 115 us -> 103 us (0.90)
  blocking collectives: 14.4 us -> 10.2 us
  local copies, waits for them, and re-layouts: 4.05 us -> 0.01 us
  Pallas kernels: 36.4 us -> 32.9 us
  starting transfers between devices: 19.4 us -> 17.8 us
    pallas_call x1 -> x0, Pallas kernels: 9.4 us -> none  [invert(): pl.pallas_call(functools.partial(invert_kernel, spheres), out_shape=(jax....]
    all_to_all x2 -> x1, waiting for transfers between devices: 7.08 us -> 0.01 us  [on_device(): got = lax.all_to_all(send, 'gx', split_axis=0, concat_axis=0, tiled=True)]
    pallas_call x1, Pallas kernels: 10.6 us -> 15.9 us  [on_device(): pl.pallas_call(functools.partial(first_kernel, spheres), out_shape=(shape...]
    all_to_all x1, blocking collectives: 14.4 us -> 10.2 us  [on_device(): lax.all_to_all(rows, ('gx', 'gy'), split_axis=0, concat_axis=0, tiled=True)]
    unnamed x12 -> x2, local copies, waits for them, and re-layouts: 4.05 us -> 0.01 us
    ppermute x3, waiting for transfers between devices: 6.14 us -> 9.48 us  [beside(): above = lax.ppermute(mid, 'gy', ring('gy', -1))]
    ppermute x3, waiting for transfers between devices: 10.1 us -> 13.2 us  [beside(): east = lax.ppermute(x, 'gx', ring('gx', -1))]
    ppermute x3, starting transfers between devices: 2.42 us -> 0.17 us  [beside(): above = lax.ppermute(mid, 'gy', ring('gy', -1))]
  transfers between devices with their start and end apart: 14 -> 13, of which waited for: 11 -> 12; matrix products, arithmetic and copies ran while one was open for 0% -> 0% of each run, Pallas kernels for 8% -> 0%
where the time goes in v3:
time: 103 us; the launch traced here: 102 us
  waiting for transfers between devices  39.8 us (39%)
  Pallas kernels  32.9 us (32%)
  starting transfers between devices  17.8 us (17%)
  blocking collectives  10.2 us (10%)
    pallas_call x1, Pallas kernels, on_device(): pl.pallas_call(functools.partial(first_kernel, spheres), out_shape=(shape...  15.9 us
    ppermute x3, waiting for transfers between devices, beside(): east = lax.ppermute(x, 'gx', ring('gx', -1))  13.2 us
    ppermute x3, waiting for transfers between devices, beside(): west = lax.ppermute(x, 'gx', ring('gx', 1))  10.7 us
    all_to_all x1, blocking collectives, on_device(): lax.all_to_all(rows, ('gx', 'gy'), split_axis=0, concat_axis=0, tiled=True)  10.2 us
    ppermute x3, waiting for transfers between devices, beside(): above = lax.ppermute(mid, 'gy', ring('gy', -1))  9.48 us
    all_to_all x1, starting transfers between devices, on_device(): got = lax.all_to_all(send, 'gx', split_axis=0, concat_axis=0, tiled=True)  7.25 us
    pallas_call x1, Pallas kernels, on_device(): pl.pallas_call(third_kernel, out_shape=(shape(field), shape((devices, LAN...  6.56 us
    ppermute x3, waiting for transfers between devices, beside(): below = lax.ppermute(mid, 'gy', ring('gy', 1))  6.43 us
  transfers between devices with their start and end apart: 13, of which 12 were waited for; matrix products, arithmetic and copies ran while one was open for 0% of the time, Pallas kernels for 0%

profile of v3, /device:TPU:0, one launch (start us, length us, event | category | flops | bytes accessed | tf_op | source)
XLA Modules:
  0.0 102.4 jit_solution(13524804945438829906)
XLA Ops:
  0.6 2.9 %pack.1 = (f32[8,6,32,128]{3,2,1,0:T(8,128)}, f32[96,128]{1,0:T(8,128)S(1)}) custom-call(s32[3,14464]{1,0:T(4,128)} %ends_ref.1, f32[5,14464]{1,0:T(8,128)} %geo_ref.1, f32[6,2048]{1,0:T(8,128)} %force_ref.1), custom_call_target="tpu_custom_call" | custom-call | tf_op jit(solution)/shard_map/pack/pallas_call | solution.py:91
  3.5 7.3 %all-to-all-start = ((f32[8,6,32,128]{3,2,1,0:T(8,128)}), f32[8,6,32,128]{3,2,1,0:T(8,128)S(1)}, u32[]{:S(2)}, u32[]{:S(2)}) async-start(f32[8,6,32,128]{3,2,1,0:T(8,128)} %get-tuple-element.59), calls=%async_computation | async-start | bytes 1572864 | tf_op jit(solution)/shard_map/all_to_all | solution.py:542
  10.8 4.7 %collective-permute-start.13 = (f32[6,16,128]{2,1,0:T(8,128)S(1)}, f32[6,16,128]{2,1,0:T(8,128)S(1)}, u32[]{:S(2)}, u32[]{:S(2)}) collective-permute-start(f32[6,16,128]{2,1,0:T(8,128)S(1)} %bitcast.38), channel_id=1, source_target_pairs={{0,28},{4,0},{8,4},{12,8},{16,12},{20,16},{24,20},{28,24},{1,29},{... | collective-permute-start | bytes 147464 | tf_op jit(solution)/shard_map/ppermute | solution.py:506
  15.5 9.1 %collective-permute-done.13 = f32[6,16,128]{2,1,0:T(8,128)S(1)} collective-permute-done((f32[6,16,128]{2,1,0:T(8,128)S(1)}, f32[6,16,128]{2,1,0:T(8,128)S(1)}, u32[]{:S(2)}, u32[]{:S(2)}) %collective-permute-start.13) | collective-permute-done | bytes 49184 | tf_op jit(solution)/shard_map/ppermute | solution.py:506
  24.6 4.9 %collective-permute-done.12 = f32[6,16,128]{2,1,0:T(8,128)S(1)} collective-permute-done((f32[6,16,128]{2,1,0:T(8,128)S(1)}, f32[6,16,128]{2,1,0:T(8,128)S(1)}, u32[]{:S(2)}, u32[]{:S(2)}) %collective-permute-start.12) | collective-permute-done | bytes 49184 | tf_op jit(solution)/shard_map/ppermute | solution.py:505
  29.6 0.1 collective-permute-start.15
  29.7 0.5 collective-permute-start.14
  30.2 2.7 %collective-permute-done.15.above = f32[3,6,16,128]{3,2,1,0:T(8,128)S(1)} collective-permute-done((f32[3,6,16,128]{3,2,1,0:T(8,128)S(1)}, f32[3,6,16,128]{3,2,1,0:T(8,128)S(1)}, u32[]{:S(2)}, u32[]{:S(2)}) %collective-permute-start.15) | collective-permute-done | bytes 147488 | tf_op jit(solution)/shard_map/ppermute | solution.py:509
  32.9 3.0 %collective-permute-done.14.below = f32[3,6,16,128]{3,2,1,0:T(8,128)S(1)} collective-permute-done((f32[3,6,16,128]{3,2,1,0:T(8,128)S(1)}, f32[3,6,16,128]{3,2,1,0:T(8,128)S(1)}, u32[]{:S(2)}, u32[]{:S(2)}) %collective-permute-start.14) | collective-permute-done | bytes 147488 | tf_op jit(solution)/shard_map/ppermute | solution.py:508
  35.9 0.0 all-to-all-done.got
  35.9 15.9 %first.1 = (f32[4,256,128]{2,1,0:T(8,128)S(1)}, s32[256,128]{1,0:T(8,128)S(1)}, s32[16,128]{1,0:T(8,128)S(1)}, f32[96,128]{1,0:T(8,128)S(1)}, f32[6,16,128]{2,1,0:T(8,128)S(1)}) custom-call(f32[8,6,32,128]{3,2,1,0:T(8,128)S(1)} %all-to-all-done.got, f32[6,2048]{1,0:T(8,128)S(1)} %copy-done, f32[3,6,16,128]{3,2,1,0:T(8,128)S(1)} %collective-permute-done.14.below, ...), custom_call_target="tpu_custom_call" | custom-call | tf_op jit(solution)/shard_map/first/pallas_call | solution.py:544
  51.7 0.1 collective-permute-start.17
  51.8 2.0 %collective-permute-start.16 = (f32[6,16,128]{2,1,0:T(8,128)S(1)}, f32[6,16,128]{2,1,0:T(8,128)S(1)}, u32[]{:S(2)}, u32[]{:S(2)}) collective-permute-start(f32[6,16,128]{2,1,0:T(8,128)S(1)} %get-tuple-element.65.k1), channel_id=1, source_target_pairs={{0,4},{4,8},{8,12},{12,16},{16,20},{20,24},{24,28},{28,0},{1,5},{5... | collective-permute-start | bytes 147464 | tf_op jit(solution)/shard_map/ppermute | solution.py:505
  53.8 2.1 %collective-permute-done.17 = f32[6,16,128]{2,1,0:T(8,128)S(1)} collective-permute-done((f32[6,16,128]{2,1,0:T(8,128)S(1)}, f32[6,16,128]{2,1,0:T(8,128)S(1)}, u32[]{:S(2)}, u32[]{:S(2)}) %collective-permute-start.17) | collective-permute-done | bytes 49184 | tf_op jit(solution)/shard_map/ppermute | solution.py:506
  55.9 2.8 %collective-permute-done.16 = f32[6,16,128]{2,1,0:T(8,128)S(1)} collective-permute-done((f32[6,16,128]{2,1,0:T(8,128)S(1)}, f32[6,16,128]{2,1,0:T(8,128)S(1)}, u32[]{:S(2)}, u32[]{:S(2)}) %collective-permute-start.16) | collective-permute-done | bytes 49184 | tf_op jit(solution)/shard_map/ppermute | solution.py:505
  58.7 0.1 collective-permute-start.19
  58.7 0.5 collective-permute-start.18
  59.2 3.7 %collective-permute-done.19.above = f32[3,6,16,128]{3,2,1,0:T(8,128)S(1)} collective-permute-done((f32[3,6,16,128]{3,2,1,0:T(8,128)S(1)}, f32[3,6,16,128]{3,2,1,0:T(8,128)S(1)}, u32[]{:S(2)}, u32[]{:S(2)}) %collective-permute-start.19) | collective-permute-done | bytes 147488 | tf_op jit(solution)/shard_map/ppermute | solution.py:509
  62.9 1.1 %collective-permute-done.18.below = f32[3,6,16,128]{3,2,1,0:T(8,128)S(1)} collective-permute-done((f32[3,6,16,128]{3,2,1,0:T(8,128)S(1)}, f32[3,6,16,128]{3,2,1,0:T(8,128)S(1)}, u32[]{:S(2)}, u32[]{:S(2)}) %collective-permute-start.18) | collective-permute-done | bytes 147488 | tf_op jit(solution)/shard_map/ppermute | solution.py:508
  64.0 5.7 %next.7.k2 = f32[6,16,128]{2,1,0:T(8,128)S(1)} custom-call(s32[16,128]{1,0:T(8,128)S(1)} %get-tuple-element.113.span, s32[256,128]{1,0:T(8,128)S(1)} %get-tuple-element.114.col, f32[4,256,128]{2,1,0:T(8,128)S(1)} %get-tuple-element.115.terms, f32[96,128]{1,0:T(8,128)S(1)} %get-tuple-element.116.drag, f32[3,6,16,128]{3,2,1,0:T(8,128)S(1)} %collective-permute-done.18.below, ...), custom_call_target="tpu_custom_call" | custom-call | tf_op jit(solution)/shard_map/next/pallas_call | solution.py:567
  69.7 0.3 collective-permute-start.21
  70.0 1.8 %collective-permute-start.20 = (f32[6,16,128]{2,1,0:T(8,128)S(1)}, f32[6,16,128]{2,1,0:T(8,128)S(1)}, u32[]{:S(2)}, u32[]{:S(2)}) collective-permute-start(f32[6,16,128]{2,1,0:T(8,128)S(1)} %next.7.k2), channel_id=1, source_target_pairs={{0,4},{4,8},{8,12},{12,16},{16,20},{20,24},{24,28},{28,0},{1,5},{5... | collective-permute-start | bytes 147464 | tf_op jit(solution)/shard_map/ppermute | solution.py:505
  71.8 2.1 %collective-permute-done.21 = f32[6,16,128]{2,1,0:T(8,128)S(1)} collective-permute-done((f32[6,16,128]{2,1,0:T(8,128)S(1)}, f32[6,16,128]{2,1,0:T(8,128)S(1)}, u32[]{:S(2)}, u32[]{:S(2)}) %collective-permute-start.21) | collective-permute-done | bytes 49184 | tf_op jit(solution)/shard_map/ppermute | solution.py:506
  73.8 2.9 %collective-permute-done.20 = f32[6,16,128]{2,1,0:T(8,128)S(1)} collective-permute-done((f32[6,16,128]{2,1,0:T(8,128)S(1)}, f32[6,16,128]{2,1,0:T(8,128)S(1)}, u32[]{:S(2)}, u32[]{:S(2)}) %collective-permute-start.20) | collective-permute-done | bytes 49184 | tf_op jit(solution)/shard_map/ppermute | solution.py:505
  76.8 0.1 collective-permute-start.23
  76.9 0.5 collective-permute-start.22
  77.4 3.0 %collective-permute-done.23.above = f32[3,6,16,128]{3,2,1,0:T(8,128)S(1)} collective-permute-done((f32[3,6,16,128]{3,2,1,0:T(8,128)S(1)}, f32[3,6,16,128]{3,2,1,0:T(8,128)S(1)}, u32[]{:S(2)}, u32[]{:S(2)}) %collective-permute-start.23) | collective-permute-done | bytes 147488 | tf_op jit(solution)/shard_map/ppermute | solution.py:509
  80.4 2.4 %collective-permute-done.22.below = f32[3,6,16,128]{3,2,1,0:T(8,128)S(1)} collective-permute-done((f32[3,6,16,128]{3,2,1,0:T(8,128)S(1)}, f32[3,6,16,128]{3,2,1,0:T(8,128)S(1)}, u32[]{:S(2)}, u32[]{:S(2)}) %collective-permute-start.22) | collective-permute-done | bytes 147488 | tf_op jit(solution)/shard_map/ppermute | solution.py:508
  82.8 6.6 %third.1 = (f32[6,16,128]{2,1,0:T(8,128)S(1)}, f32[32,128]{1,0:T(8,128)S(1)}) custom-call(s32[16,128]{1,0:T(8,128)S(1)} %get-tuple-element.113.span, s32[256,128]{1,0:T(8,128)S(1)} %get-tuple-element.114.col, f32[4,256,128]{2,1,0:T(8,128)S(1)} %get-tuple-element.115.terms, f32[96,128]{1,0:T(8,128)S(1)} %get-tuple-element.116.drag, ...), custom_call_target="tpu_custom_call" | custom-call | tf_op jit(solution)/shard_map/third/pallas_call | solution.py:577
  89.4 10.2 %all_to_all.16 = f32[32,1,128]{2,1,0:T(1,128)S(1)} all-to-all(f32[32,1,128]{2,1,0:T(1,128)S(1)} %bitcast.37), channel_id=1, replica_groups=mesh['gx'=8,'gy'=4] {'gx','gy'}, dimensions={0} | all-to-all | bytes 32768 | tf_op jit(solution)/shard_map/all_to_all | solution.py:585
  99.5 1.9 %last.1 = (f32[6,2048]{1,0:T(8,128)}, f32[6,2048]{1,0:T(8,128)}, s32[1,1]{1,0:T(1,128)}) custom-call(f32[32,128]{1,0:T(8,128)S(1)} %bitcast.36, f32[6,16,128]{2,1,0:T(8,128)S(1)} %bitcast.42, f32[6,16,128]{2,1,0:T(8,128)S(1)} %get-tuple-element.65.k1, f32[6,16,128]{2,1,0:T(8,128)S(1)} %next.7.k2, f32[6,16,128]{2,1,0:T(8,128)S(1)} %get-tuple-element.67.k3), custom_call_target="tpu_custom_call" | custom-call | tf_op jit(solution)/shard_map/last/pallas_call | solution.py:586
  101.5 0.8 while.11
  (6 shorter events, 0.0 us)
Async XLA Ops:
  3.5 32.3 %all-to-all-start = ((f32[8,6,32,128]{3,2,1,0:T(8,128)}), f32[8,6,32,128]{3,2,1,0:T(8,128)S(1)}, u32[]{:S(2)}, u32[]{:S(2)}) async-start(f32[8,6,32,128]{3,2,1,0:T(8,128)} %get-tuple-element.59), calls=%async_computation | async-start | bytes 1572864 | tf_op jit(solution)/shard_map/all_to_all | solution.py:542
  10.8 13.8 %collective-permute-start.13 = (f32[6,16,128]{2,1,0:T(8,128)S(1)}, f32[6,16,128]{2,1,0:T(8,128)S(1)}, u32[]{:S(2)}, u32[]{:S(2)}) collective-permute-start(f32[6,16,128]{2,1,0:T(8,128)S(1)} %bitcast.38), channel_id=1, source_target_pairs={{0,28},{4,0},{8,4},{12,8},{16,12},{20,16},{24,20},{28,24},{1,29},{... | collective-permute-start | bytes 147464 | tf_op jit(solution)/shard_map/ppermute | solution.py:506
  15.5 14.1 %collective-permute-start.12 = (f32[6,16,128]{2,1,0:T(8,128)S(1)}, f32[6,16,128]{2,1,0:T(8,128)S(1)}, u32[]{:S(2)}, u32[]{:S(2)}) collective-permute-start(f32[6,16,128]{2,1,0:T(8,128)S(1)} %bitcast.39), channel_id=1, source_target_pairs={{0,4},{4,8},{8,12},{12,16},{16,20},{20,24},{24,28},{28,0},{1,5},{5... | collective-permute-start | bytes 147464 | tf_op jit(solution)/shard_map/ppermute | solution.py:505
  29.6 6.3 %copy-start = (f32[6,2048]{1,0:T(8,128)S(1)}, f32[6,2048]{1,0:T(8,128)}, u32[]{:S(2)}) copy-start(f32[6,2048]{1,0:T(8,128)} %drag.1) | copy-start | bytes 147460
  29.6 3.3 %collective-permute-start.15 = (f32[3,6,16,128]{3,2,1,0:T(8,128)S(1)}, f32[3,6,16,128]{3,2,1,0:T(8,128)S(1)}, u32[]{:S(2)}, u32[]{:S(2)}) collective-permute-start(f32[3,6,16,128]{3,2,1,0:T(8,128)S(1)} %pad_maximum_fusion.3.mid), channel_id=1, source_target_pairs={{0,3},{1,0},{2,1},{3,2},{4,7},{5,4},{6,5},{7,6},{8,11},{9,8},{10,9... | collective-permute-start | bytes 442376 | tf_op jit(solution)/shard_map/ppermute | solution.py:509
  29.7 6.2 %collective-permute-start.14 = (f32[3,6,16,128]{3,2,1,0:T(8,128)S(1)}, f32[3,6,16,128]{3,2,1,0:T(8,128)S(1)}, u32[]{:S(2)}, u32[]{:S(2)}) collective-permute-start(f32[3,6,16,128]{3,2,1,0:T(8,128)S(1)} %pad_maximum_fusion.3.mid), channel_id=1, source_target_pairs={{0,1},{1,2},{2,3},{3,0},{4,5},{5,6},{6,7},{7,4},{8,9},{9,10},{10,1... | collective-permute-start | bytes 442376 | tf_op jit(solution)/shard_map/ppermute | solution.py:508
  51.7 4.1 %collective-permute-start.17 = (f32[6,16,128]{2,1,0:T(8,128)S(1)}, f32[6,16,128]{2,1,0:T(8,128)S(1)}, u32[]{:S(2)}, u32[]{:S(2)}) collective-permute-start(f32[6,16,128]{2,1,0:T(8,128)S(1)} %get-tuple-element.65.k1), channel_id=1, source_target_pairs={{0,28},{4,0},{8,4},{12,8},{16,12},{20,16},{24,20},{28,24},{1,29},{... | collective-permute-start | bytes 147464 | tf_op jit(solution)/shard_map/ppermute | solution.py:506
  51.8 6.8 %collective-permute-start.16 = (f32[6,16,128]{2,1,0:T(8,128)S(1)}, f32[6,16,128]{2,1,0:T(8,128)S(1)}, u32[]{:S(2)}, u32[]{:S(2)}) collective-permute-start(f32[6,16,128]{2,1,0:T(8,128)S(1)} %get-tuple-element.65.k1), channel_id=1, source_target_pairs={{0,4},{4,8},{8,12},{12,16},{16,20},{20,24},{24,28},{28,0},{1,5},{5... | collective-permute-start | bytes 147464 | tf_op jit(solution)/shard_map/ppermute | solution.py:505
  58.7 4.3 %collective-permute-start.19 = (f32[3,6,16,128]{3,2,1,0:T(8,128)S(1)}, f32[3,6,16,128]{3,2,1,0:T(8,128)S(1)}, u32[]{:S(2)}, u32[]{:S(2)}) collective-permute-start(f32[3,6,16,128]{3,2,1,0:T(8,128)S(1)} %pad_maximum_fusion.4.mid), channel_id=1, source_target_pairs={{0,3},{1,0},{2,1},{3,2},{4,7},{5,4},{6,5},{7,6},{8,11},{9,8},{10,9... | collective-permute-start | bytes 442376 | tf_op jit(solution)/shard_map/ppermute | solution.py:509
  58.7 5.3 %collective-permute-start.18 = (f32[3,6,16,128]{3,2,1,0:T(8,128)S(1)}, f32[3,6,16,128]{3,2,1,0:T(8,128)S(1)}, u32[]{:S(2)}, u32[]{:S(2)}) collective-permute-start(f32[3,6,16,128]{3,2,1,0:T(8,128)S(1)} %pad_maximum_fusion.4.mid), channel_id=1, source_target_pairs={{0,1},{1,2},{2,3},{3,0},{4,5},{5,6},{6,7},{7,4},{8,9},{9,10},{10,1... | collective-permute-start | bytes 442376 | tf_op jit(solution)/shard_map/ppermute | solution.py:508
  69.7 4.1 %collective-permute-start.21 = (f32[6,16,128]{2,1,0:T(8,128)S(1)}, f32[6,16,128]{2,1,0:T(8,128)S(1)}, u32[]{:S(2)}, u32[]{:S(2)}) collective-permute-start(f32[6,16,128]{2,1,0:T(8,128)S(1)} %next.7.k2), channel_id=1, source_target_pairs={{0,28},{4,0},{8,4},{12,8},{16,12},{20,16},{24,20},{28,24},{1,29},{... | collective-permute-start | bytes 147464 | tf_op jit(solution)/shard_map/ppermute | solution.py:506
  70.0 6.8 %collective-permute-start.20 = (f32[6,16,128]{2,1,0:T(8,128)S(1)}, f32[6,16,128]{2,1,0:T(8,128)S(1)}, u32[]{:S(2)}, u32[]{:S(2)}) collective-permute-start(f32[6,16,128]{2,1,0:T(8,128)S(1)} %next.7.k2), channel_id=1, source_target_pairs={{0,4},{4,8},{8,12},{12,16},{16,20},{20,24},{24,28},{28,0},{1,5},{5... | collective-permute-start | bytes 147464 | tf_op jit(solution)/shard_map/ppermute | solution.py:505
  76.8 3.6 %collective-permute-start.23 = (f32[3,6,16,128]{3,2,1,0:T(8,128)S(1)}, f32[3,6,16,128]{3,2,1,0:T(8,128)S(1)}, u32[]{:S(2)}, u32[]{:S(2)}) collective-permute-start(f32[3,6,16,128]{3,2,1,0:T(8,128)S(1)} %pad_maximum_fusion.5.mid), channel_id=1, source_target_pairs={{0,3},{1,0},{2,1},{3,2},{4,7},{5,4},{6,5},{7,6},{8,11},{9,8},{10,9... | collective-permute-start | bytes 442376 | tf_op jit(solution)/shard_map/ppermute | solution.py:509
  76.9 5.9 %collective-permute-start.22 = (f32[3,6,16,128]{3,2,1,0:T(8,128)S(1)}, f32[3,6,16,128]{3,2,1,0:T(8,128)S(1)}, u32[]{:S(2)}, u32[]{:S(2)}) collective-permute-start(f32[3,6,16,128]{3,2,1,0:T(8,128)S(1)} %pad_maximum_fusion.5.mid), channel_id=1, source_target_pairs={{0,1},{1,2},{2,3},{3,0},{4,5},{5,6},{6,7},{7,4},{8,9},{9,10},{10,1... | collective-permute-start | bytes 442376 | tf_op jit(solution)/shard_map/ppermute | solution.py:508

commit v4 on v3

--- a/solution.py
+++ b/solution.py
@@ -67,9 +67,10 @@
         out_s[c, 0:padded, :] = value
     lane = iota((cap_rows, LANES), 1)
     place = iota((cap_rows, LANES), 0) * LANES + lane
+    ends = [jnp.sum(jnp.where(owner <= o, 1.0, 0.0)).astype(i32) for o in range(slabs)]
     start = jnp.int32(0)
     for o in range(slabs):
-        end = jnp.sum(jnp.where(owner <= o, 1.0, 0.0)).astype(i32)
+        end = ends[o]
         row = start >> 7
         off = start & (LANES - 1)
         back = (LANES - off) & (LANES - 1)
@@ -190,34 +191,54 @@
 
 def place_pick(spheres, got_ref, tab_s, pos_ref, terms_ref, col_ref):
     sources, _, cap_rows, _ = got_ref.shape
-
-    def place(q, carry):
-        rows = pl.ds(pl.multiple_of(q * SUB, SUB), SUB)
-        pos = pos_ref[q]
+    groups = range(sources // SUB)
+    tiles = K * spheres // TILE
+
+    def pick(q, pos, group, kk, values):
         number = pos >> log2(LANES)
         at = pos & (LANES - 1)
-        values = tuple(jnp.zeros((SUB, LANES), f32) for _ in range(SENT - 1))
-        for group in range(sources // SUB):
-
-            def pick(kk, values):
-                values = list(values)
-                for u in range(SUB):
-                    s = group * SUB + u
-                    k = jnp.minimum(tab_s[group, 0, u, q] + kk, cap_rows - 1)
-                    match = number == s * cap_rows + k
-                    for c in range(1, SENT):
-                        row = jnp.broadcast_to(got_ref[s, c, pl.ds(k, 1), :], (SUB, LANES))
-                        found = jnp.take_along_axis(row, at, axis=1)
-                        values[c - 1] = jnp.where(match, found, values[c - 1])
-                return tuple(values)
-
-            values = lax.fori_loop(0, tab_s[group, 1, 0, q], pick, values)
-        col_ref[rows, :] = jnp.where(pos >= 0, values[0], -1.0).astype(i32)
+        values = list(values)
+        for u in range(SUB):
+            s = group * SUB + u
+            k = jnp.minimum(tab_s[group, 0, u, q] + kk, cap_rows - 1)
+            match = number == s * cap_rows + k
+            for c in range(1, SENT):
+                row = jnp.broadcast_to(got_ref[s, c, pl.ds(k, 1), :], (SUB, LANES))
+                found = jnp.take_along_axis(row, at, axis=1)
+                values[c - 1] = jnp.where(match, found, values[c - 1])
+        return tuple(values)
+
+    def save(q, values):
+        rows = pl.ds(pl.multiple_of(q * SUB, SUB), SUB)
+        col_ref[rows, :] = values[0].astype(i32)
         for c in range(SENT - 2):
             terms_ref[c, rows, :] = values[c + 1]
+
+    def first_rows(q, carry):
+        pos = pos_ref[q]
+        zero = jnp.zeros((SUB, LANES), f32)
+        values = (jnp.where(pos >= 0, 0.0, -1.0),) + (zero,) * (SENT - 2)
+        for group in groups:
+            values = pick(q, pos, group, 0, values)
+        save(q, values)
         return carry
 
-    lax.fori_loop(0, K * spheres // TILE, place, 0)
+    def more_rows(q, carry):
+        for group in groups:
+            count = tab_s[group, 1, 0, q]
+
+            @pl.when(count > 1)
+            def _():
+                rows = pl.ds(pl.multiple_of(q * SUB, SUB), SUB)
+                pos = pos_ref[q]
+                values = (col_ref[rows, :].astype(f32),) + tuple(terms_ref[c, rows, :] for c in range(SENT - 2))
+                values = lax.fori_loop(1, count, lambda kk, values: pick(q, pos, group, kk, values), values)
+                save(q, values)
+
+        return carry
+
+    lax.fori_loop(0, tiles, first_rows, 0, unroll=4)
+    lax.fori_loop(0, tiles, more_rows, 0)
 
 
 def place_blocks(spheres, col_ref, span_ref):
@@ -235,72 +256,102 @@
     span_ref[SUB : 2 * SUB, :] = jnp.broadcast_to(jnp.max(high, axis=0, keepdims=True), (SUB, LANES)).astype(i32)
 
 
-def gather_blocks(parts, table):
-    for y, part in enumerate(parts):
-        for x in range(3):
-            table[3 * y + x] = part[x]
-
-
-def apply_operator(table, span_ref, col_ref, terms_ref, drag_ref, out_ref):
-    own_ref = table.at[4]
-    chunks = table.shape[2]
-    halves = chunks // SUB
-
-    def slot(k, sums):
-        base = [(k * halves + h) * SUB for h in range(halves)]
-        rows = [pl.ds(pl.multiple_of(b, SUB), SUB) for b in base]
-        col = [col_ref[r, :] for r in rows]
-        at = [c & (LANES - 1) for c in col]
-        number = [c >> 7 for c in col]
-        low = span_ref[0, k * halves]
-        high = span_ref[SUB, k * halves]
+def tile_terms(terms_ref, rows, diff):
+    e = [terms_ref[c, rows, :] for c in range(3)]
+    c1 = terms_ref[3, rows, :]
+    size = e[0] * e[0] + e[1] * e[1] + e[2] * e[2]
+    c2 = c1 * (1.0 - size)
+    p = e[0] * diff[0] + e[1] * diff[1] + e[2] * diff[2]
+    t = e[0] * diff[3] + e[1] * diff[4] + e[2] * diff[5]
+    mix = 0.8 * c1
+    along_top = 6.0 * c2 * p + mix * t
+    along_bottom = mix * p - 2.0 * c1 * t
+    cross = mix * (size * (1.0 / 3.0))
+    strong = 2.5 * c1
+    top = [e[c] * along_top + c1 * diff[c] - cross * diff[3 + c] for c in range(3)]
+    return top + [e[c] * along_bottom - cross * diff[c] + strong * diff[3 + c] for c in range(3)]
+
+
+class Slot:
+    def __init__(self, k, halves, span_ref, col_ref):
+        self.halves = halves
+        self.rows = [pl.ds(pl.multiple_of((k * halves + h) * SUB, SUB), SUB) for h in range(halves)]
+        col = [col_ref[r, :] for r in self.rows]
+        self.at = [c & (LANES - 1) for c in col]
+        self.number = [c >> log2(LANES) for c in col]
+        self.low = span_ref[0, k * halves]
+        self.high = span_ref[SUB, k * halves]
         for h in range(1, halves):
-            low = jnp.minimum(low, span_ref[0, k * halves + h])
-            high = jnp.maximum(high, span_ref[SUB, k * halves + h])
+            self.low = jnp.minimum(self.low, span_ref[0, k * halves + h])
+            self.high = jnp.maximum(self.high, span_ref[SUB, k * halves + h])
+
+    def none(self):
+        return tuple(jnp.zeros((SUB, LANES), f32) for _ in range(FIELDS * self.halves))
+
+    def gather(self, strip, part, values):
+        chunks = part.shape[2]
 
         def block(b, values):
             values = list(values)
             for r in range(chunks):
-                match = [n == b * chunks + r for n in number]
+                match = [n == b * chunks + r for n in self.number]
                 for c in range(FIELDS):
-                    row = jnp.broadcast_to(table[b, c, r : r + 1, :], (SUB, LANES))
-                    for h in range(halves):
-                        found = jnp.take_along_axis(row, at[h], axis=1)
+                    row = jnp.broadcast_to(part[b - 3 * strip, c, r : r + 1, :], (SUB, LANES))
+                    for h in range(self.halves):
+                        found = jnp.take_along_axis(row, self.at[h], axis=1)
                         values[h * FIELDS + c] = jnp.where(match[h], found, values[h * FIELDS + c])
             return tuple(values)
 
-        zeros = tuple(jnp.zeros((SUB, LANES), f32) for _ in range(FIELDS * halves))
-        other = lax.fori_loop(low, high + 1, block, zeros)
+        start = jnp.maximum(self.low, 3 * strip)
+        return lax.fori_loop(start, jnp.minimum(self.high, 3 * strip + 2) + 1, block, values)
+
+
+def apply_inner(mid, span_ref, col_ref, terms_ref, drag_ref, out_ref):
+    chunks = mid.shape[2]
+    halves = chunks // SUB
+
+    def own(h, c):
+        return mid[1, c, h * SUB : (h + 1) * SUB, :]
+
+    def slot(k, sums):
+        here = Slot(k, halves, span_ref, col_ref)
+        other = here.gather(1, mid, here.none())
         sums = list(sums)
         for h in range(halves):
-            diff = [own_ref[c, h * SUB : (h + 1) * SUB, :] - other[h * FIELDS + c] for c in range(FIELDS)]
-            e = [terms_ref[c, rows[h], :] for c in range(3)]
-            c1 = terms_ref[3, rows[h], :]
-            size = e[0] * e[0] + e[1] * e[1] + e[2] * e[2]
-            c2 = c1 * (1.0 - size)
-            p = e[0] * diff[0] + e[1] * diff[1] + e[2] * diff[2]
-            t = e[0] * diff[3] + e[1] * diff[4] + e[2] * diff[5]
-            mix = 0.8 * c1
-            along_top = 6.0 * c2 * p + mix * t
-            along_bottom = mix * p - 2.0 * c1 * t
-            cross = mix * (size * (1.0 / 3.0))
-            strong = 2.5 * c1
-            for c in range(3):
-                top = e[c] * along_top + c1 * diff[c] - cross * diff[3 + c]
-                bottom = e[c] * along_bottom - cross * diff[c] + strong * diff[3 + c]
-                sums[h * FIELDS + c] = sums[h * FIELDS + c] + top
-                sums[h * FIELDS + 3 + c] = sums[h * FIELDS + 3 + c] + bottom
+            diff = [own(h, c) - other[h * FIELDS + c] for c in range(FIELDS)]
+            for c, term in enumerate(tile_terms(terms_ref, here.rows[h], diff)):
+                sums[h * FIELDS + c] = sums[h * FIELDS + c] + term
         return tuple(sums)
 
     start = []
     for h in range(halves):
         for c in range(FIELDS):
-            own = own_ref[c, h * SUB : (h + 1) * SUB, :]
-            start.append(drag_ref[c * chunks + h * SUB : c * chunks + (h + 1) * SUB, :] * own)
+            start.append(drag_ref[c * chunks + h * SUB : c * chunks + (h + 1) * SUB, :] * own(h, c))
     sums = lax.fori_loop(0, K, slot, tuple(start))
     for h in range(halves):
         for c in range(FIELDS):
             out_ref[c, h * SUB : (h + 1) * SUB, :] = sums[h * FIELDS + c]
+
+
+def apply_outer(below, above, span_ref, col_ref, terms_ref, part_ref, out_ref):
+    halves = below.shape[2] // SUB
+    out_ref[...] = part_ref[...]
+
+    def slot(k, carry):
+        here = Slot(k, halves, span_ref, col_ref)
+
+        @pl.when(jnp.logical_or(here.low < 3, here.high > 5))
+        def _():
+            other = here.gather(2, above, here.gather(0, below, here.none()))
+            for h in range(halves):
+                terms = tile_terms(terms_ref, here.rows[h], other[h * FIELDS : (h + 1) * FIELDS])
+                for c, term in enumerate(terms):
+                    rows = slice(h * SUB, (h + 1) * SUB)
+                    out_ref[c, rows, :] = out_ref[c, rows, :] - term
+
+        return carry
+
+    lax.fori_loop(0, K, slot, 0)
 
 
 def two_sum(a, b):
@@ -350,26 +401,30 @@
 
 
 GRAM = [(a, b) for a in range(ITERS + 1) for b in range(a, ITERS + 1)]
-
-
-def gram_row(vectors):
+EARLY = [n for n, (a, b) in enumerate(GRAM) if b < ITERS]
+LATE = [n for n, (a, b) in enumerate(GRAM) if b == ITERS]
+
+
+def gram_row(vectors, wanted):
     zero = jnp.zeros((SUB, LANES), f32)
-    sums = [(zero, zero) for _ in GRAM]
+    sums = [(zero, zero) for _ in wanted]
     fields, chunks, _ = vectors[0].shape
     for c in range(fields):
         for h in range(chunks // SUB):
             x = [v[c, h * SUB : (h + 1) * SUB, :] for v in vectors]
             parts = [halve(a) for a in x]
-            for n, (a, b) in enumerate(GRAM):
+            for n, (a, b) in enumerate(GRAM[w] for w in wanted):
                 p, e = two_prod(x[a], x[b], parts[a], parts[b])
                 s, rest = two_sum(sums[n][0], p)
                 sums[n] = (s, sums[n][1] + (e + rest))
     lane = iota((SUB, LANES), 1)
     sub = iota((SUB, LANES), 0)
     row = zero
-    for base in range(0, len(GRAM), SUB):
+    for base in range(0, len(wanted), SUB):
         packed = (zero, zero)
-        for n in range(base, min(base + SUB, len(GRAM))):
+        spot = zero.astype(i32) - 1
+        for n in range(base, min(base + SUB, len(wanted))):
+            spot = jnp.where(sub == n - base, wanted[n], spot)
             s, e = sums[n]
             for step in (4, 2, 1):
                 s, rest = two_sum(s, pltpu.roll(s, step, 0))
@@ -379,7 +434,8 @@
         for step in (64, 32, 16, 8, 4, 2, 1):
             s, rest = two_sum(s, pltpu.roll(s, step, 1))
             e = e + pltpu.roll(e, step, 1) + rest
-        row = row + jnp.where(lane == sub + base, s, 0.0) + jnp.where(lane == sub + (base + 64), e, 0.0)
+        row = row + jnp.where(lane == spot, s, 0.0)
+        row = row + jnp.where(jnp.logical_and(spot >= 0, lane == spot + 64), e, 0.0)
     return jnp.sum(row, axis=0, keepdims=True)
 
 
@@ -435,7 +491,7 @@
 
 
 def first_kernel(
-    spheres, got, drag, below, mid, above, terms, col, span, drag_out, out, table, pos, tab, tab_s, span_s, sem
+    spheres, got, drag, below, mid, above, terms, col, span, drag_out, out, part, pos, tab, tab_s, span_s, sem
 ):
     chunks = spheres // LANES
     place_ranges(got, tab)
@@ -443,7 +499,6 @@
     copy.start()
     for r in range(chunks):
         drag_out[pl.ds(r, FIELDS, stride=chunks), :] = drag[:, r * LANES : (r + 1) * LANES]
-    gather_blocks([below, mid, above], table)
     place_sort(got, pos)
     copy.wait()
     place_pick(spheres, got, tab_s, pos, terms, col)
@@ -451,18 +506,27 @@
     copy = pltpu.make_async_copy(span, span_s, sem)
     copy.start()
     copy.wait()
-    apply_operator(table, span_s, col, terms, drag_out, out)
-
-
-def next_kernel(span, col, terms, drag, below, mid, above, out, table):
-    gather_blocks([below, mid, above], table)
-    apply_operator(table, span, col, terms, drag, out)
-
-
-def third_kernel(span, col, terms, drag, below, mid, above, k0, k1, out, row_out, table):
-    next_kernel(span, col, terms, drag, below, mid, above, out, table)
-    row = gram_row([k0, k1, mid.at[1], out])
-    row_out[...] = jnp.broadcast_to(row, row_out.shape)
+    apply_inner(mid, span_s, col, terms, drag_out, part)
+    apply_outer(below, above, span_s, col, terms, part, out)
+
+
+def inner_kernel(span, col, terms, drag, mid, part):
+    apply_inner(mid, span, col, terms, drag, part)
+
+
+def outer_kernel(span, col, terms, part, below, above, out):
+    apply_outer(below, above, span, col, terms, part, out)
+
+
+def inner_gram_kernel(span, col, terms, drag, mid, k0, k1, part, row):
+    apply_inner(mid, span, col, terms, drag, part)
+    row[...] = jnp.broadcast_to(gram_row([k0, k1, mid.at[1]], EARLY), row.shape)
+
+
+def outer_gram_kernel(span, col, terms, part, below, above, k0, k1, k2, row, out, rows):
+    apply_outer(below, above, span, col, terms, part, out)
+    late = row[0:1, :] + gram_row([k0, k1, k2, out], LATE)
+    rows[...] = jnp.broadcast_to(late, rows.shape)
 
 
 def last_kernel(rows, k0, k1, k2, k3, velocity, residual, good, dense, flat, sem):
@@ -535,7 +599,7 @@
     devices = slabs * lax.axis_size("gy")
     field = (FIELDS, chunks, LANES)
     slot_rows = K * spheres // LANES
-    table = pltpu.VMEM((9, FIELDS, chunks, LANES), f32)
+    dense = pltpu.VMEM(field, f32)
     ranges = (slabs // SUB, 2, SUB, LANES)
     assert K * spheres == SUB * 4 * TILE and slabs % SUB == 0
     send, k0 = pack(pair_ends, pair_geometry, forces, slabs, lax.axis_size("gy"))
@@ -552,7 +616,7 @@
         ),
         in_specs=[VMEM] * 5,
         scratch_shapes=[
-            table,
+            dense,
             pltpu.VMEM((slot_rows // SUB, SUB, LANES), i32),
             pltpu.VMEM(ranges, i32),
             pltpu.SMEM(ranges, i32),
@@ -563,25 +627,30 @@
         name="first",
     )(got, drag_coef, *beside(k0))
 
+    def local(kernel, name, outs, cost, *args):
+        return pl.pallas_call(
+            kernel,
+            out_shape=outs,
+            in_specs=[SMEM] + [VMEM] * (len(args) + 2),
+            compiler_params=PARAMS,
+            cost_estimate=pl.CostEstimate(flops=0, bytes_accessed=cost << 20, transcendentals=0),
+            name=name,
+        )(span, col, terms, *args)
+
     def apply(x):
-        return pl.pallas_call(
-            next_kernel,
-            out_shape=shape(field),
-            in_specs=[SMEM] + [VMEM] * 6,
-            scratch_shapes=[table],
-            compiler_params=PARAMS,
-            name="next",
-        )(span, col, terms, drag, *beside(x))
+        below, mid, above = beside(x)
+        part = local(inner_kernel, "inner", shape(field), 16, drag, mid)
+        return local(outer_kernel, "outer", shape(field), 16, part, below, above)
 
     k2 = apply(k1)
-    k3, rows = pl.pallas_call(
-        third_kernel,
-        out_shape=(shape(field), shape((devices, LANES))),
-        in_specs=[SMEM] + [VMEM] * 8,
-        scratch_shapes=[table],
-        compiler_params=PARAMS,
-        name="third",
-    )(span, col, terms, drag, *beside(k2), k0, k1)
+    below, mid, above = beside(k2)
+    part, row = local(
+        inner_gram_kernel, "inner_gram", (shape(field), shape((SUB, LANES))), 16, drag, mid, k0, k1
+    )
+    k3, rows = local(
+        outer_gram_kernel, "outer_gram", (shape(field), shape((devices, LANES))), 16,
+        part, below, above, k0, k1, k2, row,
+    )
     rows = lax.all_to_all(rows, ("gx", "gy"), split_axis=0, concat_axis=0, tiled=True)
     velocity, residual, good = pl.pallas_call(
         last_kernel,

time: 103 us -> 99.4 us (0.965)
  waiting for transfers between devices: 39.8 us -> 34.7 us
  Pallas kernels: 32.9 us -> 35 us
    ppermute x3, waiting for transfers between devices: 9.48 us -> 3.93 us  [beside(): above = lax.ppermute(mid, 'gy', ring('gy', -1))]
    pallas_call x2 -> x4, Pallas kernels: 12.2 us -> 15.5 us  [local(): pl.pallas_call(kernel, out_shape=outs, in_specs=[SMEM] + [VMEM] * (len(ar...]
  transfers between devices with their start and end apart: 13 -> 13, of which waited for: 12 -> 11; matrix products, arithmetic and copies ran while one was open for 0% -> 0% of each run, Pallas kernels for 0% -> 6%
where the time goes in v4:
time: 99.4 us; the launch traced here: 99.2 us
  Pallas kernels  35 us (35%)
  waiting for transfers between devices  34.7 us (35%)
  starting transfers between devices  17.8 us (18%)
  blocking collectives  10.1 us (10%)
    pallas_call x4, Pallas kernels, local(): pl.pallas_call(kernel, out_shape=outs, in_specs=[SMEM] + [VMEM] * (len(ar...  15.5 us
    pallas_call x1, Pallas kernels, on_device(): pl.pallas_call(functools.partial(first_kernel, spheres), out_shape=(shape...  14.9 us
    ppermute x3, waiting for transfers between devices, beside(): east = lax.ppermute(x, 'gx', ring('gx', -1))  13.2 us
    ppermute x3, waiting for transfers between devices, beside(): west = lax.ppermute(x, 'gx', ring('gx', 1))  11 us
    all_to_all x1, blocking collectives, on_device(): lax.all_to_all(rows, ('gx', 'gy'), split_axis=0, concat_axis=0, tiled=True)  10.1 us
    all_to_all x1, starting transfers between devices, on_device(): got = lax.all_to_all(send, 'gx', split_axis=0, concat_axis=0, tiled=True)  7.25 us
    ppermute x3, waiting for transfers between devices, beside(): below = lax.ppermute(mid, 'gy', ring('gy', 1))  6.46 us
    ppermute x3, starting transfers between devices, beside(): east = lax.ppermute(x, 'gx', ring('gx', -1))  5.51 us
  transfers between devices with their start and end apart: 13, of which 11 were waited for; matrix products, arithmetic and copies ran while one was open for 0% of the time, Pallas kernels for 6%

profile of v4, /device:TPU:0, one launch (start us, length us, event | category | flops | bytes accessed | tf_op | source)
XLA Modules:
  0.0 99.2 jit_solution(17720960640951599980)
XLA Ops:
  0.6 2.7 %pack.1 = (f32[8,6,32,128]{3,2,1,0:T(8,128)}, f32[96,128]{1,0:T(8,128)S(1)}) custom-call(s32[3,14464]{1,0:T(4,128)} %ends_ref.1, f32[5,14464]{1,0:T(8,128)} %geo_ref.1, f32[6,2048]{1,0:T(8,128)} %force_ref.1), custom_call_target="tpu_custom_call" | custom-call | tf_op jit(solution)/shard_map/pack/pallas_call | solution.py:92
  3.3 7.3 %all-to-all-start = ((f32[8,6,32,128]{3,2,1,0:T(8,128)}), f32[8,6,32,128]{3,2,1,0:T(8,128)S(1)}, u32[]{:S(2)}, u32[]{:S(2)}) async-start(f32[8,6,32,128]{3,2,1,0:T(8,128)} %get-tuple-element.61), calls=%async_computation | async-start | bytes 1572864 | tf_op jit(solution)/shard_map/all_to_all | solution.py:606
  10.6 4.7 %collective-permute-start.13 = (f32[6,16,128]{2,1,0:T(8,128)S(1)}, f32[6,16,128]{2,1,0:T(8,128)S(1)}, u32[]{:S(2)}, u32[]{:S(2)}) collective-permute-start(f32[6,16,128]{2,1,0:T(8,128)S(1)} %bitcast.38), channel_id=1, source_target_pairs={{0,28},{4,0},{8,4},{12,8},{16,12},{20,16},{24,20},{28,24},{1,29},{... | collective-permute-start | bytes 147464 | tf_op jit(solution)/shard_map/ppermute | solution.py:570
  15.3 9.1 %collective-permute-done.13 = f32[6,16,128]{2,1,0:T(8,128)S(1)} collective-permute-done((f32[6,16,128]{2,1,0:T(8,128)S(1)}, f32[6,16,128]{2,1,0:T(8,128)S(1)}, u32[]{:S(2)}, u32[]{:S(2)}) %collective-permute-start.13) | collective-permute-done | bytes 49184 | tf_op jit(solution)/shard_map/ppermute | solution.py:570
  24.4 4.9 %collective-permute-done.12 = f32[6,16,128]{2,1,0:T(8,128)S(1)} collective-permute-done((f32[6,16,128]{2,1,0:T(8,128)S(1)}, f32[6,16,128]{2,1,0:T(8,128)S(1)}, u32[]{:S(2)}, u32[]{:S(2)}) %collective-permute-start.12) | collective-permute-done | bytes 49184 | tf_op jit(solution)/shard_map/ppermute | solution.py:569
  29.4 0.1 collective-permute-start.15
  29.5 0.5 collective-permute-start.14
  30.0 2.7 %collective-permute-done.15.above = f32[3,6,16,128]{3,2,1,0:T(8,128)S(1)} collective-permute-done((f32[3,6,16,128]{3,2,1,0:T(8,128)S(1)}, f32[3,6,16,128]{3,2,1,0:T(8,128)S(1)}, u32[]{:S(2)}, u32[]{:S(2)}) %collective-permute-start.15) | collective-permute-done | bytes 147488 | tf_op jit(solution)/shard_map/ppermute | solution.py:573
  32.7 3.0 %collective-permute-done.14.below = f32[3,6,16,128]{3,2,1,0:T(8,128)S(1)} collective-permute-done((f32[3,6,16,128]{3,2,1,0:T(8,128)S(1)}, f32[3,6,16,128]{3,2,1,0:T(8,128)S(1)}, u32[]{:S(2)}, u32[]{:S(2)}) %collective-permute-start.14) | collective-permute-done | bytes 147488 | tf_op jit(solution)/shard_map/ppermute | solution.py:572
  35.7 14.9 %first.1 = (f32[4,256,128]{2,1,0:T(8,128)S(1)}, s32[256,128]{1,0:T(8,128)S(1)}, s32[16,128]{1,0:T(8,128)S(1)}, f32[96,128]{1,0:T(8,128)S(1)}, f32[6,16,128]{2,1,0:T(8,128)S(1)}) custom-call(f32[8,6,32,128]{3,2,1,0:T(8,128)S(1)} %all-to-all-done.got, f32[6,2048]{1,0:T(8,128)S(1)} %copy-done, f32[3,6,16,128]{3,2,1,0:T(8,128)S(1)} %collective-permute-done.14.below, ...), custom_call_target="tpu_custom_call" | custom-call | tf_op jit(solution)/shard_map/first/pallas_call | solution.py:608
  50.6 0.5 collective-permute-start.17
  51.1 1.6 %collective-permute-start.16 = (f32[6,16,128]{2,1,0:T(8,128)S(1)}, f32[6,16,128]{2,1,0:T(8,128)S(1)}, u32[]{:S(2)}, u32[]{:S(2)}) collective-permute-start(f32[6,16,128]{2,1,0:T(8,128)S(1)} %get-tuple-element.67.k1), channel_id=1, source_target_pairs={{0,4},{4,8},{8,12},{12,16},{16,20},{20,24},{24,28},{28,0},{1,5},{5... | collective-permute-start | bytes 147464 | tf_op jit(solution)/shard_map/ppermute | solution.py:569
  52.7 2.1 %collective-permute-done.17 = f32[6,16,128]{2,1,0:T(8,128)S(1)} collective-permute-done((f32[6,16,128]{2,1,0:T(8,128)S(1)}, f32[6,16,128]{2,1,0:T(8,128)S(1)}, u32[]{:S(2)}, u32[]{:S(2)}) %collective-permute-start.17) | collective-permute-done | bytes 49184 | tf_op jit(solution)/shard_map/ppermute | solution.py:570
  54.7 3.2 %collective-permute-done.16 = f32[6,16,128]{2,1,0:T(8,128)S(1)} collective-permute-done((f32[6,16,128]{2,1,0:T(8,128)S(1)}, f32[6,16,128]{2,1,0:T(8,128)S(1)}, u32[]{:S(2)}, u32[]{:S(2)}) %collective-permute-start.16) | collective-permute-done | bytes 49184 | tf_op jit(solution)/shard_map/ppermute | solution.py:569
  57.9 0.1 collective-permute-start.19
  58.0 0.5 collective-permute-start.18
  58.5 2.4 %inner.7.part = f32[6,16,128]{2,1,0:T(8,128)S(1)} custom-call(s32[16,128]{1,0:T(8,128)S(1)} %get-tuple-element.117.span, s32[256,128]{1,0:T(8,128)S(1)} %get-tuple-element.118.col, f32[4,256,128]{2,1,0:T(8,128)S(1)} %get-tuple-element.119.terms, f32[96,128]{1,0:T(8,128)S(1)} %get-tuple-element.120.drag, f32[3,6,16,128]{3,2,1,0:T(8,128)S(1)} %pad_maximum_fusion.4.mid), custom_call_target="tpu_custom_call" | custom-call | bytes 16777216 | tf_op jit(solution)/shard_map/inner/pallas_call | solution.py:631
  60.8 1.2 %collective-permute-done.19.above = f32[3,6,16,128]{3,2,1,0:T(8,128)S(1)} collective-permute-done((f32[3,6,16,128]{3,2,1,0:T(8,128)S(1)}, f32[3,6,16,128]{3,2,1,0:T(8,128)S(1)}, u32[]{:S(2)}, u32[]{:S(2)}) %collective-permute-start.19) | collective-permute-done | bytes 147488 | tf_op jit(solution)/shard_map/ppermute | solution.py:573
  62.1 1.0 %collective-permute-done.18.below = f32[3,6,16,128]{3,2,1,0:T(8,128)S(1)} collective-permute-done((f32[3,6,16,128]{3,2,1,0:T(8,128)S(1)}, f32[3,6,16,128]{3,2,1,0:T(8,128)S(1)}, u32[]{:S(2)}, u32[]{:S(2)}) %collective-permute-start.18) | collective-permute-done | bytes 147488 | tf_op jit(solution)/shard_map/ppermute | solution.py:572
  63.1 4.6 %outer.7.k2 = f32[6,16,128]{2,1,0:T(8,128)S(1)} custom-call(s32[16,128]{1,0:T(8,128)S(1)} %get-tuple-element.117.span, s32[256,128]{1,0:T(8,128)S(1)} %get-tuple-element.118.col, f32[4,256,128]{2,1,0:T(8,128)S(1)} %get-tuple-element.119.terms, f32[6,16,128]{2,1,0:T(8,128)S(1)} %inner.7.part, f32[3,6,16,128]{3,2,1,0:T(8,128)S(1)} %collective-permute-done.18.below, ...), custom_call_target="tpu_custom_call" | custom-call | bytes 16777216 | tf_op jit(solution)/shard_map/outer/pallas_call | solution.py:631
  67.7 0.3 collective-permute-start.21
  68.0 1.8 %collective-permute-start.20 = (f32[6,16,128]{2,1,0:T(8,128)S(1)}, f32[6,16,128]{2,1,0:T(8,128)S(1)}, u32[]{:S(2)}, u32[]{:S(2)}) collective-permute-start(f32[6,16,128]{2,1,0:T(8,128)S(1)} %outer.7.k2), channel_id=1, source_target_pairs={{0,4},{4,8},{8,12},{12,16},{16,20},{20,24},{24,28},{28,0},{1,5},{5... | collective-permute-start | bytes 147464 | tf_op jit(solution)/shard_map/ppermute | solution.py:569
  69.8 2.1 %collective-permute-done.21 = f32[6,16,128]{2,1,0:T(8,128)S(1)} collective-permute-done((f32[6,16,128]{2,1,0:T(8,128)S(1)}, f32[6,16,128]{2,1,0:T(8,128)S(1)}, u32[]{:S(2)}, u32[]{:S(2)}) %collective-permute-start.21) | collective-permute-done | bytes 49184 | tf_op jit(solution)/shard_map/ppermute | solution.py:570
  71.9 2.9 %collective-permute-done.20 = f32[6,16,128]{2,1,0:T(8,128)S(1)} collective-permute-done((f32[6,16,128]{2,1,0:T(8,128)S(1)}, f32[6,16,128]{2,1,0:T(8,128)S(1)}, u32[]{:S(2)}, u32[]{:S(2)}) %collective-permute-start.20) | collective-permute-done | bytes 49184 | tf_op jit(solution)/shard_map/ppermute | solution.py:569
  74.8 0.1 collective-permute-start.23
  74.9 0.5 collective-permute-start.22
  75.4 3.1 %inner_gram.1 = (f32[6,16,128]{2,1,0:T(8,128)S(1)}, f32[8,128]{1,0:T(8,128)S(1)}) custom-call(s32[16,128]{1,0:T(8,128)S(1)} %get-tuple-element.117.span, s32[256,128]{1,0:T(8,128)S(1)} %get-tuple-element.118.col, f32[4,256,128]{2,1,0:T(8,128)S(1)} %get-tuple-element.119.terms, f32[96,128]{1,0:T(8,128)S(1)} %get-tuple-element.120.drag, ...), custom_call_target="tpu_custom_call" | custom-call | bytes 16777216 | tf_op jit(solution)/shard_map/inner_gram/pallas_call | solution.py:631
  78.5 2.5 %collective-permute-done.22.below = f32[3,6,16,128]{3,2,1,0:T(8,128)S(1)} collective-permute-done((f32[3,6,16,128]{3,2,1,0:T(8,128)S(1)}, f32[3,6,16,128]{3,2,1,0:T(8,128)S(1)}, u32[]{:S(2)}, u32[]{:S(2)}) %collective-permute-start.22) | collective-permute-done | bytes 147488 | tf_op jit(solution)/shard_map/ppermute | solution.py:572
  81.0 5.3 %outer_gram.1 = (f32[6,16,128]{2,1,0:T(8,128)S(1)}, f32[32,128]{1,0:T(8,128)S(1)}) custom-call(s32[16,128]{1,0:T(8,128)S(1)} %get-tuple-element.117.span, s32[256,128]{1,0:T(8,128)S(1)} %get-tuple-element.118.col, f32[4,256,128]{2,1,0:T(8,128)S(1)} %get-tuple-element.119.terms, f32[6,16,128]{2,1,0:T(8,128)S(1)} %get-tuple-element.68.part, ...), custom_call_target="tpu_custom_call" | custom-call | bytes 16777216 | tf_op jit(solution)/shard_map/outer_gram/pallas_call | solution.py:631
  86.3 10.1 %all_to_all.16 = f32[32,1,128]{2,1,0:T(1,128)S(1)} all-to-all(f32[32,1,128]{2,1,0:T(1,128)S(1)} %bitcast.37), channel_id=1, replica_groups=mesh['gx'=8,'gy'=4] {'gx','gy'}, dimensions={0} | all-to-all | bytes 32768 | tf_op jit(solution)/shard_map/all_to_all | solution.py:654
  96.4 1.9 %last.1 = (f32[6,2048]{1,0:T(8,128)}, f32[6,2048]{1,0:T(8,128)}, s32[1,1]{1,0:T(1,128)}) custom-call(f32[32,128]{1,0:T(8,128)S(1)} %bitcast.36, f32[6,16,128]{2,1,0:T(8,128)S(1)} %bitcast.43, f32[6,16,128]{2,1,0:T(8,128)S(1)} %get-tuple-element.67.k1, f32[6,16,128]{2,1,0:T(8,128)S(1)} %outer.7.k2, f32[6,16,128]{2,1,0:T(8,128)S(1)} %get-tuple-element.71.k3), custom_call_target="tpu_custom_call" | custom-call | tf_op jit(solution)/shard_map/last/pallas_call | solution.py:655
  98.3 0.7 while.11
  (8 shorter events, 0.0 us)
Async XLA Ops:
  3.3 32.3 %all-to-all-start = ((f32[8,6,32,128]{3,2,1,0:T(8,128)}), f32[8,6,32,128]{3,2,1,0:T(8,128)S(1)}, u32[]{:S(2)}, u32[]{:S(2)}) async-start(f32[8,6,32,128]{3,2,1,0:T(8,128)} %get-tuple-element.61), calls=%async_computation | async-start | bytes 1572864 | tf_op jit(solution)/shard_map/all_to_all | solution.py:606
  10.6 13.8 %collective-permute-start.13 = (f32[6,16,128]{2,1,0:T(8,128)S(1)}, f32[6,16,128]{2,1,0:T(8,128)S(1)}, u32[]{:S(2)}, u32[]{:S(2)}) collective-permute-start(f32[6,16,128]{2,1,0:T(8,128)S(1)} %bitcast.38), channel_id=1, source_target_pairs={{0,28},{4,0},{8,4},{12,8},{16,12},{20,16},{24,20},{28,24},{1,29},{... | collective-permute-start | bytes 147464 | tf_op jit(solution)/shard_map/ppermute | solution.py:570
  15.3 14.1 %collective-permute-start.12 = (f32[6,16,128]{2,1,0:T(8,128)S(1)}, f32[6,16,128]{2,1,0:T(8,128)S(1)}, u32[]{:S(2)}, u32[]{:S(2)}) collective-permute-start(f32[6,16,128]{2,1,0:T(8,128)S(1)} %bitcast.39), channel_id=1, source_target_pairs={{0,4},{4,8},{8,12},{12,16},{16,20},{20,24},{24,28},{28,0},{1,5},{5... | collective-permute-start | bytes 147464 | tf_op jit(solution)/shard_map/ppermute | solution.py:569
  29.4 6.3 %copy-start = (f32[6,2048]{1,0:T(8,128)S(1)}, f32[6,2048]{1,0:T(8,128)}, u32[]{:S(2)}) copy-start(f32[6,2048]{1,0:T(8,128)} %drag.1) | copy-start | bytes 147460
  29.4 3.3 %collective-permute-start.15 = (f32[3,6,16,128]{3,2,1,0:T(8,128)S(1)}, f32[3,6,16,128]{3,2,1,0:T(8,128)S(1)}, u32[]{:S(2)}, u32[]{:S(2)}) collective-permute-start(f32[3,6,16,128]{3,2,1,0:T(8,128)S(1)} %pad_maximum_fusion.3.mid), channel_id=1, source_target_pairs={{0,3},{1,0},{2,1},{3,2},{4,7},{5,4},{6,5},{7,6},{8,11},{9,8},{10,9... | collective-permute-start | bytes 442376 | tf_op jit(solution)/shard_map/ppermute | solution.py:573
  29.5 6.2 %collective-permute-start.14 = (f32[3,6,16,128]{3,2,1,0:T(8,128)S(1)}, f32[3,6,16,128]{3,2,1,0:T(8,128)S(1)}, u32[]{:S(2)}, u32[]{:S(2)}) collective-permute-start(f32[3,6,16,128]{3,2,1,0:T(8,128)S(1)} %pad_maximum_fusion.3.mid), channel_id=1, source_target_pairs={{0,1},{1,2},{2,3},{3,0},{4,5},{5,6},{6,7},{7,4},{8,9},{9,10},{10,1... | collective-permute-start | bytes 442376 | tf_op jit(solution)/shard_map/ppermute | solution.py:572
  50.6 4.1 %collective-permute-start.17 = (f32[6,16,128]{2,1,0:T(8,128)S(1)}, f32[6,16,128]{2,1,0:T(8,128)S(1)}, u32[]{:S(2)}, u32[]{:S(2)}) collective-permute-start(f32[6,16,128]{2,1,0:T(8,128)S(1)} %get-tuple-element.67.k1), channel_id=1, source_target_pairs={{0,28},{4,0},{8,4},{12,8},{16,12},{20,16},{24,20},{28,24},{1,29},{... | collective-permute-start | bytes 147464 | tf_op jit(solution)/shard_map/ppermute | solution.py:570
  51.1 6.8 %collective-permute-start.16 = (f32[6,16,128]{2,1,0:T(8,128)S(1)}, f32[6,16,128]{2,1,0:T(8,128)S(1)}, u32[]{:S(2)}, u32[]{:S(2)}) collective-permute-start(f32[6,16,128]{2,1,0:T(8,128)S(1)} %get-tuple-element.67.k1), channel_id=1, source_target_pairs={{0,4},{4,8},{8,12},{12,16},{16,20},{20,24},{24,28},{28,0},{1,5},{5... | collective-permute-start | bytes 147464 | tf_op jit(solution)/shard_map/ppermute | solution.py:569
  57.9 4.2 %collective-permute-start.19 = (f32[3,6,16,128]{3,2,1,0:T(8,128)S(1)}, f32[3,6,16,128]{3,2,1,0:T(8,128)S(1)}, u32[]{:S(2)}, u32[]{:S(2)}) collective-permute-start(f32[3,6,16,128]{3,2,1,0:T(8,128)S(1)} %pad_maximum_fusion.4.mid), channel_id=1, source_target_pairs={{0,3},{1,0},{2,1},{3,2},{4,7},{5,4},{6,5},{7,6},{8,11},{9,8},{10,9... | collective-permute-start | bytes 442376 | tf_op jit(solution)/shard_map/ppermute | solution.py:573
  58.0 5.1 %collective-permute-start.18 = (f32[3,6,16,128]{3,2,1,0:T(8,128)S(1)}, f32[3,6,16,128]{3,2,1,0:T(8,128)S(1)}, u32[]{:S(2)}, u32[]{:S(2)}) collective-permute-start(f32[3,6,16,128]{3,2,1,0:T(8,128)S(1)} %pad_maximum_fusion.4.mid), channel_id=1, source_target_pairs={{0,1},{1,2},{2,3},{3,0},{4,5},{5,6},{6,7},{7,4},{8,9},{9,10},{10,1... | collective-permute-start | bytes 442376 | tf_op jit(solution)/shard_map/ppermute | solution.py:572
  67.7 4.1 %collective-permute-start.21 = (f32[6,16,128]{2,1,0:T(8,128)S(1)}, f32[6,16,128]{2,1,0:T(8,128)S(1)}, u32[]{:S(2)}, u32[]{:S(2)}) collective-permute-start(f32[6,16,128]{2,1,0:T(8,128)S(1)} %outer.7.k2), channel_id=1, source_target_pairs={{0,28},{4,0},{8,4},{12,8},{16,12},{20,16},{24,20},{28,24},{1,29},{... | collective-permute-start | bytes 147464 | tf_op jit(solution)/shard_map/ppermute | solution.py:570
  68.0 6.8 %collective-permute-start.20 = (f32[6,16,128]{2,1,0:T(8,128)S(1)}, f32[6,16,128]{2,1,0:T(8,128)S(1)}, u32[]{:S(2)}, u32[]{:S(2)}) collective-permute-start(f32[6,16,128]{2,1,0:T(8,128)S(1)} %outer.7.k2), channel_id=1, source_target_pairs={{0,4},{4,8},{8,12},{12,16},{16,20},{20,24},{24,28},{28,0},{1,5},{5... | collective-permute-start | bytes 147464 | tf_op jit(solution)/shard_map/ppermute | solution.py:569
  74.8 3.7 %collective-permute-start.23 = (f32[3,6,16,128]{3,2,1,0:T(8,128)S(1)}, f32[3,6,16,128]{3,2,1,0:T(8,128)S(1)}, u32[]{:S(2)}, u32[]{:S(2)}) collective-permute-start(f32[3,6,16,128]{3,2,1,0:T(8,128)S(1)} %pad_maximum_fusion.5.mid), channel_id=1, source_target_pairs={{0,3},{1,0},{2,1},{3,2},{4,7},{5,4},{6,5},{7,6},{8,11},{9,8},{10,9... | collective-permute-start | bytes 442376 | tf_op jit(solution)/shard_map/ppermute | solution.py:573
  74.9 6.1 %collective-permute-start.22 = (f32[3,6,16,128]{3,2,1,0:T(8,128)S(1)}, f32[3,6,16,128]{3,2,1,0:T(8,128)S(1)}, u32[]{:S(2)}, u32[]{:S(2)}) collective-permute-start(f32[3,6,16,128]{3,2,1,0:T(8,128)S(1)} %pad_maximum_fusion.5.mid), channel_id=1, source_target_pairs={{0,1},{1,2},{2,3},{3,0},{4,5},{5,6},{6,7},{7,4},{8,9},{9,10},{10,1... | collective-permute-start | bytes 442376 | tf_op jit(solution)/shard_map/ppermute | solution.py:572

commit v5 on v4

--- a/solution.py
+++ b/solution.py
@@ -50,8 +50,9 @@
     second_block = second >> shift
     owner = first_block >> log2(strips)
     shift_x = ((second_block >> log2(strips)) - owner + 1) & (slabs - 1)
-    shift_y = ((second_block & (strips - 1)) - (first_block & (strips - 1)) + 1) & (strips - 1)
-    column = (shift_y * 3 + shift_x) * spheres + (second & (spheres - 1))
+    apart = (second_block ^ first_block) & (strips - 1)
+    strip = jnp.where(apart == 0, 0, jnp.where(apart == 1, 1, 2))
+    column = (strip * 3 + shift_x) * spheres + (second & (spheres - 1))
     place = first & (spheres - 1)
     tile = slot * (spheres // TILE) + (place >> log2(TILE))
     target = ((place & (LANES - 1)) * SUB + ((place >> log2(LANES)) & (SUB - 1))) * (K * spheres // TILE) + tile
@@ -306,7 +307,7 @@
         return lax.fori_loop(start, jnp.minimum(self.high, 3 * strip + 2) + 1, block, values)
 
 
-def apply_inner(mid, span_ref, col_ref, terms_ref, drag_ref, out_ref):
+def apply_inner(mid, near, span_ref, col_ref, terms_ref, drag_ref, out_ref):
     chunks = mid.shape[2]
     halves = chunks // SUB
 
@@ -315,7 +316,7 @@
 
     def slot(k, sums):
         here = Slot(k, halves, span_ref, col_ref)
-        other = here.gather(1, mid, here.none())
+        other = here.gather(1, near, here.gather(0, mid, here.none()))
         sums = list(sums)
         for h in range(halves):
             diff = [own(h, c) - other[h * FIELDS + c] for c in range(FIELDS)]
@@ -333,16 +334,16 @@
             out_ref[c, h * SUB : (h + 1) * SUB, :] = sums[h * FIELDS + c]
 
 
-def apply_outer(below, above, span_ref, col_ref, terms_ref, part_ref, out_ref):
-    halves = below.shape[2] // SUB
+def apply_outer(far, span_ref, col_ref, terms_ref, part_ref, out_ref):
+    halves = far.shape[2] // SUB
     out_ref[...] = part_ref[...]
 
     def slot(k, carry):
         here = Slot(k, halves, span_ref, col_ref)
 
-        @pl.when(jnp.logical_or(here.low < 3, here.high > 5))
+        @pl.when(here.high >= 6)
         def _():
-            other = here.gather(2, above, here.gather(0, below, here.none()))
+            other = here.gather(2, far, here.none())
             for h in range(halves):
                 terms = tile_terms(terms_ref, here.rows[h], other[h * FIELDS : (h + 1) * FIELDS])
                 for c, term in enumerate(terms):
@@ -491,7 +492,7 @@
 
 
 def first_kernel(
-    spheres, got, drag, below, mid, above, terms, col, span, drag_out, out, part, pos, tab, tab_s, span_s, sem
+    spheres, got, drag, mid, near, terms, col, span, drag_out, part, pos, tab, tab_s, span_s, sem
 ):
     chunks = spheres // LANES
     place_ranges(got, tab)
@@ -506,25 +507,24 @@
     copy = pltpu.make_async_copy(span, span_s, sem)
     copy.start()
     copy.wait()
-    apply_inner(mid, span_s, col, terms, drag_out, part)
-    apply_outer(below, above, span_s, col, terms, part, out)
-
-
-def inner_kernel(span, col, terms, drag, mid, part):
-    apply_inner(mid, span, col, terms, drag, part)
-
-
-def outer_kernel(span, col, terms, part, below, above, out):
-    apply_outer(below, above, span, col, terms, part, out)
-
-
-def inner_gram_kernel(span, col, terms, drag, mid, k0, k1, part, row):
-    apply_inner(mid, span, col, terms, drag, part)
+    apply_inner(mid, near, span_s, col, terms, drag_out, part)
+
+
+def inner_kernel(span, col, terms, drag, mid, near, part):
+    apply_inner(mid, near, span, col, terms, drag, part)
+
+
+def outer_kernel(span, col, terms, part, far, out):
+    apply_outer(far, span, col, terms, part, out)
+
+
+def inner_gram_kernel(span, col, terms, drag, mid, near, k0, k1, part, row):
+    apply_inner(mid, near, span, col, terms, drag, part)
     row[...] = jnp.broadcast_to(gram_row([k0, k1, mid.at[1]], EARLY), row.shape)
 
 
-def outer_gram_kernel(span, col, terms, part, below, above, k0, k1, k2, row, out, rows):
-    apply_outer(below, above, span, col, terms, part, out)
+def outer_gram_kernel(span, col, terms, part, far, k0, k1, k2, row, out, rows):
+    apply_outer(far, span, col, terms, part, out)
     late = row[0:1, :] + gram_row([k0, k1, k2, out], LATE)
     rows[...] = jnp.broadcast_to(late, rows.shape)
 
@@ -569,9 +569,10 @@
     west = lax.ppermute(x, "gx", ring("gx", 1))
     east = lax.ppermute(x, "gx", ring("gx", -1))
     mid = jnp.stack([west, x, east])
-    below = lax.ppermute(mid, "gy", ring("gy", 1))
-    above = lax.ppermute(mid, "gy", ring("gy", -1))
-    return below, mid, above
+    count = lax.axis_size("gy")
+    near = lax.ppermute(mid, "gy", [(i, i ^ 1) for i in range(count)])
+    far = lax.ppermute(mid, "gy", [(i, (i + 1 if i % 2 else i - 1) % count) for i in range(count)])
+    return mid, near, far
 
 
 def plain(apply, forces):
@@ -599,13 +600,13 @@
     devices = slabs * lax.axis_size("gy")
     field = (FIELDS, chunks, LANES)
     slot_rows = K * spheres // LANES
-    dense = pltpu.VMEM(field, f32)
     ranges = (slabs // SUB, 2, SUB, LANES)
     assert K * spheres == SUB * 4 * TILE and slabs % SUB == 0
     send, k0 = pack(pair_ends, pair_geometry, forces, slabs, lax.axis_size("gy"))
     got = lax.all_to_all(send, "gx", split_axis=0, concat_axis=0, tiled=True)
     k0 = k0.reshape(field)
-    terms, col, span, drag, k1 = pl.pallas_call(
+    mid, near, far = beside(k0)
+    terms, col, span, drag, part = pl.pallas_call(
         functools.partial(first_kernel, spheres),
         out_shape=(
             shape((SENT - 2, slot_rows, LANES)),
@@ -614,9 +615,8 @@
             shape((FIELDS * chunks, LANES)),
             shape(field),
         ),
-        in_specs=[VMEM] * 5,
+        in_specs=[VMEM] * 4,
         scratch_shapes=[
-            dense,
             pltpu.VMEM((slot_rows // SUB, SUB, LANES), i32),
             pltpu.VMEM(ranges, i32),
             pltpu.SMEM(ranges, i32),
@@ -624,8 +624,9 @@
             pltpu.SemaphoreType.DMA,
         ],
         compiler_params=PARAMS,
+        cost_estimate=pl.CostEstimate(flops=0, bytes_accessed=48 << 20, transcendentals=0),
         name="first",
-    )(got, drag_coef, *beside(k0))
+    )(got, drag_coef, mid, near)
 
     def local(kernel, name, outs, cost, *args):
         return pl.pallas_call(
@@ -637,19 +638,20 @@
             name=name,
         )(span, col, terms, *args)
 
+    k1 = local(outer_kernel, "outer", shape(field), 16, part, far)
+
     def apply(x):
-        below, mid, above = beside(x)
-        part = local(inner_kernel, "inner", shape(field), 16, drag, mid)
-        return local(outer_kernel, "outer", shape(field), 16, part, below, above)
+        mid, near, far = beside(x)
+        part = local(inner_kernel, "inner", shape(field), 16, drag, mid, near)
+        return local(outer_kernel, "outer", shape(field), 16, part, far)
 
     k2 = apply(k1)
-    below, mid, above = beside(k2)
+    mid, near, far = beside(k2)
     part, row = local(
-        inner_gram_kernel, "inner_gram", (shape(field), shape((SUB, LANES))), 16, drag, mid, k0, k1
+        inner_gram_kernel, "inner_gram", (shape(field), shape((SUB, LANES))), 16, drag, mid, near, k0, k1
     )
     k3, rows = local(
-        outer_gram_kernel, "outer_gram", (shape(field), shape((devices, LANES))), 16,
-        part, below, above, k0, k1, k2, row,
+        outer_gram_kernel, "outer_gram", (shape(field), shape((devices, LANES))), 16, part, far, k0, k1, k2, row
     )
     rows = lax.all_to_all(rows, ("gx", "gy"), split_axis=0, concat_axis=0, tiled=True)
     velocity, residual, good = pl.pallas_call(

time: 99.4 us -> 93.5 us (0.941)
  waiting for transfers between devices: 34.7 us -> 25.5 us
  starting transfers between devices: 17.8 us -> 21.8 us
  blocking collectives: 10.1 us -> 8.83 us
    ppermute x6, waiting for transfers between devices: 10.4 us -> 0.02 us  [the longest x3 0.01 us: beside(): lax.ppermute(mid, 'gy', [(i, (i + 1 if i % 2 else i - 1) % count) for i i...]
    ppermute x6, starting transfers between devices: 1.66 us -> 5.68 us  [the longest x3 5.47 us: beside(): lax.ppermute(mid, 'gy', [(i, (i + 1 if i % 2 else i - 1) % count) for i i...]
    pallas_call x4 -> x5, Pallas kernels: 15.5 us -> 18 us  [local(): pl.pallas_call(kernel, out_shape=outs, in_specs=[SMEM] + [VMEM] * (len(ar...]
    pallas_call x1, Pallas kernels: 14.9 us -> 12.9 us  [on_device(): pl.pallas_call(functools.partial(first_kernel, spheres), out_shape=(shape...]
    all_to_all x1, blocking collectives: 10.1 us -> 8.83 us  [on_device(): lax.all_to_all(rows, ('gx', 'gy'), split_axis=0, concat_axis=0, tiled=True)]
    ppermute x3, waiting for transfers between devices: 11 us -> 12 us  [beside(): west = lax.ppermute(x, 'gx', ring('gx', 1))]
  transfers between devices with their start and end apart: 13 -> 13, of which waited for: 11 -> 7; matrix products, arithmetic and copies ran while one was open for 0% -> 0% of each run, Pallas kernels for 6% -> 23%
where the time goes in v5:
time: 93.5 us; the launch traced here: 93.3 us
  Pallas kernels  35.5 us (38%)
  waiting for transfers between devices  25.5 us (27%)
  starting transfers between devices  21.8 us (23%)
  blocking collectives  8.83 us (9%)
    pallas_call x5, Pallas kernels, local(): pl.pallas_call(kernel, out_shape=outs, in_specs=[SMEM] + [VMEM] * (len(ar...  18 us
    ppermute x3, waiting for transfers between devices, beside(): east = lax.ppermute(x, 'gx', ring('gx', -1))  13.2 us
    pallas_call x1, Pallas kernels, on_device(): pl.pallas_call(functools.partial(first_kernel, spheres), out_shape=(shape...  12.9 us
    ppermute x3, waiting for transfers between devices, beside(): west = lax.ppermute(x, 'gx', ring('gx', 1))  12 us
    all_to_all x1, blocking collectives, on_device(): lax.all_to_all(rows, ('gx', 'gy'), split_axis=0, concat_axis=0, tiled=True)  8.83 us
    all_to_all x1, starting transfers between devices, on_device(): got = lax.all_to_all(send, 'gx', split_axis=0, concat_axis=0, tiled=True)  7.25 us
    ppermute x3, starting transfers between devices, beside(): east = lax.ppermute(x, 'gx', ring('gx', -1))  6.46 us
    ppermute x3, starting transfers between devices, beside(): lax.ppermute(mid, 'gy', [(i, (i + 1 if i % 2 else i - 1) % count) for i i...  5.47 us
  transfers between devices with their start and end apart: 13, of which 7 were waited for; matrix products, arithmetic and copies ran while one was open for 0% of the time, Pallas kernels for 23%

profile of v5, /device:TPU:0, one launch (start us, length us, event | category | flops | bytes accessed | tf_op | source)
XLA Modules:
  0.0 93.3 jit_solution(2524759541081652609)
XLA Ops:
  0.6 2.7 %pack.1 = (f32[8,6,32,128]{3,2,1,0:T(8,128)}, f32[96,128]{1,0:T(8,128)S(1)}) custom-call(s32[3,14464]{1,0:T(4,128)} %ends_ref.1, f32[5,14464]{1,0:T(8,128)} %geo_ref.1, f32[6,2048]{1,0:T(8,128)} %force_ref.1), custom_call_target="tpu_custom_call" | custom-call | tf_op jit(solution)/shard_map/pack/pallas_call | solution.py:93
  3.3 7.3 %all-to-all-start = ((f32[8,6,32,128]{3,2,1,0:T(8,128)}), f32[8,6,32,128]{3,2,1,0:T(8,128)S(1)}, u32[]{:S(2)}, u32[]{:S(2)}) async-start(f32[8,6,32,128]{3,2,1,0:T(8,128)} %get-tuple-element.61), calls=%async_computation | async-start | bytes 1572864 | tf_op jit(solution)/shard_map/all_to_all | solution.py:606
  10.6 4.7 %collective-permute-start.13 = (f32[6,16,128]{2,1,0:T(8,128)S(1)}, f32[6,16,128]{2,1,0:T(8,128)S(1)}, u32[]{:S(2)}, u32[]{:S(2)}) collective-permute-start(f32[6,16,128]{2,1,0:T(8,128)S(1)} %bitcast.38), channel_id=1, source_target_pairs={{0,28},{4,0},{8,4},{12,8},{16,12},{20,16},{24,20},{28,24},{1,29},{... | collective-permute-start | bytes 147464 | tf_op jit(solution)/shard_map/ppermute | solution.py:570
  15.3 9.1 %collective-permute-done.13 = f32[6,16,128]{2,1,0:T(8,128)S(1)} collective-permute-done((f32[6,16,128]{2,1,0:T(8,128)S(1)}, f32[6,16,128]{2,1,0:T(8,128)S(1)}, u32[]{:S(2)}, u32[]{:S(2)}) %collective-permute-start.13) | collective-permute-done | bytes 49184 | tf_op jit(solution)/shard_map/ppermute | solution.py:570
  24.4 4.9 %collective-permute-done.12 = f32[6,16,128]{2,1,0:T(8,128)S(1)} collective-permute-done((f32[6,16,128]{2,1,0:T(8,128)S(1)}, f32[6,16,128]{2,1,0:T(8,128)S(1)}, u32[]{:S(2)}, u32[]{:S(2)}) %collective-permute-start.12) | collective-permute-done | bytes 49184 | tf_op jit(solution)/shard_map/ppermute | solution.py:569
  29.4 0.1 collective-permute-start.14
  29.5 1.6 %collective-permute-start.15 = (f32[3,6,16,128]{3,2,1,0:T(8,128)S(1)}, f32[3,6,16,128]{3,2,1,0:T(8,128)S(1)}, u32[]{:S(2)}, u32[]{:S(2)}) collective-permute-start(f32[3,6,16,128]{3,2,1,0:T(8,128)S(1)} %pad_maximum_fusion.3.mid), channel_id=1, source_target_pairs={{0,3},{1,2},{2,1},{3,0},{4,7},{5,6},{6,5},{7,4},{8,11},{9,10},{10,... | collective-permute-start | bytes 442376 | tf_op jit(solution)/shard_map/ppermute | solution.py:574
  31.1 0.2 all-to-all-done.got
  31.3 12.9 %first.1 = (f32[4,256,128]{2,1,0:T(8,128)S(1)}, s32[256,128]{1,0:T(8,128)S(1)}, s32[16,128]{1,0:T(8,128)S(1)}, f32[96,128]{1,0:T(8,128)S(1)}, f32[6,16,128]{2,1,0:T(8,128)S(1)}) custom-call(f32[8,6,32,128]{3,2,1,0:T(8,128)S(1)} %all-to-all-done.got, f32[6,2048]{1,0:T(8,128)S(1)} %copy-done, f32[3,6,16,128]{3,2,1,0:T(8,128)S(1)} %pad_maximum_fusion.3.mid, ...), custom_call_target="tpu_custom_call" | custom-call | bytes 50331648 | tf_op jit(solution)/shard_map/first/pallas_call | solution.py:609
  44.2 0.0 collective-permute-done.15.far
  44.2 2.8 %outer.8.k1 = f32[6,16,128]{2,1,0:T(8,128)S(1)} custom-call(s32[16,128]{1,0:T(8,128)S(1)} %get-tuple-element.117.span, s32[256,128]{1,0:T(8,128)S(1)} %get-tuple-element.118.col, f32[4,256,128]{2,1,0:T(8,128)S(1)} %get-tuple-element.119.terms, f32[6,16,128]{2,1,0:T(8,128)S(1)} %get-tuple-element.67.part, f32[3,6,16,128]{3,2,1,0:T(8,128)S(1)} %collective-permute-done.15.far), custom_call_target="tpu_custom_call" | custom-call | bytes 16777216 | tf_op jit(solution)/shard_map/outer/pallas_call | solution.py:632
  47.0 1.7 %collective-permute-start.17 = (f32[6,16,128]{2,1,0:T(8,128)S(1)}, f32[6,16,128]{2,1,0:T(8,128)S(1)}, u32[]{:S(2)}, u32[]{:S(2)}) collective-permute-start(f32[6,16,128]{2,1,0:T(8,128)S(1)} %outer.8.k1), channel_id=1, source_target_pairs={{0,28},{4,0},{8,4},{12,8},{16,12},{20,16},{24,20},{28,24},{1,29},{... | collective-permute-start | bytes 147464 | tf_op jit(solution)/shard_map/ppermute | solution.py:570
  48.7 0.4 collective-permute-start.16
  49.1 2.1 %collective-permute-done.17 = f32[6,16,128]{2,1,0:T(8,128)S(1)} collective-permute-done((f32[6,16,128]{2,1,0:T(8,128)S(1)}, f32[6,16,128]{2,1,0:T(8,128)S(1)}, u32[]{:S(2)}, u32[]{:S(2)}) %collective-permute-start.17) | collective-permute-done | bytes 49184 | tf_op jit(solution)/shard_map/ppermute | solution.py:570
  51.2 4.3 %collective-permute-done.16 = f32[6,16,128]{2,1,0:T(8,128)S(1)} collective-permute-done((f32[6,16,128]{2,1,0:T(8,128)S(1)}, f32[6,16,128]{2,1,0:T(8,128)S(1)}, u32[]{:S(2)}, u32[]{:S(2)}) %collective-permute-start.16) | collective-permute-done | bytes 49184 | tf_op jit(solution)/shard_map/ppermute | solution.py:569
  55.5 0.1 collective-permute-start.18
  55.6 2.3 %collective-permute-start.19 = (f32[3,6,16,128]{3,2,1,0:T(8,128)S(1)}, f32[3,6,16,128]{3,2,1,0:T(8,128)S(1)}, u32[]{:S(2)}, u32[]{:S(2)}) collective-permute-start(f32[3,6,16,128]{3,2,1,0:T(8,128)S(1)} %pad_maximum_fusion.4.mid), channel_id=1, source_target_pairs={{0,3},{1,2},{2,1},{3,0},{4,7},{5,6},{6,5},{7,4},{8,11},{9,10},{10,... | collective-permute-start | bytes 442376 | tf_op jit(solution)/shard_map/ppermute | solution.py:574
  57.9 0.0 collective-permute-done.18.near
  57.9 4.1 %inner.7.part = f32[6,16,128]{2,1,0:T(8,128)S(1)} custom-call(s32[16,128]{1,0:T(8,128)S(1)} %get-tuple-element.117.span, s32[256,128]{1,0:T(8,128)S(1)} %get-tuple-element.118.col, f32[4,256,128]{2,1,0:T(8,128)S(1)} %get-tuple-element.119.terms, f32[96,128]{1,0:T(8,128)S(1)} %get-tuple-element.120.drag, f32[3,6,16,128]{3,2,1,0:T(8,128)S(1)} %pad_maximum_fusion.4.mid, ...), custom_call_target="tpu_custom_call" | custom-call | bytes 16777216 | tf_op jit(solution)/shard_map/inner/pallas_call | solution.py:632
  62.0 0.0 collective-permute-done.19.far
  62.0 2.8 %outer.9.k2 = f32[6,16,128]{2,1,0:T(8,128)S(1)} custom-call(s32[16,128]{1,0:T(8,128)S(1)} %get-tuple-element.117.span, s32[256,128]{1,0:T(8,128)S(1)} %get-tuple-element.118.col, f32[4,256,128]{2,1,0:T(8,128)S(1)} %get-tuple-element.119.terms, f32[6,16,128]{2,1,0:T(8,128)S(1)} %inner.7.part, f32[3,6,16,128]{3,2,1,0:T(8,128)S(1)} %collective-permute-done.19.far), custom_call_target="tpu_custom_call" | custom-call | bytes 16777216 | tf_op jit(solution)/shard_map/outer/pallas_call | solution.py:632
  64.8 0.1 collective-permute-start.21
  64.9 2.0 %collective-permute-start.20 = (f32[6,16,128]{2,1,0:T(8,128)S(1)}, f32[6,16,128]{2,1,0:T(8,128)S(1)}, u32[]{:S(2)}, u32[]{:S(2)}) collective-permute-start(f32[6,16,128]{2,1,0:T(8,128)S(1)} %outer.9.k2), channel_id=1, source_target_pairs={{0,4},{4,8},{8,12},{12,16},{16,20},{20,24},{24,28},{28,0},{1,5},{5... | collective-permute-start | bytes 147464 | tf_op jit(solution)/shard_map/ppermute | solution.py:569
  66.9 2.1 %collective-permute-done.21 = f32[6,16,128]{2,1,0:T(8,128)S(1)} collective-permute-done((f32[6,16,128]{2,1,0:T(8,128)S(1)}, f32[6,16,128]{2,1,0:T(8,128)S(1)}, u32[]{:S(2)}, u32[]{:S(2)}) %collective-permute-start.21) | collective-permute-done | bytes 49184 | tf_op jit(solution)/shard_map/ppermute | solution.py:570
  69.0 2.8 %collective-permute-done.20 = f32[6,16,128]{2,1,0:T(8,128)S(1)} collective-permute-done((f32[6,16,128]{2,1,0:T(8,128)S(1)}, f32[6,16,128]{2,1,0:T(8,128)S(1)}, u32[]{:S(2)}, u32[]{:S(2)}) %collective-permute-start.20) | collective-permute-done | bytes 49184 | tf_op jit(solution)/shard_map/ppermute | solution.py:569
  71.7 0.1 collective-permute-start.22
  71.8 1.5 %collective-permute-start.23 = (f32[3,6,16,128]{3,2,1,0:T(8,128)S(1)}, f32[3,6,16,128]{3,2,1,0:T(8,128)S(1)}, u32[]{:S(2)}, u32[]{:S(2)}) collective-permute-start(f32[3,6,16,128]{3,2,1,0:T(8,128)S(1)} %pad_maximum_fusion.5.mid), channel_id=1, source_target_pairs={{0,3},{1,2},{2,1},{3,0},{4,7},{5,6},{6,5},{7,4},{8,11},{9,10},{10,... | collective-permute-start | bytes 442376 | tf_op jit(solution)/shard_map/ppermute | solution.py:574
  73.3 4.9 %inner_gram.1 = (f32[6,16,128]{2,1,0:T(8,128)S(1)}, f32[8,128]{1,0:T(8,128)S(1)}) custom-call(s32[16,128]{1,0:T(8,128)S(1)} %get-tuple-element.117.span, s32[256,128]{1,0:T(8,128)S(1)} %get-tuple-element.118.col, f32[4,256,128]{2,1,0:T(8,128)S(1)} %get-tuple-element.119.terms, f32[96,128]{1,0:T(8,128)S(1)} %get-tuple-element.120.drag, ...), custom_call_target="tpu_custom_call" | custom-call | bytes 16777216 | tf_op jit(solution)/shard_map/inner_gram/pallas_call | solution.py:632
  78.2 3.5 %outer_gram.1 = (f32[6,16,128]{2,1,0:T(8,128)S(1)}, f32[32,128]{1,0:T(8,128)S(1)}) custom-call(s32[16,128]{1,0:T(8,128)S(1)} %get-tuple-element.117.span, s32[256,128]{1,0:T(8,128)S(1)} %get-tuple-element.118.col, f32[4,256,128]{2,1,0:T(8,128)S(1)} %get-tuple-element.119.terms, f32[6,16,128]{2,1,0:T(8,128)S(1)} %get-tuple-element.68.part, ...), custom_call_target="tpu_custom_call" | custom-call | bytes 16777216 | tf_op jit(solution)/shard_map/outer_gram/pallas_call | solution.py:632
  81.7 8.8 %all_to_all.16 = f32[32,1,128]{2,1,0:T(1,128)S(1)} all-to-all(f32[32,1,128]{2,1,0:T(1,128)S(1)} %bitcast.37), channel_id=1, replica_groups=mesh['gx'=8,'gy'=4] {'gx','gy'}, dimensions={0} | all-to-all | bytes 32768 | tf_op jit(solution)/shard_map/all_to_all | solution.py:656
  90.5 1.9 %last.1 = (f32[6,2048]{1,0:T(8,128)}, f32[6,2048]{1,0:T(8,128)}, s32[1,1]{1,0:T(1,128)}) custom-call(f32[32,128]{1,0:T(8,128)S(1)} %bitcast.36, f32[6,16,128]{2,1,0:T(8,128)S(1)} %bitcast.43, f32[6,16,128]{2,1,0:T(8,128)S(1)} %outer.8.k1, f32[6,16,128]{2,1,0:T(8,128)S(1)} %outer.9.k2, f32[6,16,128]{2,1,0:T(8,128)S(1)} %get-tuple-element.71.k3), custom_call_target="tpu_custom_call" | custom-call | tf_op jit(solution)/shard_map/last/pallas_call | solution.py:657
  92.4 0.7 while.11
  (9 shorter events, 0.0 us)
Async XLA Ops:
  3.3 28.0 %all-to-all-start = ((f32[8,6,32,128]{3,2,1,0:T(8,128)}), f32[8,6,32,128]{3,2,1,0:T(8,128)S(1)}, u32[]{:S(2)}, u32[]{:S(2)}) async-start(f32[8,6,32,128]{3,2,1,0:T(8,128)} %get-tuple-element.61), calls=%async_computation | async-start | bytes 1572864 | tf_op jit(solution)/shard_map/all_to_all | solution.py:606
  10.6 13.8 %collective-permute-start.13 = (f32[6,16,128]{2,1,0:T(8,128)S(1)}, f32[6,16,128]{2,1,0:T(8,128)S(1)}, u32[]{:S(2)}, u32[]{:S(2)}) collective-permute-start(f32[6,16,128]{2,1,0:T(8,128)S(1)} %bitcast.38), channel_id=1, source_target_pairs={{0,28},{4,0},{8,4},{12,8},{16,12},{20,16},{24,20},{28,24},{1,29},{... | collective-permute-start | bytes 147464 | tf_op jit(solution)/shard_map/ppermute | solution.py:570
  15.3 14.1 %collective-permute-start.12 = (f32[6,16,128]{2,1,0:T(8,128)S(1)}, f32[6,16,128]{2,1,0:T(8,128)S(1)}, u32[]{:S(2)}, u32[]{:S(2)}) collective-permute-start(f32[6,16,128]{2,1,0:T(8,128)S(1)} %bitcast.39), channel_id=1, source_target_pairs={{0,4},{4,8},{8,12},{12,16},{16,20},{20,24},{24,28},{28,0},{1,5},{5... | collective-permute-start | bytes 147464 | tf_op jit(solution)/shard_map/ppermute | solution.py:569
  29.4 1.9 %copy-start = (f32[6,2048]{1,0:T(8,128)S(1)}, f32[6,2048]{1,0:T(8,128)}, u32[]{:S(2)}) copy-start(f32[6,2048]{1,0:T(8,128)} %drag.1) | copy-start | bytes 147460
  29.4 1.7 %collective-permute-start.14 = (f32[3,6,16,128]{3,2,1,0:T(8,128)S(1)}, f32[3,6,16,128]{3,2,1,0:T(8,128)S(1)}, u32[]{:S(2)}, u32[]{:S(2)}) collective-permute-start(f32[3,6,16,128]{3,2,1,0:T(8,128)S(1)} %pad_maximum_fusion.3.mid), channel_id=1, source_target_pairs={{0,1},{1,0},{2,3},{3,2},{4,5},{5,4},{6,7},{7,6},{8,9},{9,8},{10,11... | collective-permute-start | bytes 442376 | tf_op jit(solution)/shard_map/ppermute | solution.py:573
  29.5 14.7 %collective-permute-start.15 = (f32[3,6,16,128]{3,2,1,0:T(8,128)S(1)}, f32[3,6,16,128]{3,2,1,0:T(8,128)S(1)}, u32[]{:S(2)}, u32[]{:S(2)}) collective-permute-start(f32[3,6,16,128]{3,2,1,0:T(8,128)S(1)} %pad_maximum_fusion.3.mid), channel_id=1, source_target_pairs={{0,3},{1,2},{2,1},{3,0},{4,7},{5,6},{6,5},{7,4},{8,11},{9,10},{10,... | collective-permute-start | bytes 442376 | tf_op jit(solution)/shard_map/ppermute | solution.py:574
  47.0 4.1 %collective-permute-start.17 = (f32[6,16,128]{2,1,0:T(8,128)S(1)}, f32[6,16,128]{2,1,0:T(8,128)S(1)}, u32[]{:S(2)}, u32[]{:S(2)}) collective-permute-start(f32[6,16,128]{2,1,0:T(8,128)S(1)} %outer.8.k1), channel_id=1, source_target_pairs={{0,28},{4,0},{8,4},{12,8},{16,12},{20,16},{24,20},{28,24},{1,29},{... | collective-permute-start | bytes 147464 | tf_op jit(solution)/shard_map/ppermute | solution.py:570
  48.7 6.8 %collective-permute-start.16 = (f32[6,16,128]{2,1,0:T(8,128)S(1)}, f32[6,16,128]{2,1,0:T(8,128)S(1)}, u32[]{:S(2)}, u32[]{:S(2)}) collective-permute-start(f32[6,16,128]{2,1,0:T(8,128)S(1)} %outer.8.k1), channel_id=1, source_target_pairs={{0,4},{4,8},{8,12},{12,16},{16,20},{20,24},{24,28},{28,0},{1,5},{5... | collective-permute-start | bytes 147464 | tf_op jit(solution)/shard_map/ppermute | solution.py:569
  55.5 2.4 %collective-permute-start.18 = (f32[3,6,16,128]{3,2,1,0:T(8,128)S(1)}, f32[3,6,16,128]{3,2,1,0:T(8,128)S(1)}, u32[]{:S(2)}, u32[]{:S(2)}) collective-permute-start(f32[3,6,16,128]{3,2,1,0:T(8,128)S(1)} %pad_maximum_fusion.4.mid), channel_id=1, source_target_pairs={{0,1},{1,0},{2,3},{3,2},{4,5},{5,4},{6,7},{7,6},{8,9},{9,8},{10,11... | collective-permute-start | bytes 442376 | tf_op jit(solution)/shard_map/ppermute | solution.py:573
  55.6 6.5 %collective-permute-start.19 = (f32[3,6,16,128]{3,2,1,0:T(8,128)S(1)}, f32[3,6,16,128]{3,2,1,0:T(8,128)S(1)}, u32[]{:S(2)}, u32[]{:S(2)}) collective-permute-start(f32[3,6,16,128]{3,2,1,0:T(8,128)S(1)} %pad_maximum_fusion.4.mid), channel_id=1, source_target_pairs={{0,3},{1,2},{2,1},{3,0},{4,7},{5,6},{6,5},{7,4},{8,11},{9,10},{10,... | collective-permute-start | bytes 442376 | tf_op jit(solution)/shard_map/ppermute | solution.py:574
  64.8 4.1 %collective-permute-start.21 = (f32[6,16,128]{2,1,0:T(8,128)S(1)}, f32[6,16,128]{2,1,0:T(8,128)S(1)}, u32[]{:S(2)}, u32[]{:S(2)}) collective-permute-start(f32[6,16,128]{2,1,0:T(8,128)S(1)} %outer.9.k2), channel_id=1, source_target_pairs={{0,28},{4,0},{8,4},{12,8},{16,12},{20,16},{24,20},{28,24},{1,29},{... | collective-permute-start | bytes 147464 | tf_op jit(solution)/shard_map/ppermute | solution.py:570
  64.9 6.8 %collective-permute-start.20 = (f32[6,16,128]{2,1,0:T(8,128)S(1)}, f32[6,16,128]{2,1,0:T(8,128)S(1)}, u32[]{:S(2)}, u32[]{:S(2)}) collective-permute-start(f32[6,16,128]{2,1,0:T(8,128)S(1)} %outer.9.k2), channel_id=1, source_target_pairs={{0,4},{4,8},{8,12},{12,16},{16,20},{20,24},{24,28},{28,0},{1,5},{5... | collective-permute-start | bytes 147464 | tf_op jit(solution)/shard_map/ppermute | solution.py:569
  71.7 1.6 %collective-permute-start.22 = (f32[3,6,16,128]{3,2,1,0:T(8,128)S(1)}, f32[3,6,16,128]{3,2,1,0:T(8,128)S(1)}, u32[]{:S(2)}, u32[]{:S(2)}) collective-permute-start(f32[3,6,16,128]{3,2,1,0:T(8,128)S(1)} %pad_maximum_fusion.5.mid), channel_id=1, source_target_pairs={{0,1},{1,0},{2,3},{3,2},{4,5},{5,4},{6,7},{7,6},{8,9},{9,8},{10,11... | collective-permute-start | bytes 442376 | tf_op jit(solution)/shard_map/ppermute | solution.py:573
  71.8 6.4 %collective-permute-start.23 = (f32[3,6,16,128]{3,2,1,0:T(8,128)S(1)}, f32[3,6,16,128]{3,2,1,0:T(8,128)S(1)}, u32[]{:S(2)}, u32[]{:S(2)}) collective-permute-start(f32[3,6,16,128]{3,2,1,0:T(8,128)S(1)} %pad_maximum_fusion.5.mid), channel_id=1, source_target_pairs={{0,3},{1,2},{2,1},{3,0},{4,7},{5,6},{6,5},{7,4},{8,11},{9,10},{10,... | collective-permute-start | bytes 442376 | tf_op jit(solution)/shard_map/ppermute | solution.py:574

commit v6 on v5

--- a/solution.py
+++ b/solution.py
@@ -49,10 +49,11 @@
     first_block = first >> shift
     second_block = second >> shift
     owner = first_block >> log2(strips)
-    shift_x = ((second_block >> log2(strips)) - owner + 1) & (slabs - 1)
+    apart = (second_block >> log2(strips)) ^ owner
+    slab = jnp.where(apart == 0, 1, jnp.where(apart == 1, 2, 0))
     apart = (second_block ^ first_block) & (strips - 1)
     strip = jnp.where(apart == 0, 0, jnp.where(apart == 1, 1, 2))
-    column = (strip * 3 + shift_x) * spheres + (second & (spheres - 1))
+    column = (strip * 3 + slab) * spheres + (second & (spheres - 1))
     place = first & (spheres - 1)
     tile = slot * (spheres // TILE) + (place >> log2(TILE))
     target = ((place & (LANES - 1)) * SUB + ((place >> log2(LANES)) & (SUB - 1))) * (K * spheres // TILE) + tile
@@ -76,9 +77,8 @@
         off = start & (LANES - 1)
         back = (LANES - off) & (LANES - 1)
         for c in range(SENT):
-            here = pltpu.roll(out_s[c, pl.ds(row, cap_rows), :], back, 1)
-            after = pltpu.roll(out_s[c, pl.ds(row + 1, cap_rows), :], back, 1)
-            value = jnp.where(lane < LANES - off, here, after)
+            rolled = pltpu.roll(out_s[c, pl.ds(row, cap_rows + SUB), :], back, 1)
+            value = jnp.where(lane < LANES - off, rolled[:cap_rows], rolled[1 : cap_rows + 1])
             if c == 0:
                 value = jnp.where(place < end - start, value, -1.0)
             send_ref[o, c] = value
@@ -150,6 +150,9 @@
             2, LANES, 1 << (bit - tile_bits - sub_bits))
         if 2 * d == size:
             return pltpu.roll(x, d, axis)
+        if axis == 1:
+            at = iota((SUB, LANES), 0) ^ d
+            return jnp.stack([jnp.take_along_axis(x[n], at, axis=0) for n in range(tiles)])
         upper = (iota(dims, axis) & d) != 0
         return jnp.where(upper, pltpu.roll(x, d, axis), pltpu.roll(x, size - d, axis))
 
@@ -238,7 +241,7 @@
 
         return carry
 
-    lax.fori_loop(0, tiles, first_rows, 0, unroll=4)
+    lax.fori_loop(0, tiles, first_rows, 0, unroll=8)
     lax.fori_loop(0, tiles, more_rows, 0)
 
 
@@ -565,14 +568,18 @@
     return [(i, (i + step) % count) for i in range(count)]
 
 
+def partners(axis):
+    count = lax.axis_size(axis)
+    return [(i, i ^ 1) for i in range(count)], [(i, (i + 1 if i % 2 else i - 1) % count) for i in range(count)]
+
+
 def beside(x):
-    west = lax.ppermute(x, "gx", ring("gx", 1))
-    east = lax.ppermute(x, "gx", ring("gx", -1))
-    mid = jnp.stack([west, x, east])
-    count = lax.axis_size("gy")
-    near = lax.ppermute(mid, "gy", [(i, i ^ 1) for i in range(count)])
-    far = lax.ppermute(mid, "gy", [(i, (i + 1 if i % 2 else i - 1) % count) for i in range(count)])
-    return mid, near, far
+    pairs, others = partners("gx")
+    far = lax.ppermute(x, "gx", others)
+    near = lax.ppermute(x, "gx", pairs)
+    mid = jnp.stack([far, x, near])
+    pairs, others = partners("gy")
+    return mid, lax.ppermute(mid, "gy", pairs), lax.ppermute(mid, "gy", others)
 
 
 def plain(apply, forces):

time: 93.5 us -> 93 us (level)
  transfers between devices with their start and end apart: 13 -> 13, of which waited for: 7 -> 7; matrix products, arithmetic and copies ran while one was open for 0% -> 0% of each run, Pallas kernels for 23% -> 24%
where the time goes in v6:
time: 93 us; the launch traced here: 92.5 us
  Pallas kernels  35.2 us (38%)
  waiting for transfers between devices  24.9 us (27%)
  starting transfers between devices  21.6 us (23%)
  blocking collectives  9.17 us (10%)
    pallas_call x5, Pallas kernels, local(): pl.pallas_call(kernel, out_shape=outs, in_specs=[SMEM] + [VMEM] * (len(ar...  17.6 us
    ppermute x3, waiting for transfers between devices, beside(): far = lax.ppermute(x, 'gx', others)  17.2 us
    pallas_call x1, Pallas kernels, on_device(): pl.pallas_call(functools.partial(first_kernel, spheres), out_shape=(shape...  13 us
    all_to_all x1, blocking collectives, on_device(): lax.all_to_all(rows, ('gx', 'gy'), split_axis=0, concat_axis=0, tiled=True)  9.17 us
    ppermute x3, waiting for transfers between devices, beside(): near = lax.ppermute(x, 'gx', pairs)  7.55 us
    all_to_all x1, starting transfers between devices, on_device(): got = lax.all_to_all(send, 'gx', split_axis=0, concat_axis=0, tiled=True)  7.25 us
    ppermute x3, starting transfers between devices, beside(): far = lax.ppermute(x, 'gx', others)  5.69 us
    ppermute x3, starting transfers between devices, beside(): lax.ppermute(mid, 'gy', others)  4.85 us
  transfers between devices with their start and end apart: 13, of which 7 were waited for; matrix products, arithmetic and copies ran while one was open for 0% of the time, Pallas kernels for 24%

profile of v6, /device:TPU:0, one launch (start us, length us, event | category | flops | bytes accessed | tf_op | source)
XLA Modules:
  0.0 92.5 jit_solution(17536241077401419288)
XLA Ops:
  0.6 2.6 %pack.1 = (f32[8,6,32,128]{3,2,1,0:T(8,128)}, f32[96,128]{1,0:T(8,128)S(1)}) custom-call(s32[3,14464]{1,0:T(4,128)} %ends_ref.1, f32[5,14464]{1,0:T(8,128)} %geo_ref.1, f32[6,2048]{1,0:T(8,128)} %force_ref.1), custom_call_target="tpu_custom_call" | custom-call | tf_op jit(solution)/shard_map/pack/pallas_call | solution.py:93
  3.2 7.3 %all-to-all-start = ((f32[8,6,32,128]{3,2,1,0:T(8,128)}), f32[8,6,32,128]{3,2,1,0:T(8,128)S(1)}, u32[]{:S(2)}, u32[]{:S(2)}) async-start(f32[8,6,32,128]{3,2,1,0:T(8,128)} %get-tuple-element.61), calls=%async_computation | async-start | bytes 1572864 | tf_op jit(solution)/shard_map/all_to_all | solution.py:613
  10.5 2.0 %collective-permute-start.13 = (f32[6,16,128]{2,1,0:T(8,128)S(1)}, f32[6,16,128]{2,1,0:T(8,128)S(1)}, u32[]{:S(2)}, u32[]{:S(2)}) collective-permute-start(f32[6,16,128]{2,1,0:T(8,128)S(1)} %bitcast.38), channel_id=1, source_target_pairs={{0,4},{4,0},{8,12},{12,8},{16,20},{20,16},{24,28},{28,24},{1,5},{5... | collective-permute-start | bytes 147464 | tf_op jit(solution)/shard_map/ppermute | solution.py:579
  12.5 3.3 %collective-permute-start.12 = (f32[6,16,128]{2,1,0:T(8,128)S(1)}, f32[6,16,128]{2,1,0:T(8,128)S(1)}, u32[]{:S(2)}, u32[]{:S(2)}) collective-permute-start(f32[6,16,128]{2,1,0:T(8,128)S(1)} %bitcast.39), channel_id=1, source_target_pairs={{0,28},{4,8},{8,4},{12,16},{16,12},{20,24},{24,20},{28,0},{1,29},{... | collective-permute-start | bytes 147464 | tf_op jit(solution)/shard_map/ppermute | solution.py:578
  15.8 3.3 %collective-permute-done.13 = f32[6,16,128]{2,1,0:T(8,128)S(1)} collective-permute-done((f32[6,16,128]{2,1,0:T(8,128)S(1)}, f32[6,16,128]{2,1,0:T(8,128)S(1)}, u32[]{:S(2)}, u32[]{:S(2)}) %collective-permute-start.13) | collective-permute-done | bytes 49184 | tf_op jit(solution)/shard_map/ppermute | solution.py:579
  19.0 10.2 %collective-permute-done.12 = f32[6,16,128]{2,1,0:T(8,128)S(1)} collective-permute-done((f32[6,16,128]{2,1,0:T(8,128)S(1)}, f32[6,16,128]{2,1,0:T(8,128)S(1)}, u32[]{:S(2)}, u32[]{:S(2)}) %collective-permute-start.12) | collective-permute-done | bytes 49184 | tf_op jit(solution)/shard_map/ppermute | solution.py:578
  29.3 0.1 collective-permute-start.14
  29.4 1.6 %collective-permute-start.15 = (f32[3,6,16,128]{3,2,1,0:T(8,128)S(1)}, f32[3,6,16,128]{3,2,1,0:T(8,128)S(1)}, u32[]{:S(2)}, u32[]{:S(2)}) collective-permute-start(f32[3,6,16,128]{3,2,1,0:T(8,128)S(1)} %pad_maximum_fusion.3.mid), channel_id=1, source_target_pairs={{0,3},{1,2},{2,1},{3,0},{4,7},{5,6},{6,5},{7,4},{8,11},{9,10},{10,... | collective-permute-start | bytes 442376 | tf_op jit(solution)/shard_map/ppermute | solution.py:582
  31.0 0.0 collective-permute-done.14.near
  31.0 0.2 all-to-all-done.got
  31.2 13.0 %first.1 = (f32[4,256,128]{2,1,0:T(8,128)S(1)}, s32[256,128]{1,0:T(8,128)S(1)}, s32[16,128]{1,0:T(8,128)S(1)}, f32[96,128]{1,0:T(8,128)S(1)}, f32[6,16,128]{2,1,0:T(8,128)S(1)}) custom-call(f32[8,6,32,128]{3,2,1,0:T(8,128)S(1)} %all-to-all-done.got, f32[6,2048]{1,0:T(8,128)S(1)} %copy-done, f32[3,6,16,128]{3,2,1,0:T(8,128)S(1)} %pad_maximum_fusion.3.mid, ...), custom_call_target="tpu_custom_call" | custom-call | bytes 50331648 | tf_op jit(solution)/shard_map/first/pallas_call | solution.py:616
  44.2 2.5 %outer.8.k1 = f32[6,16,128]{2,1,0:T(8,128)S(1)} custom-call(s32[16,128]{1,0:T(8,128)S(1)} %get-tuple-element.117.span, s32[256,128]{1,0:T(8,128)S(1)} %get-tuple-element.118.col, f32[4,256,128]{2,1,0:T(8,128)S(1)} %get-tuple-element.119.terms, f32[6,16,128]{2,1,0:T(8,128)S(1)} %get-tuple-element.67.part, f32[3,6,16,128]{3,2,1,0:T(8,128)S(1)} %collective-permute-done.15.far), custom_call_target="tpu_custom_call" | custom-call | bytes 16777216 | tf_op jit(solution)/shard_map/outer/pallas_call | solution.py:639
  46.7 1.5 %collective-permute-start.17 = (f32[6,16,128]{2,1,0:T(8,128)S(1)}, f32[6,16,128]{2,1,0:T(8,128)S(1)}, u32[]{:S(2)}, u32[]{:S(2)}) collective-permute-start(f32[6,16,128]{2,1,0:T(8,128)S(1)} %outer.8.k1), channel_id=1, source_target_pairs={{0,4},{4,0},{8,12},{12,8},{16,20},{20,16},{24,28},{28,24},{1,5},{5... | collective-permute-start | bytes 147464 | tf_op jit(solution)/shard_map/ppermute | solution.py:579
  48.2 1.2 %collective-permute-start.16 = (f32[6,16,128]{2,1,0:T(8,128)S(1)}, f32[6,16,128]{2,1,0:T(8,128)S(1)}, u32[]{:S(2)}, u32[]{:S(2)}) collective-permute-start(f32[6,16,128]{2,1,0:T(8,128)S(1)} %outer.8.k1), channel_id=1, source_target_pairs={{0,28},{4,8},{8,4},{12,16},{16,12},{20,24},{24,20},{28,0},{1,29},{... | collective-permute-start | bytes 147464 | tf_op jit(solution)/shard_map/ppermute | solution.py:578
  49.4 1.5 %collective-permute-done.17 = f32[6,16,128]{2,1,0:T(8,128)S(1)} collective-permute-done((f32[6,16,128]{2,1,0:T(8,128)S(1)}, f32[6,16,128]{2,1,0:T(8,128)S(1)}, u32[]{:S(2)}, u32[]{:S(2)}) %collective-permute-start.17) | collective-permute-done | bytes 49184 | tf_op jit(solution)/shard_map/ppermute | solution.py:579
  50.9 4.1 %collective-permute-done.16 = f32[6,16,128]{2,1,0:T(8,128)S(1)} collective-permute-done((f32[6,16,128]{2,1,0:T(8,128)S(1)}, f32[6,16,128]{2,1,0:T(8,128)S(1)}, u32[]{:S(2)}, u32[]{:S(2)}) %collective-permute-start.16) | collective-permute-done | bytes 49184 | tf_op jit(solution)/shard_map/ppermute | solution.py:578
  55.0 0.1 collective-permute-start.18
  55.1 1.9 %collective-permute-start.19 = (f32[3,6,16,128]{3,2,1,0:T(8,128)S(1)}, f32[3,6,16,128]{3,2,1,0:T(8,128)S(1)}, u32[]{:S(2)}, u32[]{:S(2)}) collective-permute-start(f32[3,6,16,128]{3,2,1,0:T(8,128)S(1)} %pad_maximum_fusion.4.mid), channel_id=1, source_target_pairs={{0,3},{1,2},{2,1},{3,0},{4,7},{5,6},{6,5},{7,4},{8,11},{9,10},{10,... | collective-permute-start | bytes 442376 | tf_op jit(solution)/shard_map/ppermute | solution.py:582
  57.0 4.4 %inner.7.part = f32[6,16,128]{2,1,0:T(8,128)S(1)} custom-call(s32[16,128]{1,0:T(8,128)S(1)} %get-tuple-element.117.span, s32[256,128]{1,0:T(8,128)S(1)} %get-tuple-element.118.col, f32[4,256,128]{2,1,0:T(8,128)S(1)} %get-tuple-element.119.terms, f32[96,128]{1,0:T(8,128)S(1)} %get-tuple-element.120.drag, f32[3,6,16,128]{3,2,1,0:T(8,128)S(1)} %pad_maximum_fusion.4.mid, ...), custom_call_target="tpu_custom_call" | custom-call | bytes 16777216 | tf_op jit(solution)/shard_map/inner/pallas_call | solution.py:639
  61.4 2.5 %outer.9.k2 = f32[6,16,128]{2,1,0:T(8,128)S(1)} custom-call(s32[16,128]{1,0:T(8,128)S(1)} %get-tuple-element.117.span, s32[256,128]{1,0:T(8,128)S(1)} %get-tuple-element.118.col, f32[4,256,128]{2,1,0:T(8,128)S(1)} %get-tuple-element.119.terms, f32[6,16,128]{2,1,0:T(8,128)S(1)} %inner.7.part, f32[3,6,16,128]{3,2,1,0:T(8,128)S(1)} %collective-permute-done.19.far), custom_call_target="tpu_custom_call" | custom-call | bytes 16777216 | tf_op jit(solution)/shard_map/outer/pallas_call | solution.py:639
  63.9 0.1 collective-permute-start.21
  64.0 1.2 %collective-permute-start.20 = (f32[6,16,128]{2,1,0:T(8,128)S(1)}, f32[6,16,128]{2,1,0:T(8,128)S(1)}, u32[]{:S(2)}, u32[]{:S(2)}) collective-permute-start(f32[6,16,128]{2,1,0:T(8,128)S(1)} %outer.9.k2), channel_id=1, source_target_pairs={{0,28},{4,8},{8,4},{12,16},{16,12},{20,24},{24,20},{28,0},{1,29},{... | collective-permute-start | bytes 147464 | tf_op jit(solution)/shard_map/ppermute | solution.py:578
  65.2 2.8 %collective-permute-done.21 = f32[6,16,128]{2,1,0:T(8,128)S(1)} collective-permute-done((f32[6,16,128]{2,1,0:T(8,128)S(1)}, f32[6,16,128]{2,1,0:T(8,128)S(1)}, u32[]{:S(2)}, u32[]{:S(2)}) %collective-permute-start.21) | collective-permute-done | bytes 49184 | tf_op jit(solution)/shard_map/ppermute | solution.py:579
  68.0 2.8 %collective-permute-done.20 = f32[6,16,128]{2,1,0:T(8,128)S(1)} collective-permute-done((f32[6,16,128]{2,1,0:T(8,128)S(1)}, f32[6,16,128]{2,1,0:T(8,128)S(1)}, u32[]{:S(2)}, u32[]{:S(2)}) %collective-permute-start.20) | collective-permute-done | bytes 49184 | tf_op jit(solution)/shard_map/ppermute | solution.py:578
  70.8 0.1 collective-permute-start.22
  70.9 1.4 %collective-permute-start.23 = (f32[3,6,16,128]{3,2,1,0:T(8,128)S(1)}, f32[3,6,16,128]{3,2,1,0:T(8,128)S(1)}, u32[]{:S(2)}, u32[]{:S(2)}) collective-permute-start(f32[3,6,16,128]{3,2,1,0:T(8,128)S(1)} %pad_maximum_fusion.5.mid), channel_id=1, source_target_pairs={{0,3},{1,2},{2,1},{3,0},{4,7},{5,6},{6,5},{7,4},{8,11},{9,10},{10,... | collective-permute-start | bytes 442376 | tf_op jit(solution)/shard_map/ppermute | solution.py:582
  72.3 0.0 collective-permute-done.22.near
  72.3 5.1 %inner_gram.1 = (f32[6,16,128]{2,1,0:T(8,128)S(1)}, f32[8,128]{1,0:T(8,128)S(1)}) custom-call(s32[16,128]{1,0:T(8,128)S(1)} %get-tuple-element.117.span, s32[256,128]{1,0:T(8,128)S(1)} %get-tuple-element.118.col, f32[4,256,128]{2,1,0:T(8,128)S(1)} %get-tuple-element.119.terms, f32[96,128]{1,0:T(8,128)S(1)} %get-tuple-element.120.drag, ...), custom_call_target="tpu_custom_call" | custom-call | bytes 16777216 | tf_op jit(solution)/shard_map/inner_gram/pallas_call | solution.py:639
  77.4 3.2 %outer_gram.1 = (f32[6,16,128]{2,1,0:T(8,128)S(1)}, f32[32,128]{1,0:T(8,128)S(1)}) custom-call(s32[16,128]{1,0:T(8,128)S(1)} %get-tuple-element.117.span, s32[256,128]{1,0:T(8,128)S(1)} %get-tuple-element.118.col, f32[4,256,128]{2,1,0:T(8,128)S(1)} %get-tuple-element.119.terms, f32[6,16,128]{2,1,0:T(8,128)S(1)} %get-tuple-element.68.part, ...), custom_call_target="tpu_custom_call" | custom-call | bytes 16777216 | tf_op jit(solution)/shard_map/outer_gram/pallas_call | solution.py:639
  80.5 9.2 %all_to_all.16 = f32[32,1,128]{2,1,0:T(1,128)S(1)} all-to-all(f32[32,1,128]{2,1,0:T(1,128)S(1)} %bitcast.37), channel_id=1, replica_groups=mesh['gx'=8,'gy'=4] {'gx','gy'}, dimensions={0} | all-to-all | bytes 32768 | tf_op jit(solution)/shard_map/all_to_all | solution.py:663
  89.7 1.9 %last.1 = (f32[6,2048]{1,0:T(8,128)}, f32[6,2048]{1,0:T(8,128)}, s32[1,1]{1,0:T(1,128)}) custom-call(f32[32,128]{1,0:T(8,128)S(1)} %bitcast.36, f32[6,16,128]{2,1,0:T(8,128)S(1)} %bitcast.43, f32[6,16,128]{2,1,0:T(8,128)S(1)} %outer.8.k1, f32[6,16,128]{2,1,0:T(8,128)S(1)} %outer.9.k2, f32[6,16,128]{2,1,0:T(8,128)S(1)} %get-tuple-element.71.k3), custom_call_target="tpu_custom_call" | custom-call | tf_op jit(solution)/shard_map/last/pallas_call | solution.py:664
  91.6 0.7 while.11
  (9 shorter events, 0.0 us)
Async XLA Ops:
  3.2 28.0 %all-to-all-start = ((f32[8,6,32,128]{3,2,1,0:T(8,128)}), f32[8,6,32,128]{3,2,1,0:T(8,128)S(1)}, u32[]{:S(2)}, u32[]{:S(2)}) async-start(f32[8,6,32,128]{3,2,1,0:T(8,128)} %get-tuple-element.61), calls=%async_computation | async-start | bytes 1572864 | tf_op jit(solution)/shard_map/all_to_all | solution.py:613
  10.5 8.5 %collective-permute-start.13 = (f32[6,16,128]{2,1,0:T(8,128)S(1)}, f32[6,16,128]{2,1,0:T(8,128)S(1)}, u32[]{:S(2)}, u32[]{:S(2)}) collective-permute-start(f32[6,16,128]{2,1,0:T(8,128)S(1)} %bitcast.38), channel_id=1, source_target_pairs={{0,4},{4,0},{8,12},{12,8},{16,20},{20,16},{24,28},{28,24},{1,5},{5... | collective-permute-start | bytes 147464 | tf_op jit(solution)/shard_map/ppermute | solution.py:579
  12.5 16.8 %collective-permute-start.12 = (f32[6,16,128]{2,1,0:T(8,128)S(1)}, f32[6,16,128]{2,1,0:T(8,128)S(1)}, u32[]{:S(2)}, u32[]{:S(2)}) collective-permute-start(f32[6,16,128]{2,1,0:T(8,128)S(1)} %bitcast.39), channel_id=1, source_target_pairs={{0,28},{4,8},{8,4},{12,16},{16,12},{20,24},{24,20},{28,0},{1,29},{... | collective-permute-start | bytes 147464 | tf_op jit(solution)/shard_map/ppermute | solution.py:578
  29.3 1.9 %copy-start = (f32[6,2048]{1,0:T(8,128)S(1)}, f32[6,2048]{1,0:T(8,128)}, u32[]{:S(2)}) copy-start(f32[6,2048]{1,0:T(8,128)} %drag.1) | copy-start | bytes 147460
  29.3 1.7 %collective-permute-start.14 = (f32[3,6,16,128]{3,2,1,0:T(8,128)S(1)}, f32[3,6,16,128]{3,2,1,0:T(8,128)S(1)}, u32[]{:S(2)}, u32[]{:S(2)}) collective-permute-start(f32[3,6,16,128]{3,2,1,0:T(8,128)S(1)} %pad_maximum_fusion.3.mid), channel_id=1, source_target_pairs={{0,1},{1,0},{2,3},{3,2},{4,5},{5,4},{6,7},{7,6},{8,9},{9,8},{10,11... | collective-permute-start | bytes 442376 | tf_op jit(solution)/shard_map/ppermute | solution.py:582
  29.4 14.9 %collective-permute-start.15 = (f32[3,6,16,128]{3,2,1,0:T(8,128)S(1)}, f32[3,6,16,128]{3,2,1,0:T(8,128)S(1)}, u32[]{:S(2)}, u32[]{:S(2)}) collective-permute-start(f32[3,6,16,128]{3,2,1,0:T(8,128)S(1)} %pad_maximum_fusion.3.mid), channel_id=1, source_target_pairs={{0,3},{1,2},{2,1},{3,0},{4,7},{5,6},{6,5},{7,4},{8,11},{9,10},{10,... | collective-permute-start | bytes 442376 | tf_op jit(solution)/shard_map/ppermute | solution.py:582
  46.7 4.2 %collective-permute-start.17 = (f32[6,16,128]{2,1,0:T(8,128)S(1)}, f32[6,16,128]{2,1,0:T(8,128)S(1)}, u32[]{:S(2)}, u32[]{:S(2)}) collective-permute-start(f32[6,16,128]{2,1,0:T(8,128)S(1)} %outer.8.k1), channel_id=1, source_target_pairs={{0,4},{4,0},{8,12},{12,8},{16,20},{20,16},{24,28},{28,24},{1,5},{5... | collective-permute-start | bytes 147464 | tf_op jit(solution)/shard_map/ppermute | solution.py:579
  48.2 6.8 %collective-permute-start.16 = (f32[6,16,128]{2,1,0:T(8,128)S(1)}, f32[6,16,128]{2,1,0:T(8,128)S(1)}, u32[]{:S(2)}, u32[]{:S(2)}) collective-permute-start(f32[6,16,128]{2,1,0:T(8,128)S(1)} %outer.8.k1), channel_id=1, source_target_pairs={{0,28},{4,8},{8,4},{12,16},{16,12},{20,24},{24,20},{28,0},{1,29},{... | collective-permute-start | bytes 147464 | tf_op jit(solution)/shard_map/ppermute | solution.py:578
  55.0 1.9 %collective-permute-start.18 = (f32[3,6,16,128]{3,2,1,0:T(8,128)S(1)}, f32[3,6,16,128]{3,2,1,0:T(8,128)S(1)}, u32[]{:S(2)}, u32[]{:S(2)}) collective-permute-start(f32[3,6,16,128]{3,2,1,0:T(8,128)S(1)} %pad_maximum_fusion.4.mid), channel_id=1, source_target_pairs={{0,1},{1,0},{2,3},{3,2},{4,5},{5,4},{6,7},{7,6},{8,9},{9,8},{10,11... | collective-permute-start | bytes 442376 | tf_op jit(solution)/shard_map/ppermute | solution.py:582
  55.1 6.3 %collective-permute-start.19 = (f32[3,6,16,128]{3,2,1,0:T(8,128)S(1)}, f32[3,6,16,128]{3,2,1,0:T(8,128)S(1)}, u32[]{:S(2)}, u32[]{:S(2)}) collective-permute-start(f32[3,6,16,128]{3,2,1,0:T(8,128)S(1)} %pad_maximum_fusion.4.mid), channel_id=1, source_target_pairs={{0,3},{1,2},{2,1},{3,0},{4,7},{5,6},{6,5},{7,4},{8,11},{9,10},{10,... | collective-permute-start | bytes 442376 | tf_op jit(solution)/shard_map/ppermute | solution.py:582
  63.9 4.2 %collective-permute-start.21 = (f32[6,16,128]{2,1,0:T(8,128)S(1)}, f32[6,16,128]{2,1,0:T(8,128)S(1)}, u32[]{:S(2)}, u32[]{:S(2)}) collective-permute-start(f32[6,16,128]{2,1,0:T(8,128)S(1)} %outer.9.k2), channel_id=1, source_target_pairs={{0,4},{4,0},{8,12},{12,8},{16,20},{20,16},{24,28},{28,24},{1,5},{5... | collective-permute-start | bytes 147464 | tf_op jit(solution)/shard_map/ppermute | solution.py:579
  64.0 6.9 %collective-permute-start.20 = (f32[6,16,128]{2,1,0:T(8,128)S(1)}, f32[6,16,128]{2,1,0:T(8,128)S(1)}, u32[]{:S(2)}, u32[]{:S(2)}) collective-permute-start(f32[6,16,128]{2,1,0:T(8,128)S(1)} %outer.9.k2), channel_id=1, source_target_pairs={{0,28},{4,8},{8,4},{12,16},{16,12},{20,24},{24,20},{28,0},{1,29},{... | collective-permute-start | bytes 147464 | tf_op jit(solution)/shard_map/ppermute | solution.py:578
  70.8 1.4 %collective-permute-start.22 = (f32[3,6,16,128]{3,2,1,0:T(8,128)S(1)}, f32[3,6,16,128]{3,2,1,0:T(8,128)S(1)}, u32[]{:S(2)}, u32[]{:S(2)}) collective-permute-start(f32[3,6,16,128]{3,2,1,0:T(8,128)S(1)} %pad_maximum_fusion.5.mid), channel_id=1, source_target_pairs={{0,1},{1,0},{2,3},{3,2},{4,5},{5,4},{6,7},{7,6},{8,9},{9,8},{10,11... | collective-permute-start | bytes 442376 | tf_op jit(solution)/shard_map/ppermute | solution.py:582
  70.9 6.5 %collective-permute-start.23 = (f32[3,6,16,128]{3,2,1,0:T(8,128)S(1)}, f32[3,6,16,128]{3,2,1,0:T(8,128)S(1)}, u32[]{:S(2)}, u32[]{:S(2)}) collective-permute-start(f32[3,6,16,128]{3,2,1,0:T(8,128)S(1)} %pad_maximum_fusion.5.mid), channel_id=1, source_target_pairs={{0,3},{1,2},{2,1},{3,0},{4,7},{5,6},{6,5},{7,4},{8,11},{9,10},{10,... | collective-permute-start | bytes 442376 | tf_op jit(solution)/shard_map/ppermute | solution.py:582
